TPU v7x, 32 devices: a whole 2x2x4 slice. The times are simulated.
32 devices in a mesh: ctx: 8 (over y, x, core), head: 4 (over z).
Axes of the slice: x: 2, y: 2, z: 4, core: 2. Of those that a mesh axis runs over, the one named last changes fastest.
Arguments:
- queries: bfloat16 [8192, 2048], P('ctx', 'head'), may hold values from -18 to 18
- keys: bfloat16 [8192, 2048], P('ctx', 'head'), may hold values from -6 to 6
- values: bfloat16 [8192, 2048], P('ctx', 'head'), may hold values from -6 to 6
- rates: float32 [8192, 4], P('ctx', 'head'), may hold values from 0.00048828125 to 0.0048828125
- fast_w1: bfloat16 [4, 512, 512], P('head'), may hold values from -0.25 to 0.25
- fast_w2: bfloat16 [4, 512, 512], P('head'), may hold values from -2 to 2
- fast_w3: bfloat16 [4, 512, 512], P('head'), may hold values from -0.25 to 0.25
- norm_gain: bfloat16 [2048], P('head'), may hold values from 0.25 to 1.75
- out_weight: bfloat16 [2048, 2048], P('head'), may hold values from -0.125 to 0.125
Outputs:
- output: bfloat16 [8192, 2048], P(('ctx', 'head'))
All inputs are finite; a program needn't handle non-finite values.
Results may differ from a plain program's by a relative error of at most 0.014.
Values may be sent and summed in bfloat16 or wider, within the bound.
No kernel may reach another device: no remote copies, remote signals or barrier semaphores. Data moves between devices by JAX's collectives and lax.ppermute only.
A program may use at most 64 MiB of HBM per device.

v0:
```python
import functools
import math

import jax
import jax.numpy as jnp
from jax import lax
from jax.experimental import pallas as pl
from jax.experimental.pallas import tpu as pltpu
from jax.sharding import PartitionSpec as P


WINDOW = 256
EPSILON = 1e-06

VMEM = pl.BlockSpec(memory_space=pltpu.VMEM)
HBM = pl.BlockSpec(memory_space=pltpu.HBM)


def near_core(*arrays):
    return [pltpu.with_memory_space_constraint(a, pltpu.VMEM) for a in arrays]


def far_core(*arrays):
    return [pltpu.with_memory_space_constraint(a, pltpu.HBM) for a in arrays]


def grant(mib):
    return pltpu.CompilerParams(vmem_limit_bytes=mib << 20)


def swap(value, axis, mask):
    return lax.ppermute(value, axis, [(i, i ^ mask) for i in range(lax.axis_size(axis))])


def dot(left, right, left_dim=1, right_dim=0):
    return lax.dot_general(
        left, right, (((left_dim,), (right_dim,)), ((), ())), preferred_element_type=jnp.float32
    )


def place():
    me = lax.axis_index("ctx").astype(jnp.int32)
    return me & 1, ((me >> 1) ^ (me >> 2)) & 1


def column(row, width):
    tall = jnp.transpose(jnp.broadcast_to(row, (128, row.shape[1])))
    return jnp.concatenate([tall] * (width // 128), axis=1)


def load_kernel(k_hbm, v_hbm, gain_hbm, w_hbm, tail_ref, piece_ref, w_ref, gain_ref, sem):
    rows, columns = piece_ref.shape
    _, side = place()
    first = pl.multiple_of(side * rows, rows)
    last = pl.ds(k_hbm.shape[0] - WINDOW, WINDOW)
    steps = 4
    block = rows // steps
    moves = [(gain_hbm, gain_ref)]
    for i in range(steps):
        at = pl.ds(i * block, block)
        moves.append((w_hbm.at[pl.ds(first + i * block, block), :], w_ref.at[at, :]))
    moves += [(k_hbm.at[last, :], tail_ref.at[pl.ds(0, WINDOW), :])]
    moves += [(v_hbm.at[last, :], tail_ref.at[pl.ds(WINDOW, WINDOW), :])]
    copies = [pltpu.make_async_copy(src, dst, sem.at[j]) for j, (src, dst) in enumerate(moves)]
    for copy in copies:
        copy.start()
    copies[0].wait()
    gain = gain_ref[...].reshape(1, 2 * rows).astype(jnp.float32)
    gain = jnp.transpose(jnp.broadcast_to(jnp.where(side == 0, gain[:, :rows], gain[:, rows:]), (128, rows)))
    for i in range(steps):
        at = slice(i * block, (i + 1) * block)
        copies[1 + i].wait()
        for left in range(0, columns, 128):
            here = slice(left, left + 128)
            piece_ref[at, here] = (w_ref[at, here].astype(jnp.float32) * gain[at, :]).astype(jnp.bfloat16)
    for copy in copies[1 + steps :]:
        copy.wait()


def load(keys, values, gain, weight):
    piece = pltpu.VMEM((weight.shape[0] // 2, weight.shape[1]), jnp.bfloat16)
    return pl.pallas_call(
        load_kernel,
        out_shape=[pltpu.VMEM((2 * WINDOW, keys.shape[1]), jnp.bfloat16), piece],
        compiler_params=grant(8),
        in_specs=[HBM] * 4,
        out_specs=[VMEM] * 2,
        scratch_shapes=[piece, pltpu.VMEM(gain.shape, gain.dtype), pltpu.SemaphoreType.DMA((7,))],
        name="load",
    )(*far_core(keys, values, gain, weight))


def halves(width):
    core, _ = place()
    half = width // 2
    mine = pl.ds(pl.multiple_of(core * half, half), half)
    theirs = pl.ds(pl.multiple_of((1 - core) * half, half), half)
    return mine, theirs


def forward_kernel(k_ref, v_ref, r_ref, w1_ref, w3_ref, give_ref, act_ref, sc_ref, gs_ref, slope_ref):
    rows, width = k_ref.shape
    steps = 4
    block = rows // steps
    for i in range(steps):
        at = slice(i * block, (i + 1) * block)
        k = k_ref[at, :]
        gate = dot(k, w1_ref[0])
        up = dot(k, w3_ref[0])
        rate = column(r_ref[:, at], width)
        s = jax.nn.sigmoid(gate)
        gs = gate * s
        act_ref[at, :] = (gs * up).astype(jnp.bfloat16)
        sc_ref[at, :] = (v_ref[at, :].astype(jnp.float32) * rate).astype(jnp.bfloat16)
        gs_ref[at, :] = gs
        slope_ref[at, :] = up * (s + gs * (1.0 - s))
    _, theirs = halves(width)
    give_ref[0] = dot(act_ref[...], sc_ref[:, theirs], 0, 0).astype(jnp.bfloat16)


def push_forward(keys, values, rates, w1, w3):
    rows, width = keys.shape
    return pl.pallas_call(
        forward_kernel,
        out_shape=[pltpu.VMEM((1, width, width // 2), jnp.bfloat16)]
        + [pltpu.VMEM((rows, width), jnp.bfloat16)] * 2
        + [pltpu.VMEM((rows, width), jnp.float32)] * 2,
        compiler_params=grant(12),
        in_specs=[VMEM] * 5,
        out_specs=[VMEM] * 5,
        name="push_forward",
    )(*near_core(keys, values, rates.reshape(1, rows), w1, w3))


def backward_kernel(k_ref, act_ref, sc_ref, gs_ref, slope_ref, w2_ref, give_ref, keep_ref, g1_ref, g3_ref):
    rows, width = k_ref.shape
    steps = 4
    block = rows // steps
    for i in range(steps):
        at = slice(i * block, (i + 1) * block)
        back = dot(sc_ref[at, :], w2_ref[0], 1, 1)
        g1_ref[at, :] = (back * slope_ref[at, :]).astype(jnp.bfloat16)
        g3_ref[at, :] = (back * gs_ref[at, :]).astype(jnp.bfloat16)
    mine, theirs = halves(width)
    give_ref[0] = dot(k_ref[...], g1_ref[:, theirs], 0, 0).astype(jnp.bfloat16)
    give_ref[1] = dot(k_ref[...], g3_ref[:, theirs], 0, 0).astype(jnp.bfloat16)
    keep_ref[0] = dot(act_ref[...], sc_ref[:, mine], 0, 0)


def push_backward(keys, act, scaled, gs, slope, w2):
    rows, width = keys.shape
    return pl.pallas_call(
        backward_kernel,
        out_shape=[
            pltpu.VMEM((2, width, width // 2), jnp.bfloat16),
            pltpu.VMEM((1, width, width // 2), jnp.float32),
        ]
        + [pltpu.VMEM((rows, width), jnp.bfloat16)] * 2,
        compiler_params=grant(12),
        in_specs=[VMEM] * 6,
        out_specs=[VMEM] * 4,
        name="push_backward",
    )(*near_core(keys, act, scaled, gs, slope, w2))


def keep_kernel(k_ref, g1_ref, g3_ref, keep_ref):
    mine, _ = halves(k_ref.shape[1])
    for j, ref in enumerate((g1_ref, g3_ref)):
        keep_ref[j] = dot(k_ref[...], ref[:, mine], 0, 0)


def kept(keys, g1, g3):
    width = keys.shape[1]
    return pl.pallas_call(
        keep_kernel,
        out_shape=pltpu.VMEM((2, width, width // 2), jnp.float32),
        compiler_params=grant(12),
        in_specs=[VMEM] * 3,
        out_specs=VMEM,
        name="kept",
    )(*near_core(keys, g1, g3))


def add_kernel(keep_ref, got_ref, sum_ref, send_ref):
    total = keep_ref[...] + got_ref[...].astype(jnp.float32)
    sum_ref[...] = total
    send_ref[...] = total.astype(jnp.bfloat16)


def add(keep, got):
    return pl.pallas_call(
        add_kernel,
        out_shape=(pltpu.VMEM(keep.shape, jnp.float32), pltpu.VMEM(keep.shape, jnp.bfloat16)),
        compiler_params=grant(8),
        in_specs=[VMEM] * 2,
        out_specs=(VMEM,) * 2,
        name="add",
    )(*near_core(keep, got))


def renorm_kernel(keep_ref, got_ref, *refs):
    *weights, out_ref = refs
    half = keep_ref.shape[2]
    block = half // 2
    core, _ = place()
    for j, w_ref in enumerate(weights):
        for first in (0, block):
            at = slice(first, first + block)
            start = pl.multiple_of(core * half + first, block)
            old = w_ref[0, :, pl.ds(start, block)].astype(jnp.float32)
            new = old + (keep_ref[j, :, at] + got_ref[j, :, at].astype(jnp.float32))
            old_norm = jnp.sqrt(jnp.mean(old * old, axis=0, keepdims=True) + EPSILON)
            new_norm = jnp.sqrt(jnp.mean(new * new, axis=0, keepdims=True) + EPSILON)
            out_ref[j, :, at] = (new * (old_norm / new_norm)).astype(jnp.bfloat16)


def renorm(keep, got, *weights):
    return pl.pallas_call(
        renorm_kernel,
        out_shape=pltpu.VMEM(keep.shape, jnp.bfloat16),
        compiler_params=grant(8),
        in_specs=[VMEM] * (2 + len(weights)),
        out_specs=VMEM,
        name="renorm",
    )(*near_core(keep, got, *weights))


def window_kernel(q_hbm, k_hbm, v_hbm, tail_ref, out_ref, q_ref, k_ref, v_ref, sem):
    rows, width = q_ref.shape
    scale = 1.0 / math.sqrt(width)
    query = lax.broadcasted_iota(jnp.int32, (WINDOW, 2 * WINDOW), 0)
    key = lax.broadcasted_iota(jnp.int32, (WINDOW, 2 * WINDOW), 1)
    allowed = (key > query) & (key <= query + WINDOW)
    allowed_first = allowed & ((key >= WINDOW) | (lax.axis_index("ctx") > 0))
    count = rows // WINDOW
    loads = [[
        pltpu.make_async_copy(tail_ref.at[pl.ds(j * WINDOW, WINDOW), :], dst.at[pl.ds(0, WINDOW), :], sem.at[j])
        for j, dst in enumerate((k_ref, v_ref))
    ]]
    for i in range(count):
        at, after = pl.ds(i * WINDOW, WINDOW), pl.ds((i + 1) * WINDOW, WINDOW)
        loads.append([
            pltpu.make_async_copy(q_hbm.at[at, :], q_ref.at[at, :], sem.at[3 * i + 2]),
            pltpu.make_async_copy(k_hbm.at[at, :], k_ref.at[after, :], sem.at[3 * i + 3]),
            pltpu.make_async_copy(v_hbm.at[at, :], v_ref.at[after, :], sem.at[3 * i + 4]),
        ])
    for group in loads:
        for load in group:
            load.start()
    for load in loads[0]:
        load.wait()
    for i in range(count):
        for load in loads[i + 1]:
            load.wait()
        at = slice(i * WINDOW, (i + 1) * WINDOW)
        seen = slice(i * WINDOW, (i + 2) * WINDOW)
        scores = dot(q_ref[at, :], k_ref[seen, :], 1, 1) * scale
        scores = jnp.where(allowed_first if i == 0 else allowed, scores, -jnp.inf)
        peak = jnp.max(scores, axis=1, keepdims=True)
        exponent = jnp.exp(scores - peak)
        weights = exponent / jnp.sum(exponent, axis=1, keepdims=True)
        out_ref[at, :] = dot(weights.astype(jnp.bfloat16), v_ref[seen, :])


def window(queries, keys, values, tail):
    rows, width = queries.shape
    return pl.pallas_call(
        window_kernel,
        out_shape=pltpu.VMEM(queries.shape, jnp.float32),
        compiler_params=grant(24),
        in_specs=[HBM] * 3 + [VMEM],
        out_specs=VMEM,
        scratch_shapes=[pltpu.VMEM((rows, width), jnp.bfloat16)]
        + [pltpu.VMEM((rows + WINDOW, width), jnp.bfloat16)] * 2
        + [pltpu.SemaphoreType.DMA((2 + 3 * (rows // WINDOW),))],
        name="window",
    )(*far_core(queries, keys, values), *near_core(tail))


def apply_kernel(slot, q_ref, seen_ref, down_ref, up_ref, down_c_ref, up_c_ref, out_ref):
    rows, width = out_ref.shape
    own, rest = halves(width)
    here = pl.ds(pl.multiple_of((lax.axis_index("head").astype(jnp.int32) ^ slot) * rows, rows), rows)
    q = q_ref[here, :]
    mixed = []
    for ref in (up_ref, up_c_ref):
        gate = dot(q, ref[0])
        up = dot(q, ref[1])
        mixed.append((gate * jax.nn.sigmoid(gate) * up).astype(jnp.bfloat16))
    mixed = jnp.concatenate(mixed, axis=1)
    for ref, at in ((down_ref, own), (down_c_ref, rest)):
        down = jnp.concatenate([ref[0, own, :], ref[0, rest, :]], axis=0)
        out_ref[:, at] = (dot(mixed, down) + seen_ref[here, at]).astype(jnp.bfloat16)


def apply_fast(slot, queries, seen, weights, rows):
    return pl.pallas_call(
        functools.partial(apply_kernel, slot),
        out_shape=pltpu.VMEM((rows, queries.shape[1]), jnp.bfloat16),
        compiler_params=grant(16),
        in_specs=[VMEM] * 6,
        out_specs=VMEM,
        name="apply",
    )(*near_core(queries, seen, *weights))


def own_project_kernel(x_ref, gain_ref, w_ref, out_ref, squares_ref):
    wide = x_ref[...].astype(jnp.float32)
    squares_ref[...] = jnp.sum(wide * wide, axis=1, keepdims=True)
    gain = gain_ref[...].reshape(1, wide.shape[1]).astype(jnp.float32)
    x = (wide * gain).astype(jnp.bfloat16)
    out_ref[...] = dot(x, w_ref[...])


def own_project(x, gain, weight):
    return pl.pallas_call(
        own_project_kernel,
        out_shape=(
            pltpu.VMEM((x.shape[0], weight.shape[1]), jnp.float32),
            pltpu.VMEM((x.shape[0], 1), jnp.float32),
        ),
        compiler_params=grant(16),
        in_specs=[VMEM] * 3,
        out_specs=(VMEM, VMEM),
        name="own_project",
    )(*near_core(x, gain, weight))


def pick_kernel(early_ref, early_c_ref, out_ref, sem):
    columns = out_ref.shape[1]
    core, _ = place()
    here = pl.ds(pl.multiple_of(core * columns, columns), columns)

    @pl.when(core == 1)
    def _():
        copy = pltpu.make_async_copy(early_ref.at[:, here], out_ref, sem)
        copy.start()
        copy.wait()

    @pl.when(core == 0)
    def _():
        copy = pltpu.make_async_copy(early_c_ref.at[:, here], out_ref, sem)
        copy.start()
        copy.wait()


def pick(early, early_c):
    return pl.pallas_call(
        pick_kernel,
        out_shape=pltpu.VMEM((early.shape[0], early.shape[1] // 2), early.dtype),
        compiler_params=grant(4),
        in_specs=[VMEM] * 2,
        out_specs=VMEM,
        scratch_shapes=[pltpu.SemaphoreType.DMA],
        name="pick",
    )(*near_core(early, early_c))


def project_kernel(holder, scale_by, x_ref, base_ref, squares_ref, near, near_c, far, far_c,
                   out_ref, *rest):
    rows = near.shape[0]
    columns = out_ref.shape[1] // 2
    core, half = place()
    wide = x_ref[...].astype(jnp.float32)
    squares = squares_ref[...] + jnp.sum(wide * wide, axis=1, keepdims=True)
    mine = pl.ds(pl.multiple_of(half * rows, rows), rows)
    theirs = pl.ds(pl.multiple_of((1 - half) * rows, rows), rows)
    x = jnp.concatenate([x_ref[:, mine], x_ref[:, theirs]], axis=1)
    scale = lax.rsqrt(squares * scale_by + EPSILON) if scale_by else None
    block = columns // 2
    stores = []
    for side in range(2):
        for j in range(2):
            if holder is None:
                w_near, w_far = ((near, far), (near_c, far_c))[side]
                start = core if side == 0 else 1 - core
                here = slice(j * block, (j + 1) * block)
                w = jnp.concatenate([w_near[:, here], w_far[:, here]], axis=0)
                at = pl.ds(pl.multiple_of(start * columns + j * block, block), block)
            else:
                at = slice(side * columns + j * block, side * columns + (j + 1) * block)
                w = [jnp.where(core == holder, a[:, at], b[:, at]) for a, b in ((near, near_c), (far, far_c))]
                w = jnp.concatenate(w, axis=0)
            total = base_ref[:, at] + dot(x, w)
            if scale_by:
                ready_ref, sem = rest
                ready_ref[2 * side + j] = (total * scale).astype(jnp.bfloat16)
                store = pltpu.make_async_copy(ready_ref.at[2 * side + j], out_ref.at[:, at], sem.at[2 * side + j])
                store.start()
                stores.append(store)
            else:
                out_ref[:, at] = total
    if not scale_by:
        rest[0][...] = squares
    for store in stores:
        store.wait()


def project(holder, scale_by, x, base, squares, pieces):
    rows, columns = base.shape
    if scale_by:
        shape = jax.ShapeDtypeStruct((rows, columns), jnp.bfloat16)
        scratch = [pltpu.VMEM((4, rows, columns // 4), jnp.bfloat16), pltpu.SemaphoreType.DMA((4,))]
    else:
        shape = (pltpu.VMEM((rows, columns), jnp.float32), pltpu.VMEM((rows, 1), jnp.float32))
        scratch = []
    return pl.pallas_call(
        functools.partial(project_kernel, holder, scale_by),
        out_shape=shape,
        in_specs=[VMEM] * 7,
        out_specs=HBM if scale_by else (VMEM, VMEM),
        scratch_shapes=scratch,
        compiler_params=grant(16),
        name="project",
    )(*near_core(x, base, squares, *pieces))


def step(queries, keys, values, rates, fast_w1, fast_w2, fast_w3, norm_gain, out_weight):
    tok_rows, width = queries.shape
    ctx_count = lax.axis_size("ctx")
    heads = lax.axis_size("head")
    bits = ctx_count.bit_length() - 1
    assert ctx_count == 1 << bits and bits >= 3 and heads == 4

    tail, piece = load(keys, values, norm_gain, out_weight)
    tail = lax.ppermute(tail, "ctx", [(i, i + 1) for i in range(ctx_count - 1)])

    over = [(i, i ^ (2 if i // heads & 1 else 1)) for i in range(ctx_count * heads)]
    early = lax.ppermute(piece, ("ctx", "head"), over)
    early_c = swap(early, "ctx", 1)
    late = pick(early, early_c)
    late = swap(late, "head", 1)
    cross = [(i, i ^ (2 if i & 1 else 4)) for i in range(ctx_count)]
    early_far = lax.ppermute(early, "ctx", cross)
    late_far = lax.ppermute(late, "ctx", cross)
    late_c = swap(late, "ctx", 1)
    early_far_c = swap(early_far, "ctx", 1)
    late_far_c = swap(late_far, "ctx", 1)
    early_pieces = (early, early_c, early_far, early_far_c)
    late_pieces = (late, late_c, late_far, late_far_c)

    give_a, act, scaled, gs, slope = push_forward(keys, values, rates, fast_w1, fast_w3)
    give_b, keep_a, g1, g3 = push_backward(keys, act, scaled, gs, slope, fast_w2)
    keep_b = kept(keys, g1, g3)

    masks = [1 << b for b in range(1, bits)]
    crossing = [
        [(i, i ^ (backward if i & 1 else forward)) for i in range(ctx_count)]
        for forward, backward in zip(masks, masks[::-1])
    ]
    weights = []
    for give, keep, olds in ((give_a, keep_a, (fast_w2,)), (give_b, keep_b, (fast_w1, fast_w3))):
        got = swap(give, "ctx", 1)
        for pairs in crossing:
            keep, send = add(keep, got)
            got = lax.ppermute(send, "ctx", pairs)
        mine = renorm(keep, got, *olds)
        other = swap(mine, "ctx", 1)
        weights.append((mine, other))
    weights = (weights[0][0], weights[1][0], weights[0][1], weights[1][1])

    seen = window(queries, keys, values, tail)

    rows = tok_rows // heads
    blocks = {}
    for k in send_order(heads) + [0]:
        combined = apply_fast(k, queries, seen, weights, rows)
        blocks[k] = swap(combined, "head", k) if k else combined
    base, squares = own_project(blocks[0], norm_gain, out_weight)
    for k in send_order(heads):
        holder, pieces = (None, late_pieces) if k == heads - 1 else (k - 1, early_pieces)
        scale_by = 1.0 / (heads * width) if k == send_order(heads)[-1] else None
        result = project(holder, scale_by, blocks[k], base, squares, pieces)
        if scale_by is None:
            base, squares = result
    return result


def send_order(heads):
    return [heads - 1] + list(range(1, heads - 1))


def solution(mesh):
    placed = (
        P("ctx", "head"),
        P("ctx", "head"),
        P("ctx", "head"),
        P("ctx", "head"),
        P("head", None, None),
        P("head", None, None),
        P("head", None, None),
        P("head"),
        P("head", None),
    )
    return jax.shard_map(step, mesh=mesh, in_specs=placed, out_specs=P(("ctx", "head"), None), check_vma=False)
```

profile of v0, /device:TPU:0, one launch (start us, length us, event | category | flops | bytes accessed | tf_op | source)
XLA Modules:
  0.0 107.8 jit_solution(13398386383629119289)
XLA Ops:
  0.0 1.6 %load.1 = (bf16[512,512]{1,0:T(8,128)(2,1)S(1)}, bf16[256,2048]{1,0:T(8,128)(2,1)S(1)}) custom-call(bf16[1024,512]{1,0:T(8,128)(2,1)} %k_ref.5, bf16[1024,512]{1,0:T(8,128)(2,1)} %v_ref.1, bf16[512]{0:T(512)(128)(2,1)} %gain_ref.1, bf16[512,2048]{1,0:T(8,128)(2,1)} %w_ref.1), custom_call_target="tpu_custom_call" | custom-call | tf_op jit(solution)/shard_map/load/pallas_call | solution.py:82
  1.6 3.1 %collective-permute-start.12 = (bf16[256,2048]{1,0:T(8,128)(2,1)S(1)}, bf16[256,2048]{1,0:T(8,128)(2,1)S(1)}, u32[]{:S(2)}, u32[]{:S(2)}) collective-permute-start(bf16[256,2048]{1,0:T(8,128)(2,1)S(1)} %get-tuple-element.50), channel_id=1, source_target_pairs={{0,1},{1,0},{2,3},{3,2},{4,6},{5,7},{6,4},{7,5},{8,9},{9,8},{10,11... | collective-permute-start | bytes 3145736 | tf_op jit(solution)/shard_map/ppermute | solution.py:429
  4.8 1.9 %push_forward.1 = (bf16[1,512,256]{2,1,0:T(8,128)(2,1)S(1)}, bf16[1024,512]{1,0:T(8,128)(2,1)S(1)}, bf16[1024,512]{1,0:T(8,128)(2,1)S(1)}, f32[1024,512]{1,0:T(8,128)S(1)}, f32[1024,512]{1,0:T(8,128)S(1)}) custom-call(bf16[1024,512]{1,0:T(8,128)(2,1)S(1)} %copy-done.1, bf16[1024,512]{1,0:T(8,128)(2,1)S(1)} %copy-done.2, f32[1,1024]{1,0:T(1,128)S(1)} %bitcast.1, ...), custom_call_target="tpu_custom_call" | custom-call | tf_op jit(solution)/shard_map/push_forward/pallas_call | solution.py:123
  6.7 1.8 %push_backward.1 = (bf16[2,512,256]{2,1,0:T(8,128)(2,1)S(1)}, f32[1,512,256]{2,1,0:T(8,128)S(1)}, bf16[1024,512]{1,0:T(8,128)(2,1)S(1)}, bf16[1024,512]{1,0:T(8,128)(2,1)S(1)}) custom-call(bf16[1024,512]{1,0:T(8,128)(2,1)S(1)} %copy-done.1, bf16[1024,512]{1,0:T(8,128)(2,1)S(1)} %get-tuple-element.31.act_ref, bf16[1024,512]{1,0:T(8,128)(2,1)S(1)} %get-tuple-element.32.sc_ref, ...), custom_call_target="tpu_custom_call" | custom-call | tf_op jit(solution)/shard_map/push_backward/pallas_call | solution.py:152
  8.5 0.6 collective-permute-start.4
  9.1 19.3 %collective-permute-done.12.early_ref.near = bf16[256,2048]{1,0:T(8,128)(2,1)S(1)} collective-permute-done((bf16[256,2048]{1,0:T(8,128)(2,1)S(1)}, bf16[256,2048]{1,0:T(8,128)(2,1)S(1)}, u32[]{:S(2)}, u32[]{:S(2)}) %collective-permute-start.12) | collective-permute-done | bytes 1048608 | tf_op jit(solution)/shard_map/ppermute | solution.py:429
  28.8 0.8 kept.1.keep_ref
  29.7 1.6 %collective-permute-start.5 = (bf16[2,512,256]{2,1,0:T(8,128)(2,1)S(1)}, bf16[2,512,256]{2,1,0:T(8,128)(2,1)S(1)}, u32[]{:S(2)}, u32[]{:S(2)}) collective-permute-start(bf16[2,512,256]{2,1,0:T(8,128)(2,1)S(1)} %get-tuple-element.45), channel_id=1, source_target_pairs={{0,8},{4,20},{8,0},{12,28},{16,24},{20,4},{24,16},{28,12},{1,9},{5... | collective-permute-start | bytes 1572872 | tf_op jit(solution)/shard_map/ppermute | solution.py:456
  31.3 1.5 %collective-permute-start.18 = (bf16[256,2048]{1,0:T(8,128)(2,1)S(1)}, bf16[256,2048]{1,0:T(8,128)(2,1)S(1)}, u32[]{:S(2)}, u32[]{:S(2)}) collective-permute-start(bf16[256,2048]{1,0:T(8,128)(2,1)S(1)} %collective-permute-done.12.early_ref.near), channel_id=1, source_target_pairs={{0,16},{4,12},{8,24},{12,4},{16,0},{20,28},{24,8},{28,20},{1,17},{... | collective-permute-start | bytes 3145736 | tf_op jit(solution)/shard_map/ppermute | solution.py:434
  32.9 1.9 %collective-permute-start.14 = (bf16[256,1024]{1,0:T(8,128)(2,1)S(1)}, bf16[256,1024]{1,0:T(8,128)(2,1)S(1)}, u32[]{:S(2)}, u32[]{:S(2)}) collective-permute-start(bf16[256,1024]{1,0:T(8,128)(2,1)S(1)} %pick.1), channel_id=1, source_target_pairs={{0,1},{1,0},{2,3},{3,2},{4,5},{5,4},{6,7},{7,6},{8,9},{9,8},{10,11... | collective-permute-start | bytes 1572872 | tf_op jit(solution)/shard_map/ppermute | solution.py:32
  34.8 9.0 %collective-permute-done.5.got_ref = bf16[2,512,256]{2,1,0:T(8,128)(2,1)S(1)} collective-permute-done((bf16[2,512,256]{2,1,0:T(8,128)(2,1)S(1)}, bf16[2,512,256]{2,1,0:T(8,128)(2,1)S(1)}, u32[]{:S(2)}, u32[]{:S(2)}) %collective-permute-start.5) | collective-permute-done | bytes 524320 | tf_op jit(solution)/shard_map/ppermute | solution.py:456
  43.9 2.4 %collective-permute-start.6 = (bf16[2,512,256]{2,1,0:T(8,128)(2,1)S(1)}, bf16[2,512,256]{2,1,0:T(8,128)(2,1)S(1)}, u32[]{:S(2)}, u32[]{:S(2)}) collective-permute-start(bf16[2,512,256]{2,1,0:T(8,128)(2,1)S(1)} %get-tuple-element.47), channel_id=1, source_target_pairs={{0,16},{4,12},{8,24},{12,4},{16,0},{20,28},{24,8},{28,20},{1,17},{... | collective-permute-start | bytes 1572872 | tf_op jit(solution)/shard_map/ppermute | solution.py:456
  46.4 1.6 %collective-permute-start.2 = (bf16[1,512,256]{2,1,0:T(8,128)(2,1)S(1)}, bf16[1,512,256]{2,1,0:T(8,128)(2,1)S(1)}, u32[]{:S(2)}, u32[]{:S(2)}) collective-permute-start(bf16[1,512,256]{2,1,0:T(8,128)(2,1)S(1)} %get-tuple-element.38), channel_id=1, source_target_pairs={{0,8},{4,20},{8,0},{12,28},{16,24},{20,4},{24,16},{28,12},{1,9},{5... | collective-permute-start | bytes 786440 | tf_op jit(solution)/shard_map/ppermute | solution.py:456
  48.0 1.5 %collective-permute-start = (bf16[512,512]{1,0:T(8,128)(2,1)S(1)}, bf16[512,512]{1,0:T(8,128)(2,1)S(1)}, u32[]{:S(2)}, u32[]{:S(2)}) collective-permute-start(bf16[512,512]{1,0:T(8,128)(2,1)S(1)} %get-tuple-element.30), channel_id=1, source_target_pairs={{0,4},{4,8},{8,12},{12,16},{16,20},{20,24},{24,28},{1,5},{5,9},{9,... | collective-permute-start | bytes 1572872 | tf_op jit(solution)/shard_map/ppermute | solution.py:426
  49.5 6.2 %collective-permute-done.2.got_ref = bf16[1,512,256]{2,1,0:T(8,128)(2,1)S(1)} collective-permute-done((bf16[1,512,256]{2,1,0:T(8,128)(2,1)S(1)}, bf16[1,512,256]{2,1,0:T(8,128)(2,1)S(1)}, u32[]{:S(2)}, u32[]{:S(2)}) %collective-permute-start.2) | collective-permute-done | bytes 262176 | tf_op jit(solution)/shard_map/ppermute | solution.py:456
  55.8 2.0 %collective-permute-start.3 = (bf16[1,512,256]{2,1,0:T(8,128)(2,1)S(1)}, bf16[1,512,256]{2,1,0:T(8,128)(2,1)S(1)}, u32[]{:S(2)}, u32[]{:S(2)}) collective-permute-start(bf16[1,512,256]{2,1,0:T(8,128)(2,1)S(1)} %get-tuple-element.40), channel_id=1, source_target_pairs={{0,16},{4,12},{8,24},{12,4},{16,0},{20,28},{24,8},{28,20},{1,17},{... | collective-permute-start | bytes 786440 | tf_op jit(solution)/shard_map/ppermute | solution.py:456
  58.4 0.5 collective-permute-start.19
  59.0 12.3 %collective-permute-done.3.got_ref = bf16[1,512,256]{2,1,0:T(8,128)(2,1)S(1)} collective-permute-done((bf16[1,512,256]{2,1,0:T(8,128)(2,1)S(1)}, bf16[1,512,256]{2,1,0:T(8,128)(2,1)S(1)}, u32[]{:S(2)}, u32[]{:S(2)}) %collective-permute-start.3) | collective-permute-done | bytes 262176 | tf_op jit(solution)/shard_map/ppermute | solution.py:456
  71.5 1.3 %collective-permute-start.7 = (bf16[1,512,256]{2,1,0:T(8,128)(2,1)S(1)}, bf16[1,512,256]{2,1,0:T(8,128)(2,1)S(1)}, u32[]{:S(2)}, u32[]{:S(2)}) collective-permute-start(bf16[1,512,256]{2,1,0:T(8,128)(2,1)S(1)} %renorm.2.down_ref), channel_id=1, source_target_pairs={{0,4},{4,0},{8,12},{12,8},{16,20},{20,16},{24,28},{28,24},{1,5},{5... | collective-permute-start | bytes 786440 | tf_op jit(solution)/shard_map/ppermute | solution.py:32
  73.3 4.4 %window.1.seen_ref = f32[1024,512]{1,0:T(8,128)S(1)} custom-call(bf16[1024,512]{1,0:T(8,128)(2,1)} %q_ref.7, bf16[1024,512]{1,0:T(8,128)(2,1)} %k_ref.5, bf16[1024,512]{1,0:T(8,128)(2,1)} %v_ref.1, bf16[512,512]{1,0:T(8,128)(2,1)S(1)} %collective-permute-done.tail_ref), custom_call_target="tpu_custom_call" | custom-call | tf_op jit(solution)/shard_map/window/pallas_call | solution.py:267
  77.7 0.6 apply.6
  78.3 4.0 %collective-permute-start.11 = (bf16[256,512]{1,0:T(8,128)(2,1)S(1)}, bf16[256,512]{1,0:T(8,128)(2,1)S(1)}, u32[]{:S(2)}, u32[]{:S(2)}) collective-permute-start(bf16[256,512]{1,0:T(8,128)(2,1)S(1)} %apply.6), channel_id=1, source_target_pairs={{0,3},{1,2},{2,1},{3,0},{4,7},{5,6},{6,5},{7,4},{8,11},{9,10},{10,... | collective-permute-start | bytes 786440 | tf_op jit(solution)/shard_map/ppermute | solution.py:32
  82.3 0.6 apply.5
  83.0 0.6 apply.4
  83.6 6.0 %collective-permute-done.11.x_ref = bf16[256,512]{1,0:T(8,128)(2,1)S(1)} collective-permute-done((bf16[256,512]{1,0:T(8,128)(2,1)S(1)}, bf16[256,512]{1,0:T(8,128)(2,1)S(1)}, u32[]{:S(2)}, u32[]{:S(2)}) %collective-permute-start.11) | collective-permute-done | bytes 262176 | tf_op jit(solution)/shard_map/ppermute | solution.py:32
  89.5 5.2 %collective-permute-start.9 = (bf16[256,512]{1,0:T(8,128)(2,1)S(1)}, bf16[256,512]{1,0:T(8,128)(2,1)S(1)}, u32[]{:S(2)}, u32[]{:S(2)}) collective-permute-start(bf16[256,512]{1,0:T(8,128)(2,1)S(1)} %apply.4), channel_id=1, source_target_pairs={{0,2},{1,3},{2,0},{3,1},{4,6},{5,7},{6,4},{7,5},{8,10},{9,11},{10,... | collective-permute-start | bytes 786440 | tf_op jit(solution)/shard_map/ppermute | solution.py:32
  94.8 0.6 apply.7.x_ref
  95.4 0.7 own_project.1
  96.1 0.7 project.3
  96.9 0.8 project.4
  97.7 8.4 %collective-permute-done.9.x_ref = bf16[256,512]{1,0:T(8,128)(2,1)S(1)} collective-permute-done((bf16[256,512]{1,0:T(8,128)(2,1)S(1)}, bf16[256,512]{1,0:T(8,128)(2,1)S(1)}, u32[]{:S(2)}, u32[]{:S(2)}) %collective-permute-start.9) | collective-permute-done | bytes 262176 | tf_op jit(solution)/shard_map/ppermute | solution.py:32
  106.1 1.6 %project.5 = bf16[256,2048]{1,0:T(8,128)(2,1)} custom-call(bf16[256,512]{1,0:T(8,128)(2,1)S(1)} %collective-permute-done.9.x_ref, f32[256,2048]{1,0:T(8,128)S(1)} %get-tuple-element.53.base_ref, f32[256,1]{1,0:T(8,128)S(1)} %get-tuple-element.54.squares_ref, bf16[256,2048]{1,0:T(8,128)(2,1)S(1)} %collective-permute-done.12.early_ref.near, ...), custom_call_target="tpu_custom_call" | custom-call | tf_op jit(solution)/shard_map/project/pallas_call | solution.py:407
  (46 shorter events, 2.4 us)
Async XLA Ops:
  0.0 4.7 %copy-start.1 = (bf16[1024,512]{1,0:T(8,128)(2,1)S(1)}, bf16[1024,512]{1,0:T(8,128)(2,1)}, u32[]{:S(2)}) copy-start(bf16[1024,512]{1,0:T(8,128)(2,1)} %k_ref.5) | copy-start | bytes 3145732
  0.0 4.7 %copy-start.2 = (bf16[1024,512]{1,0:T(8,128)(2,1)S(1)}, bf16[1024,512]{1,0:T(8,128)(2,1)}, u32[]{:S(2)}) copy-start(bf16[1024,512]{1,0:T(8,128)(2,1)} %v_ref.1) | copy-start | bytes 3145732
  0.0 4.7 %copy-start.7 = (f32[1024,1]{0,1:T(1,128)S(1)}, f32[1024,1]{0,1:T(1,128)}, u32[]{:S(2)}) copy-start(f32[1024,1]{0,1:T(1,128)} %param.12) | copy-start | bytes 12292
  0.0 4.7 %copy-start.4 = (bf16[1,512,512]{2,1,0:T(8,128)(2,1)S(1)}, bf16[1,512,512]{2,1,0:T(8,128)(2,1)}, u32[]{:S(2)}) copy-start(bf16[1,512,512]{2,1,0:T(8,128)(2,1)} %refs_0_.3) | copy-start | bytes 1572868
  0.0 4.7 %copy-start.5 = (bf16[1,512,512]{2,1,0:T(8,128)(2,1)S(1)}, bf16[1,512,512]{2,1,0:T(8,128)(2,1)}, u32[]{:S(2)}) copy-start(bf16[1,512,512]{2,1,0:T(8,128)(2,1)} %refs_1_.1) | copy-start | bytes 1572868
  1.6 5.1 %copy-start.6 = (bf16[1,512,512]{2,1,0:T(8,128)(2,1)S(1)}, bf16[1,512,512]{2,1,0:T(8,128)(2,1)}, u32[]{:S(2)}) copy-start(bf16[1,512,512]{2,1,0:T(8,128)(2,1)} %refs_0_.2) | copy-start | bytes 1572868
  1.6 26.8 %collective-permute-start.12 = (bf16[256,2048]{1,0:T(8,128)(2,1)S(1)}, bf16[256,2048]{1,0:T(8,128)(2,1)S(1)}, u32[]{:S(2)}, u32[]{:S(2)}) collective-permute-start(bf16[256,2048]{1,0:T(8,128)(2,1)S(1)} %get-tuple-element.50), channel_id=1, source_target_pairs={{0,1},{1,0},{2,3},{3,2},{4,6},{5,7},{6,4},{7,5},{8,9},{9,8},{10,11... | collective-permute-start | bytes 3145736 | tf_op jit(solution)/shard_map/ppermute | solution.py:429
  8.5 21.1 %collective-permute-start.4 = (bf16[2,512,256]{2,1,0:T(8,128)(2,1)S(1)}, bf16[2,512,256]{2,1,0:T(8,128)(2,1)S(1)}, u32[]{:S(2)}, u32[]{:S(2)}) collective-permute-start(bf16[2,512,256]{2,1,0:T(8,128)(2,1)S(1)} %get-tuple-element.43), channel_id=1, source_target_pairs={{0,4},{4,0},{8,12},{12,8},{16,20},{20,16},{24,28},{28,24},{1,5},{5... | collective-permute-start | bytes 1572872 | tf_op jit(solution)/shard_map/ppermute | solution.py:32
  28.4 4.4 %collective-permute-start.13 = (bf16[256,2048]{1,0:T(8,128)(2,1)S(1)}, bf16[256,2048]{1,0:T(8,128)(2,1)S(1)}, u32[]{:S(2)}, u32[]{:S(2)}) collective-permute-start(bf16[256,2048]{1,0:T(8,128)(2,1)S(1)} %collective-permute-done.12.early_ref.near), channel_id=1, source_target_pairs={{0,4},{4,0},{8,12},{12,8},{16,20},{20,16},{24,28},{28,24},{1,5},{5... | collective-permute-start | bytes 3145736 | tf_op jit(solution)/shard_map/ppermute | solution.py:32
  29.7 14.1 %collective-permute-start.5 = (bf16[2,512,256]{2,1,0:T(8,128)(2,1)S(1)}, bf16[2,512,256]{2,1,0:T(8,128)(2,1)S(1)}, u32[]{:S(2)}, u32[]{:S(2)}) collective-permute-start(bf16[2,512,256]{2,1,0:T(8,128)(2,1)S(1)} %get-tuple-element.45), channel_id=1, source_target_pairs={{0,8},{4,20},{8,0},{12,28},{16,24},{20,4},{24,16},{28,12},{1,9},{5... | collective-permute-start | bytes 1572872 | tf_op jit(solution)/shard_map/ppermute | solution.py:456
  31.3 27.1 %collective-permute-start.18 = (bf16[256,2048]{1,0:T(8,128)(2,1)S(1)}, bf16[256,2048]{1,0:T(8,128)(2,1)S(1)}, u32[]{:S(2)}, u32[]{:S(2)}) collective-permute-start(bf16[256,2048]{1,0:T(8,128)(2,1)S(1)} %collective-permute-done.12.early_ref.near), channel_id=1, source_target_pairs={{0,16},{4,12},{8,24},{12,4},{16,0},{20,28},{24,8},{28,20},{1,17},{... | collective-permute-start | bytes 3145736 | tf_op jit(solution)/shard_map/ppermute | solution.py:434
  32.8 13.5 %collective-permute-start.1 = (bf16[1,512,256]{2,1,0:T(8,128)(2,1)S(1)}, bf16[1,512,256]{2,1,0:T(8,128)(2,1)S(1)}, u32[]{:S(2)}, u32[]{:S(2)}) collective-permute-start(bf16[1,512,256]{2,1,0:T(8,128)(2,1)S(1)} %get-tuple-element.36), channel_id=1, source_target_pairs={{0,4},{4,0},{8,12},{12,8},{16,20},{20,16},{24,28},{28,24},{1,5},{5... | collective-permute-start | bytes 786440 | tf_op jit(solution)/shard_map/ppermute | solution.py:32
  32.9 22.8 %collective-permute-start.14 = (bf16[256,1024]{1,0:T(8,128)(2,1)S(1)}, bf16[256,1024]{1,0:T(8,128)(2,1)S(1)}, u32[]{:S(2)}, u32[]{:S(2)}) collective-permute-start(bf16[256,1024]{1,0:T(8,128)(2,1)S(1)} %pick.1), channel_id=1, source_target_pairs={{0,1},{1,0},{2,3},{3,2},{4,5},{5,4},{6,7},{7,6},{8,9},{9,8},{10,11... | collective-permute-start | bytes 1572872 | tf_op jit(solution)/shard_map/ppermute | solution.py:32
  43.9 14.1 %collective-permute-start.6 = (bf16[2,512,256]{2,1,0:T(8,128)(2,1)S(1)}, bf16[2,512,256]{2,1,0:T(8,128)(2,1)S(1)}, u32[]{:S(2)}, u32[]{:S(2)}) collective-permute-start(bf16[2,512,256]{2,1,0:T(8,128)(2,1)S(1)} %get-tuple-element.47), channel_id=1, source_target_pairs={{0,16},{4,12},{8,24},{12,4},{16,0},{20,28},{24,8},{28,20},{1,17},{... | collective-permute-start | bytes 1572872 | tf_op jit(solution)/shard_map/ppermute | solution.py:456
  46.4 9.2 %collective-permute-start.2 = (bf16[1,512,256]{2,1,0:T(8,128)(2,1)S(1)}, bf16[1,512,256]{2,1,0:T(8,128)(2,1)S(1)}, u32[]{:S(2)}, u32[]{:S(2)}) collective-permute-start(bf16[1,512,256]{2,1,0:T(8,128)(2,1)S(1)} %get-tuple-element.38), channel_id=1, source_target_pairs={{0,8},{4,20},{8,0},{12,28},{16,24},{20,4},{24,16},{28,12},{1,9},{5... | collective-permute-start | bytes 786440 | tf_op jit(solution)/shard_map/ppermute | solution.py:456
  48.0 24.9 %collective-permute-start = (bf16[512,512]{1,0:T(8,128)(2,1)S(1)}, bf16[512,512]{1,0:T(8,128)(2,1)S(1)}, u32[]{:S(2)}, u32[]{:S(2)}) collective-permute-start(bf16[512,512]{1,0:T(8,128)(2,1)S(1)} %get-tuple-element.30), channel_id=1, source_target_pairs={{0,4},{4,8},{8,12},{12,16},{16,20},{20,24},{24,28},{1,5},{5,9},{9,... | collective-permute-start | bytes 1572872 | tf_op jit(solution)/shard_map/ppermute | solution.py:426
  55.7 17.2 %collective-permute-start.16 = (bf16[256,1024]{1,0:T(8,128)(2,1)S(1)}, bf16[256,1024]{1,0:T(8,128)(2,1)S(1)}, u32[]{:S(2)}, u32[]{:S(2)}) collective-permute-start(bf16[256,1024]{1,0:T(8,128)(2,1)S(1)} %collective-permute-done.14.near), channel_id=1, source_target_pairs={{0,16},{4,12},{8,24},{12,4},{16,0},{20,28},{24,8},{28,20},{1,17},{... | collective-permute-start | bytes 1572872 | tf_op jit(solution)/shard_map/ppermute | solution.py:435
  55.8 15.4 %collective-permute-start.3 = (bf16[1,512,256]{2,1,0:T(8,128)(2,1)S(1)}, bf16[1,512,256]{2,1,0:T(8,128)(2,1)S(1)}, u32[]{:S(2)}, u32[]{:S(2)}) collective-permute-start(bf16[1,512,256]{2,1,0:T(8,128)(2,1)S(1)} %get-tuple-element.40), channel_id=1, source_target_pairs={{0,16},{4,12},{8,24},{12,4},{16,0},{20,28},{24,8},{28,20},{1,17},{... | collective-permute-start | bytes 786440 | tf_op jit(solution)/shard_map/ppermute | solution.py:456
  58.4 38.5 %collective-permute-start.19 = (bf16[256,2048]{1,0:T(8,128)(2,1)S(1)}, bf16[256,2048]{1,0:T(8,128)(2,1)S(1)}, u32[]{:S(2)}, u32[]{:S(2)}) collective-permute-start(bf16[256,2048]{1,0:T(8,128)(2,1)S(1)} %collective-permute-done.18.far), channel_id=1, source_target_pairs={{0,4},{4,0},{8,12},{12,8},{16,20},{20,16},{24,28},{28,24},{1,5},{5... | collective-permute-start | bytes 3145736 | tf_op jit(solution)/shard_map/ppermute | solution.py:32
  58.9 18.8 %collective-permute-start.8 = (bf16[2,512,256]{2,1,0:T(8,128)(2,1)S(1)}, bf16[2,512,256]{2,1,0:T(8,128)(2,1)S(1)}, u32[]{:S(2)}, u32[]{:S(2)}) collective-permute-start(bf16[2,512,256]{2,1,0:T(8,128)(2,1)S(1)} %renorm.3.up_ref), channel_id=1, source_target_pairs={{0,4},{4,0},{8,12},{12,8},{16,20},{20,16},{24,28},{28,24},{1,5},{5... | collective-permute-start | bytes 1572872 | tf_op jit(solution)/shard_map/ppermute | solution.py:32
  71.5 6.3 %copy-start = (bf16[1024,512]{1,0:T(8,128)(2,1)S(1)}, bf16[1024,512]{1,0:T(8,128)(2,1)}, u32[]{:S(2)}) copy-start(bf16[1024,512]{1,0:T(8,128)(2,1)} %q_ref.7) | copy-start | bytes 3145732
  71.5 6.2 %collective-permute-start.7 = (bf16[1,512,256]{2,1,0:T(8,128)(2,1)S(1)}, bf16[1,512,256]{2,1,0:T(8,128)(2,1)S(1)}, u32[]{:S(2)}, u32[]{:S(2)}) collective-permute-start(bf16[1,512,256]{2,1,0:T(8,128)(2,1)S(1)} %renorm.2.down_ref), channel_id=1, source_target_pairs={{0,4},{4,0},{8,12},{12,8},{16,20},{20,16},{24,28},{28,24},{1,5},{5... | collective-permute-start | bytes 786440 | tf_op jit(solution)/shard_map/ppermute | solution.py:32
  72.8 23.3 %collective-permute-start.15 = (bf16[256,1024]{1,0:T(8,128)(2,1)S(1)}, bf16[256,1024]{1,0:T(8,128)(2,1)S(1)}, u32[]{:S(2)}, u32[]{:S(2)}) collective-permute-start(bf16[256,1024]{1,0:T(8,128)(2,1)S(1)} %collective-permute-done.14.near), channel_id=1, source_target_pairs={{0,4},{4,0},{8,12},{12,8},{16,20},{20,16},{24,28},{28,24},{1,5},{5... | collective-permute-start | bytes 1572872 | tf_op jit(solution)/shard_map/ppermute | solution.py:32
  72.9 23.2 %collective-permute-start.17 = (bf16[256,1024]{1,0:T(8,128)(2,1)S(1)}, bf16[256,1024]{1,0:T(8,128)(2,1)S(1)}, u32[]{:S(2)}, u32[]{:S(2)}) collective-permute-start(bf16[256,1024]{1,0:T(8,128)(2,1)S(1)} %collective-permute-done.16.far), channel_id=1, source_target_pairs={{0,4},{4,0},{8,12},{12,8},{16,20},{20,16},{24,28},{28,24},{1,5},{5... | collective-permute-start | bytes 1572872 | tf_op jit(solution)/shard_map/ppermute | solution.py:32
  78.3 11.2 %collective-permute-start.11 = (bf16[256,512]{1,0:T(8,128)(2,1)S(1)}, bf16[256,512]{1,0:T(8,128)(2,1)S(1)}, u32[]{:S(2)}, u32[]{:S(2)}) collective-permute-start(bf16[256,512]{1,0:T(8,128)(2,1)S(1)} %apply.6), channel_id=1, source_target_pairs={{0,3},{1,2},{2,1},{3,0},{4,7},{5,6},{6,5},{7,4},{8,11},{9,10},{10,... | collective-permute-start | bytes 786440 | tf_op jit(solution)/shard_map/ppermute | solution.py:32
  82.9 14.0 %collective-permute-start.10 = (bf16[256,512]{1,0:T(8,128)(2,1)S(1)}, bf16[256,512]{1,0:T(8,128)(2,1)S(1)}, u32[]{:S(2)}, u32[]{:S(2)}) collective-permute-start(bf16[256,512]{1,0:T(8,128)(2,1)S(1)} %apply.5), channel_id=1, source_target_pairs={{0,1},{1,0},{2,3},{3,2},{4,5},{5,4},{6,7},{7,6},{8,9},{9,8},{10,11... | collective-permute-start | bytes 786440 | tf_op jit(solution)/shard_map/ppermute | solution.py:32
  83.5 11.8 %copy-start.3 = (bf16[512,2048]{1,0:T(8,128)(2,1)S(1)}, bf16[512,2048]{1,0:T(8,128)(2,1)}, u32[]{:S(2)}) copy-start(bf16[512,2048]{1,0:T(8,128)(2,1)} %w_ref.1) | copy-start | bytes 6291460
  83.6 11.8 %copy-start.8 = (bf16[512]{0:T(512)(128)(2,1)S(1)}, bf16[512]{0:T(512)(128)(2,1)}, u32[]{:S(2)}) copy-start(bf16[512]{0:T(512)(128)(2,1)} %gain_ref.1) | copy-start | bytes 3076
  89.5 16.6 %collective-permute-start.9 = (bf16[256,512]{1,0:T(8,128)(2,1)S(1)}, bf16[256,512]{1,0:T(8,128)(2,1)S(1)}, u32[]{:S(2)}, u32[]{:S(2)}) collective-permute-start(bf16[256,512]{1,0:T(8,128)(2,1)S(1)} %apply.4), channel_id=1, source_target_pairs={{0,2},{1,3},{2,0},{3,1},{4,6},{5,7},{6,4},{7,5},{8,10},{9,11},{10,... | collective-permute-start | bytes 786440 | tf_op jit(solution)/shard_map/ppermute | solution.py:32
where the time goes:
time: 108 us
  waiting for transfers between devices  61.3 us (57%)
  starting transfers between devices  28.4 us (26%)
  Pallas kernels  17.6 us (16%)
    ppermute x4, waiting for transfers between devices, step(): got = lax.ppermute(send, 'ctx', pairs)  27.5 us
    ppermute x1, waiting for transfers between devices, step(): early = lax.ppermute(piece, ('ctx', 'head'), over)  19.3 us
    ppermute x12, starting transfers between devices, swap(): lax.ppermute(value, axis, [(i, i ^ mask) for i in range(lax.axis_size(axi...  14.6 us
    ppermute x12, waiting for transfers between devices, swap(): lax.ppermute(value, axis, [(i, i ^ mask) for i in range(lax.axis_size(axi...  14.5 us
    ppermute x4, starting transfers between devices, step(): got = lax.ppermute(send, 'ctx', pairs)  7.58 us
    pallas_call x1, Pallas kernels, window(): pl.pallas_call(window_kernel, out_shape=pltpu.VMEM(queries.shape, jnp.flo...  4.37 us
    ppermute x1, starting transfers between devices, step(): early = lax.ppermute(piece, ('ctx', 'head'), over)  3.13 us
    pallas_call x3, Pallas kernels, project(): pl.pallas_call(functools.partial(project_kernel, holder, scale_by), out_s...  3.07 us
  transfers between devices with their start and end apart: 20, of which 7 were waited for; matrix products, arithmetic and copies ran while one was open for 0% of the time, Pallas kernels for 13%

commit v1 on v0

--- a/solution.py
+++ b/solution.py
@@ -98,7 +98,7 @@
     return mine, theirs
 
 
-def forward_kernel(k_ref, v_ref, r_ref, w1_ref, w3_ref, give_ref, act_ref, sc_ref, gs_ref, slope_ref):
+def push_kernel(k_ref, v_ref, r_ref, w1_ref, w2_ref, w3_ref, give_ref, act_ref, sc_ref, g1_ref, g3_ref):
     rows, width = k_ref.shape
     steps = 4
     block = rows // steps
@@ -108,77 +108,50 @@
         gate = dot(k, w1_ref[0])
         up = dot(k, w3_ref[0])
         rate = column(r_ref[:, at], width)
+        scaled = (v_ref[at, :].astype(jnp.float32) * rate).astype(jnp.bfloat16)
+        back = dot(scaled, w2_ref[0], 1, 1)
         s = jax.nn.sigmoid(gate)
         gs = gate * s
         act_ref[at, :] = (gs * up).astype(jnp.bfloat16)
-        sc_ref[at, :] = (v_ref[at, :].astype(jnp.float32) * rate).astype(jnp.bfloat16)
-        gs_ref[at, :] = gs
-        slope_ref[at, :] = up * (s + gs * (1.0 - s))
+        sc_ref[at, :] = scaled
+        g1_ref[at, :] = (back * up * (s + gs * (1.0 - s))).astype(jnp.bfloat16)
+        g3_ref[at, :] = (back * gs).astype(jnp.bfloat16)
     _, theirs = halves(width)
-    give_ref[0] = dot(act_ref[...], sc_ref[:, theirs], 0, 0).astype(jnp.bfloat16)
-
-
-def push_forward(keys, values, rates, w1, w3):
+    for j, ref in enumerate((g1_ref, g3_ref)):
+        give_ref[j] = dot(k_ref[...], ref[:, theirs], 0, 0).astype(jnp.bfloat16)
+
+
+def pushes(keys, values, rates, w1, w2, w3):
     rows, width = keys.shape
-    return pl.pallas_call(
-        forward_kernel,
-        out_shape=[pltpu.VMEM((1, width, width // 2), jnp.bfloat16)]
-        + [pltpu.VMEM((rows, width), jnp.bfloat16)] * 2
-        + [pltpu.VMEM((rows, width), jnp.float32)] * 2,
+    wide = pltpu.VMEM((rows, width), jnp.bfloat16)
+    return pl.pallas_call(
+        push_kernel,
+        out_shape=[pltpu.VMEM((2, width, width // 2), jnp.bfloat16)] + [wide] * 4,
+        compiler_params=grant(16),
+        in_specs=[VMEM] * 6,
+        out_specs=[VMEM] * 5,
+        name="pushes",
+    )(*near_core(keys, values, rates.reshape(1, rows), w1, w2, w3))
+
+
+def contract_kernel(kept, left_ref, *refs):
+    *rights, out_ref = refs
+    mine, theirs = halves(left_ref.shape[1])
+    for j, ref in enumerate(rights):
+        out_ref[j] = dot(left_ref[...], ref[:, mine if kept else theirs], 0, 0).astype(out_ref.dtype)
+
+
+def contract(kept, left, *rights):
+    width = left.shape[1]
+    dtype = jnp.float32 if kept else jnp.bfloat16
+    return pl.pallas_call(
+        functools.partial(contract_kernel, kept),
+        out_shape=pltpu.VMEM((len(rights), width, width // 2), dtype),
         compiler_params=grant(12),
-        in_specs=[VMEM] * 5,
-        out_specs=[VMEM] * 5,
-        name="push_forward",
-    )(*near_core(keys, values, rates.reshape(1, rows), w1, w3))
-
-
-def backward_kernel(k_ref, act_ref, sc_ref, gs_ref, slope_ref, w2_ref, give_ref, keep_ref, g1_ref, g3_ref):
-    rows, width = k_ref.shape
-    steps = 4
-    block = rows // steps
-    for i in range(steps):
-        at = slice(i * block, (i + 1) * block)
-        back = dot(sc_ref[at, :], w2_ref[0], 1, 1)
-        g1_ref[at, :] = (back * slope_ref[at, :]).astype(jnp.bfloat16)
-        g3_ref[at, :] = (back * gs_ref[at, :]).astype(jnp.bfloat16)
-    mine, theirs = halves(width)
-    give_ref[0] = dot(k_ref[...], g1_ref[:, theirs], 0, 0).astype(jnp.bfloat16)
-    give_ref[1] = dot(k_ref[...], g3_ref[:, theirs], 0, 0).astype(jnp.bfloat16)
-    keep_ref[0] = dot(act_ref[...], sc_ref[:, mine], 0, 0)
-
-
-def push_backward(keys, act, scaled, gs, slope, w2):
-    rows, width = keys.shape
-    return pl.pallas_call(
-        backward_kernel,
-        out_shape=[
-            pltpu.VMEM((2, width, width // 2), jnp.bfloat16),
-            pltpu.VMEM((1, width, width // 2), jnp.float32),
-        ]
-        + [pltpu.VMEM((rows, width), jnp.bfloat16)] * 2,
-        compiler_params=grant(12),
-        in_specs=[VMEM] * 6,
-        out_specs=[VMEM] * 4,
-        name="push_backward",
-    )(*near_core(keys, act, scaled, gs, slope, w2))
-
-
-def keep_kernel(k_ref, g1_ref, g3_ref, keep_ref):
-    mine, _ = halves(k_ref.shape[1])
-    for j, ref in enumerate((g1_ref, g3_ref)):
-        keep_ref[j] = dot(k_ref[...], ref[:, mine], 0, 0)
-
-
-def kept(keys, g1, g3):
-    width = keys.shape[1]
-    return pl.pallas_call(
-        keep_kernel,
-        out_shape=pltpu.VMEM((2, width, width // 2), jnp.float32),
-        compiler_params=grant(12),
-        in_specs=[VMEM] * 3,
+        in_specs=[VMEM] * (1 + len(rights)),
         out_specs=VMEM,
-        name="kept",
-    )(*near_core(keys, g1, g3))
+        name="contract",
+    )(*near_core(left, *rights))
 
 
 def add_kernel(keep_ref, got_ref, sum_ref, send_ref):
@@ -439,9 +412,10 @@
     early_pieces = (early, early_c, early_far, early_far_c)
     late_pieces = (late, late_c, late_far, late_far_c)
 
-    give_a, act, scaled, gs, slope = push_forward(keys, values, rates, fast_w1, fast_w3)
-    give_b, keep_a, g1, g3 = push_backward(keys, act, scaled, gs, slope, fast_w2)
-    keep_b = kept(keys, g1, g3)
+    give_a, act, scaled, g1, g3 = pushes(keys, values, rates, fast_w1, fast_w2, fast_w3)
+    give_b = contract(False, act, scaled)
+    keep_a = contract(True, keys, g1, g3)
+    keep_b = contract(True, act, scaled)
 
     masks = [1 << b for b in range(1, bits)]
     crossing = [
@@ -449,7 +423,7 @@
         for forward, backward in zip(masks, masks[::-1])
     ]
     weights = []
-    for give, keep, olds in ((give_a, keep_a, (fast_w2,)), (give_b, keep_b, (fast_w1, fast_w3))):
+    for give, keep, olds in ((give_a, keep_a, (fast_w1, fast_w3)), (give_b, keep_b, (fast_w2,))):
         got = swap(give, "ctx", 1)
         for pairs in crossing:
             keep, send = add(keep, got)
@@ -457,7 +431,7 @@
         mine = renorm(keep, got, *olds)
         other = swap(mine, "ctx", 1)
         weights.append((mine, other))
-    weights = (weights[0][0], weights[1][0], weights[0][1], weights[1][1])
+    weights = (weights[1][0], weights[0][0], weights[1][1], weights[0][1])
 
     seen = window(queries, keys, values, tail)
 

time: 108 us -> 108 us (level)
    pallas_call x3 -> x4, Pallas kernels: 4.45 us -> 4.79 us  [the longest x1 3.07 us: pushes(): pl.pallas_call(push_kernel, out_shape=[pltpu.VMEM((2, width, width // 2),...]
  transfers between devices with their start and end apart: 20 -> 20, of which waited for: 7 -> 6; matrix products, arithmetic and copies ran while one was open for 0% -> 0% of each run, Pallas kernels for 13% -> 14%
where the time goes in v1:
time: 108 us
  waiting for transfers between devices  61 us (56%)
  starting transfers between devices  28.3 us (26%)
  Pallas kernels  18 us (17%)
    ppermute x4, waiting for transfers between devices, step(): got = lax.ppermute(send, 'ctx', pairs)  26.6 us
    ppermute x1, waiting for transfers between devices, step(): early = lax.ppermute(piece, ('ctx', 'head'), over)  19.9 us
    ppermute x12, starting transfers between devices, swap(): lax.ppermute(value, axis, [(i, i ^ mask) for i in range(lax.axis_size(axi...  14.5 us
    ppermute x12, waiting for transfers between devices, swap(): lax.ppermute(value, axis, [(i, i ^ mask) for i in range(lax.axis_size(axi...  14.4 us
    ppermute x4, starting transfers between devices, step(): got = lax.ppermute(send, 'ctx', pairs)  7.62 us
    pallas_call x1, Pallas kernels, window(): pl.pallas_call(window_kernel, out_shape=pltpu.VMEM(queries.shape, jnp.flo...  4.37 us
    ppermute x1, starting transfers between devices, step(): early = lax.ppermute(piece, ('ctx', 'head'), over)  3.13 us
    pallas_call x3, Pallas kernels, project(): pl.pallas_call(functools.partial(project_kernel, holder, scale_by), out_s...  3.07 us
  transfers between devices with their start and end apart: 20, of which 6 were waited for; matrix products, arithmetic and copies ran while one was open for 0% of the time, Pallas kernels for 14%

profile of v1, /device:TPU:0, one launch (start us, length us, event | category | flops | bytes accessed | tf_op | source)
XLA Modules:
  0.0 107.8 jit_solution(10386813302107429076)
XLA Ops:
  0.0 1.6 %load.1 = (bf16[512,512]{1,0:T(8,128)(2,1)S(1)}, bf16[256,2048]{1,0:T(8,128)(2,1)S(1)}) custom-call(bf16[1024,512]{1,0:T(8,128)(2,1)} %left_ref.1, bf16[1024,512]{1,0:T(8,128)(2,1)} %v_ref.1, bf16[512]{0:T(512)(128)(2,1)} %gain_ref.1, bf16[512,2048]{1,0:T(8,128)(2,1)} %w_ref.1), custom_call_target="tpu_custom_call" | custom-call | tf_op jit(solution)/shard_map/load/pallas_call | solution.py:82
  1.6 3.1 %collective-permute-start.12 = (bf16[256,2048]{1,0:T(8,128)(2,1)S(1)}, bf16[256,2048]{1,0:T(8,128)(2,1)S(1)}, u32[]{:S(2)}, u32[]{:S(2)}) collective-permute-start(bf16[256,2048]{1,0:T(8,128)(2,1)S(1)} %get-tuple-element.42), channel_id=1, source_target_pairs={{0,1},{1,0},{2,3},{3,2},{4,6},{5,7},{6,4},{7,5},{8,9},{9,8},{10,11... | collective-permute-start | bytes 3145736 | tf_op jit(solution)/shard_map/ppermute | solution.py:402
  4.8 3.1 %pushes.1 = (bf16[2,512,256]{2,1,0:T(8,128)(2,1)S(1)}, bf16[1024,512]{1,0:T(8,128)(2,1)S(1)}, bf16[1024,512]{1,0:T(8,128)(2,1)S(1)}, bf16[1024,512]{1,0:T(8,128)(2,1)S(1)}, bf16[1024,512]{1,0:T(8,128)(2,1)S(1)}) custom-call(bf16[1024,512]{1,0:T(8,128)(2,1)S(1)} %copy-done.1, bf16[1024,512]{1,0:T(8,128)(2,1)S(1)} %copy-done.2, f32[1,1024]{1,0:T(1,128)S(1)} %bitcast.1, ...), custom_call_target="tpu_custom_call" | custom-call | tf_op jit(solution)/shard_map/pushes/pallas_call | solution.py:127
  7.9 0.6 collective-permute-start.4
  8.5 19.9 %collective-permute-done.12.early_ref.near = bf16[256,2048]{1,0:T(8,128)(2,1)S(1)} collective-permute-done((bf16[256,2048]{1,0:T(8,128)(2,1)S(1)}, bf16[256,2048]{1,0:T(8,128)(2,1)S(1)}, u32[]{:S(2)}, u32[]{:S(2)}) %collective-permute-start.12) | collective-permute-done | bytes 1048608 | tf_op jit(solution)/shard_map/ppermute | solution.py:402
  28.8 0.7 contract.5.keep_ref
  29.7 1.6 %collective-permute-start.5 = (bf16[2,512,256]{2,1,0:T(8,128)(2,1)S(1)}, bf16[2,512,256]{2,1,0:T(8,128)(2,1)S(1)}, u32[]{:S(2)}, u32[]{:S(2)}) collective-permute-start(bf16[2,512,256]{2,1,0:T(8,128)(2,1)S(1)} %get-tuple-element.37), channel_id=1, source_target_pairs={{0,8},{4,20},{8,0},{12,28},{16,24},{20,4},{24,16},{28,12},{1,9},{5... | collective-permute-start | bytes 1572872 | tf_op jit(solution)/shard_map/ppermute | solution.py:430
  31.3 1.5 %collective-permute-start.18 = (bf16[256,2048]{1,0:T(8,128)(2,1)S(1)}, bf16[256,2048]{1,0:T(8,128)(2,1)S(1)}, u32[]{:S(2)}, u32[]{:S(2)}) collective-permute-start(bf16[256,2048]{1,0:T(8,128)(2,1)S(1)} %collective-permute-done.12.early_ref.near), channel_id=1, source_target_pairs={{0,16},{4,12},{8,24},{12,4},{16,0},{20,28},{24,8},{28,20},{1,17},{... | collective-permute-start | bytes 3145736 | tf_op jit(solution)/shard_map/ppermute | solution.py:407
  32.8 0.5 contract.4
  33.5 1.9 %collective-permute-start.14 = (bf16[256,1024]{1,0:T(8,128)(2,1)S(1)}, bf16[256,1024]{1,0:T(8,128)(2,1)S(1)}, u32[]{:S(2)}, u32[]{:S(2)}) collective-permute-start(bf16[256,1024]{1,0:T(8,128)(2,1)S(1)} %pick.1), channel_id=1, source_target_pairs={{0,1},{1,0},{2,3},{3,2},{4,5},{5,4},{6,7},{7,6},{8,9},{9,8},{10,11... | collective-permute-start | bytes 1572872 | tf_op jit(solution)/shard_map/ppermute | solution.py:32
  35.4 8.3 %collective-permute-done.5.got_ref = bf16[2,512,256]{2,1,0:T(8,128)(2,1)S(1)} collective-permute-done((bf16[2,512,256]{2,1,0:T(8,128)(2,1)S(1)}, bf16[2,512,256]{2,1,0:T(8,128)(2,1)S(1)}, u32[]{:S(2)}, u32[]{:S(2)}) %collective-permute-start.5) | collective-permute-done | bytes 524320 | tf_op jit(solution)/shard_map/ppermute | solution.py:430
  43.9 2.4 %collective-permute-start.6 = (bf16[2,512,256]{2,1,0:T(8,128)(2,1)S(1)}, bf16[2,512,256]{2,1,0:T(8,128)(2,1)S(1)}, u32[]{:S(2)}, u32[]{:S(2)}) collective-permute-start(bf16[2,512,256]{2,1,0:T(8,128)(2,1)S(1)} %get-tuple-element.39), channel_id=1, source_target_pairs={{0,16},{4,12},{8,24},{12,4},{16,0},{20,28},{24,8},{28,20},{1,17},{... | collective-permute-start | bytes 1572872 | tf_op jit(solution)/shard_map/ppermute | solution.py:430
  46.3 0.5 contract.3.keep_ref
  46.9 1.6 %collective-permute-start.2 = (bf16[1,512,256]{2,1,0:T(8,128)(2,1)S(1)}, bf16[1,512,256]{2,1,0:T(8,128)(2,1)S(1)}, u32[]{:S(2)}, u32[]{:S(2)}) collective-permute-start(bf16[1,512,256]{2,1,0:T(8,128)(2,1)S(1)} %get-tuple-element.30), channel_id=1, source_target_pairs={{0,8},{4,20},{8,0},{12,28},{16,24},{20,4},{24,16},{28,12},{1,9},{5... | collective-permute-start | bytes 786440 | tf_op jit(solution)/shard_map/ppermute | solution.py:430
  48.5 1.5 %collective-permute-start = (bf16[512,512]{1,0:T(8,128)(2,1)S(1)}, bf16[512,512]{1,0:T(8,128)(2,1)S(1)}, u32[]{:S(2)}, u32[]{:S(2)}) collective-permute-start(bf16[512,512]{1,0:T(8,128)(2,1)S(1)} %get-tuple-element.26), channel_id=1, source_target_pairs={{0,4},{4,8},{8,12},{12,16},{16,20},{20,24},{24,28},{1,5},{5,9},{9,... | collective-permute-start | bytes 1572872 | tf_op jit(solution)/shard_map/ppermute | solution.py:399
  50.0 6.2 %collective-permute-done.2.got_ref = bf16[1,512,256]{2,1,0:T(8,128)(2,1)S(1)} collective-permute-done((bf16[1,512,256]{2,1,0:T(8,128)(2,1)S(1)}, bf16[1,512,256]{2,1,0:T(8,128)(2,1)S(1)}, u32[]{:S(2)}, u32[]{:S(2)}) %collective-permute-start.2) | collective-permute-done | bytes 262176 | tf_op jit(solution)/shard_map/ppermute | solution.py:430
  56.3 2.0 %collective-permute-start.3 = (bf16[1,512,256]{2,1,0:T(8,128)(2,1)S(1)}, bf16[1,512,256]{2,1,0:T(8,128)(2,1)S(1)}, u32[]{:S(2)}, u32[]{:S(2)}) collective-permute-start(bf16[1,512,256]{2,1,0:T(8,128)(2,1)S(1)} %get-tuple-element.32), channel_id=1, source_target_pairs={{0,16},{4,12},{8,24},{12,4},{16,0},{20,28},{24,8},{28,20},{1,17},{... | collective-permute-start | bytes 786440 | tf_op jit(solution)/shard_map/ppermute | solution.py:430
  59.3 12.1 %collective-permute-done.3.got_ref = bf16[1,512,256]{2,1,0:T(8,128)(2,1)S(1)} collective-permute-done((bf16[1,512,256]{2,1,0:T(8,128)(2,1)S(1)}, bf16[1,512,256]{2,1,0:T(8,128)(2,1)S(1)}, u32[]{:S(2)}, u32[]{:S(2)}) %collective-permute-start.3) | collective-permute-done | bytes 262176 | tf_op jit(solution)/shard_map/ppermute | solution.py:430
  71.7 1.1 %collective-permute-start.7 = (bf16[1,512,256]{2,1,0:T(8,128)(2,1)S(1)}, bf16[1,512,256]{2,1,0:T(8,128)(2,1)S(1)}, u32[]{:S(2)}, u32[]{:S(2)}) collective-permute-start(bf16[1,512,256]{2,1,0:T(8,128)(2,1)S(1)} %renorm.2.down_ref), channel_id=1, source_target_pairs={{0,4},{4,0},{8,12},{12,8},{16,20},{20,16},{24,28},{28,24},{1,5},{5... | collective-permute-start | bytes 786440 | tf_op jit(solution)/shard_map/ppermute | solution.py:32
  73.3 4.4 %window.1.seen_ref = f32[1024,512]{1,0:T(8,128)S(1)} custom-call(bf16[1024,512]{1,0:T(8,128)(2,1)} %q_ref.7, bf16[1024,512]{1,0:T(8,128)(2,1)} %left_ref.1, bf16[1024,512]{1,0:T(8,128)(2,1)} %v_ref.1, bf16[512,512]{1,0:T(8,128)(2,1)S(1)} %collective-permute-done.tail_ref), custom_call_target="tpu_custom_call" | custom-call | tf_op jit(solution)/shard_map/window/pallas_call | solution.py:240
  77.7 0.6 apply.6
  78.3 4.0 %collective-permute-start.11 = (bf16[256,512]{1,0:T(8,128)(2,1)S(1)}, bf16[256,512]{1,0:T(8,128)(2,1)S(1)}, u32[]{:S(2)}, u32[]{:S(2)}) collective-permute-start(bf16[256,512]{1,0:T(8,128)(2,1)S(1)} %apply.6), channel_id=1, source_target_pairs={{0,3},{1,2},{2,1},{3,0},{4,7},{5,6},{6,5},{7,4},{8,11},{9,10},{10,... | collective-permute-start | bytes 786440 | tf_op jit(solution)/shard_map/ppermute | solution.py:32
  82.3 0.6 apply.5
  83.0 0.6 apply.4
  83.6 6.0 %collective-permute-done.11.x_ref = bf16[256,512]{1,0:T(8,128)(2,1)S(1)} collective-permute-done((bf16[256,512]{1,0:T(8,128)(2,1)S(1)}, bf16[256,512]{1,0:T(8,128)(2,1)S(1)}, u32[]{:S(2)}, u32[]{:S(2)}) %collective-permute-start.11) | collective-permute-done | bytes 262176 | tf_op jit(solution)/shard_map/ppermute | solution.py:32
  89.5 5.2 %collective-permute-start.9 = (bf16[256,512]{1,0:T(8,128)(2,1)S(1)}, bf16[256,512]{1,0:T(8,128)(2,1)S(1)}, u32[]{:S(2)}, u32[]{:S(2)}) collective-permute-start(bf16[256,512]{1,0:T(8,128)(2,1)S(1)} %apply.4), channel_id=1, source_target_pairs={{0,2},{1,3},{2,0},{3,1},{4,6},{5,7},{6,4},{7,5},{8,10},{9,11},{10,... | collective-permute-start | bytes 786440 | tf_op jit(solution)/shard_map/ppermute | solution.py:32
  94.8 0.6 apply.7.x_ref
  95.4 0.7 own_project.1
  96.1 0.7 project.3
  96.9 0.8 project.4
  97.6 8.4 %collective-permute-done.9.x_ref = bf16[256,512]{1,0:T(8,128)(2,1)S(1)} collective-permute-done((bf16[256,512]{1,0:T(8,128)(2,1)S(1)}, bf16[256,512]{1,0:T(8,128)(2,1)S(1)}, u32[]{:S(2)}, u32[]{:S(2)}) %collective-permute-start.9) | collective-permute-done | bytes 262176 | tf_op jit(solution)/shard_map/ppermute | solution.py:32
  106.1 1.6 %project.5 = bf16[256,2048]{1,0:T(8,128)(2,1)} custom-call(bf16[256,512]{1,0:T(8,128)(2,1)S(1)} %collective-permute-done.9.x_ref, f32[256,2048]{1,0:T(8,128)S(1)} %get-tuple-element.45.base_ref, f32[256,1]{1,0:T(8,128)S(1)} %get-tuple-element.46.squares_ref, bf16[256,2048]{1,0:T(8,128)(2,1)S(1)} %collective-permute-done.12.early_ref.near, ...), custom_call_target="tpu_custom_call" | custom-call | tf_op jit(solution)/shard_map/project/pallas_call | solution.py:380
  (47 shorter events, 2.9 us)
Async XLA Ops:
  0.0 4.7 %copy-start.1 = (bf16[1024,512]{1,0:T(8,128)(2,1)S(1)}, bf16[1024,512]{1,0:T(8,128)(2,1)}, u32[]{:S(2)}) copy-start(bf16[1024,512]{1,0:T(8,128)(2,1)} %left_ref.1) | copy-start | bytes 3145732
  0.0 4.7 %copy-start.2 = (bf16[1024,512]{1,0:T(8,128)(2,1)S(1)}, bf16[1024,512]{1,0:T(8,128)(2,1)}, u32[]{:S(2)}) copy-start(bf16[1024,512]{1,0:T(8,128)(2,1)} %v_ref.1) | copy-start | bytes 3145732
  0.0 4.7 %copy-start.8 = (f32[1024,1]{0,1:T(1,128)S(1)}, f32[1024,1]{0,1:T(1,128)}, u32[]{:S(2)}) copy-start(f32[1024,1]{0,1:T(1,128)} %param.12) | copy-start | bytes 12292
  0.0 4.7 %copy-start.5 = (bf16[1,512,512]{2,1,0:T(8,128)(2,1)S(1)}, bf16[1,512,512]{2,1,0:T(8,128)(2,1)}, u32[]{:S(2)}) copy-start(bf16[1,512,512]{2,1,0:T(8,128)(2,1)} %refs_0_.3) | copy-start | bytes 1572868
  0.0 4.7 %copy-start.4 = (bf16[1,512,512]{2,1,0:T(8,128)(2,1)S(1)}, bf16[1,512,512]{2,1,0:T(8,128)(2,1)}, u32[]{:S(2)}) copy-start(bf16[1,512,512]{2,1,0:T(8,128)(2,1)} %refs_0_.2) | copy-start | bytes 1572868
  0.0 4.8 %copy-start.6 = (bf16[1,512,512]{2,1,0:T(8,128)(2,1)S(1)}, bf16[1,512,512]{2,1,0:T(8,128)(2,1)}, u32[]{:S(2)}) copy-start(bf16[1,512,512]{2,1,0:T(8,128)(2,1)} %refs_1_.1) | copy-start | bytes 1572868
  1.6 26.8 %collective-permute-start.12 = (bf16[256,2048]{1,0:T(8,128)(2,1)S(1)}, bf16[256,2048]{1,0:T(8,128)(2,1)S(1)}, u32[]{:S(2)}, u32[]{:S(2)}) collective-permute-start(bf16[256,2048]{1,0:T(8,128)(2,1)S(1)} %get-tuple-element.42), channel_id=1, source_target_pairs={{0,1},{1,0},{2,3},{3,2},{4,6},{5,7},{6,4},{7,5},{8,9},{9,8},{10,11... | collective-permute-start | bytes 3145736 | tf_op jit(solution)/shard_map/ppermute | solution.py:402
  7.9 21.7 %collective-permute-start.4 = (bf16[2,512,256]{2,1,0:T(8,128)(2,1)S(1)}, bf16[2,512,256]{2,1,0:T(8,128)(2,1)S(1)}, u32[]{:S(2)}, u32[]{:S(2)}) collective-permute-start(bf16[2,512,256]{2,1,0:T(8,128)(2,1)S(1)} %get-tuple-element.35), channel_id=1, source_target_pairs={{0,4},{4,0},{8,12},{12,8},{16,20},{20,16},{24,28},{28,24},{1,5},{5... | collective-permute-start | bytes 1572872 | tf_op jit(solution)/shard_map/ppermute | solution.py:32
  28.4 5.0 %collective-permute-start.13 = (bf16[256,2048]{1,0:T(8,128)(2,1)S(1)}, bf16[256,2048]{1,0:T(8,128)(2,1)S(1)}, u32[]{:S(2)}, u32[]{:S(2)}) collective-permute-start(bf16[256,2048]{1,0:T(8,128)(2,1)S(1)} %collective-permute-done.12.early_ref.near), channel_id=1, source_target_pairs={{0,4},{4,0},{8,12},{12,8},{16,20},{20,16},{24,28},{28,24},{1,5},{5... | collective-permute-start | bytes 3145736 | tf_op jit(solution)/shard_map/ppermute | solution.py:32
  29.7 14.0 %collective-permute-start.5 = (bf16[2,512,256]{2,1,0:T(8,128)(2,1)S(1)}, bf16[2,512,256]{2,1,0:T(8,128)(2,1)S(1)}, u32[]{:S(2)}, u32[]{:S(2)}) collective-permute-start(bf16[2,512,256]{2,1,0:T(8,128)(2,1)S(1)} %get-tuple-element.37), channel_id=1, source_target_pairs={{0,8},{4,20},{8,0},{12,28},{16,24},{20,4},{24,16},{28,12},{1,9},{5... | collective-permute-start | bytes 1572872 | tf_op jit(solution)/shard_map/ppermute | solution.py:430
  31.3 27.5 %collective-permute-start.18 = (bf16[256,2048]{1,0:T(8,128)(2,1)S(1)}, bf16[256,2048]{1,0:T(8,128)(2,1)S(1)}, u32[]{:S(2)}, u32[]{:S(2)}) collective-permute-start(bf16[256,2048]{1,0:T(8,128)(2,1)S(1)} %collective-permute-done.12.early_ref.near), channel_id=1, source_target_pairs={{0,16},{4,12},{8,24},{12,4},{16,0},{20,28},{24,8},{28,20},{1,17},{... | collective-permute-start | bytes 3145736 | tf_op jit(solution)/shard_map/ppermute | solution.py:407
  33.3 13.5 %collective-permute-start.1 = (bf16[1,512,256]{2,1,0:T(8,128)(2,1)S(1)}, bf16[1,512,256]{2,1,0:T(8,128)(2,1)S(1)}, u32[]{:S(2)}, u32[]{:S(2)}) collective-permute-start(bf16[1,512,256]{2,1,0:T(8,128)(2,1)S(1)} %contract.4), channel_id=1, source_target_pairs={{0,4},{4,0},{8,12},{12,8},{16,20},{20,16},{24,28},{28,24},{1,5},{5... | collective-permute-start | bytes 786440 | tf_op jit(solution)/shard_map/ppermute | solution.py:32
  33.5 22.7 %collective-permute-start.14 = (bf16[256,1024]{1,0:T(8,128)(2,1)S(1)}, bf16[256,1024]{1,0:T(8,128)(2,1)S(1)}, u32[]{:S(2)}, u32[]{:S(2)}) collective-permute-start(bf16[256,1024]{1,0:T(8,128)(2,1)S(1)} %pick.1), channel_id=1, source_target_pairs={{0,1},{1,0},{2,3},{3,2},{4,5},{5,4},{6,7},{7,6},{8,9},{9,8},{10,11... | collective-permute-start | bytes 1572872 | tf_op jit(solution)/shard_map/ppermute | solution.py:32
  43.9 14.5 %collective-permute-start.6 = (bf16[2,512,256]{2,1,0:T(8,128)(2,1)S(1)}, bf16[2,512,256]{2,1,0:T(8,128)(2,1)S(1)}, u32[]{:S(2)}, u32[]{:S(2)}) collective-permute-start(bf16[2,512,256]{2,1,0:T(8,128)(2,1)S(1)} %get-tuple-element.39), channel_id=1, source_target_pairs={{0,16},{4,12},{8,24},{12,4},{16,0},{20,28},{24,8},{28,20},{1,17},{... | collective-permute-start | bytes 1572872 | tf_op jit(solution)/shard_map/ppermute | solution.py:430
  46.9 9.2 %collective-permute-start.2 = (bf16[1,512,256]{2,1,0:T(8,128)(2,1)S(1)}, bf16[1,512,256]{2,1,0:T(8,128)(2,1)S(1)}, u32[]{:S(2)}, u32[]{:S(2)}) collective-permute-start(bf16[1,512,256]{2,1,0:T(8,128)(2,1)S(1)} %get-tuple-element.30), channel_id=1, source_target_pairs={{0,8},{4,20},{8,0},{12,28},{16,24},{20,4},{24,16},{28,12},{1,9},{5... | collective-permute-start | bytes 786440 | tf_op jit(solution)/shard_map/ppermute | solution.py:430
  48.5 24.3 %collective-permute-start = (bf16[512,512]{1,0:T(8,128)(2,1)S(1)}, bf16[512,512]{1,0:T(8,128)(2,1)S(1)}, u32[]{:S(2)}, u32[]{:S(2)}) collective-permute-start(bf16[512,512]{1,0:T(8,128)(2,1)S(1)} %get-tuple-element.26), channel_id=1, source_target_pairs={{0,4},{4,8},{8,12},{12,16},{16,20},{20,24},{24,28},{1,5},{5,9},{9,... | collective-permute-start | bytes 1572872 | tf_op jit(solution)/shard_map/ppermute | solution.py:399
  56.2 16.7 %collective-permute-start.16 = (bf16[256,1024]{1,0:T(8,128)(2,1)S(1)}, bf16[256,1024]{1,0:T(8,128)(2,1)S(1)}, u32[]{:S(2)}, u32[]{:S(2)}) collective-permute-start(bf16[256,1024]{1,0:T(8,128)(2,1)S(1)} %collective-permute-done.14.near), channel_id=1, source_target_pairs={{0,16},{4,12},{8,24},{12,4},{16,0},{20,28},{24,8},{28,20},{1,17},{... | collective-permute-start | bytes 1572872 | tf_op jit(solution)/shard_map/ppermute | solution.py:408
  56.3 15.1 %collective-permute-start.3 = (bf16[1,512,256]{2,1,0:T(8,128)(2,1)S(1)}, bf16[1,512,256]{2,1,0:T(8,128)(2,1)S(1)}, u32[]{:S(2)}, u32[]{:S(2)}) collective-permute-start(bf16[1,512,256]{2,1,0:T(8,128)(2,1)S(1)} %get-tuple-element.32), channel_id=1, source_target_pairs={{0,16},{4,12},{8,24},{12,4},{16,0},{20,28},{24,8},{28,20},{1,17},{... | collective-permute-start | bytes 786440 | tf_op jit(solution)/shard_map/ppermute | solution.py:430
  58.8 38.1 %collective-permute-start.19 = (bf16[256,2048]{1,0:T(8,128)(2,1)S(1)}, bf16[256,2048]{1,0:T(8,128)(2,1)S(1)}, u32[]{:S(2)}, u32[]{:S(2)}) collective-permute-start(bf16[256,2048]{1,0:T(8,128)(2,1)S(1)} %collective-permute-done.18.far), channel_id=1, source_target_pairs={{0,4},{4,0},{8,12},{12,8},{16,20},{20,16},{24,28},{28,24},{1,5},{5... | collective-permute-start | bytes 3145736 | tf_op jit(solution)/shard_map/ppermute | solution.py:32
  58.9 18.8 %collective-permute-start.8 = (bf16[2,512,256]{2,1,0:T(8,128)(2,1)S(1)}, bf16[2,512,256]{2,1,0:T(8,128)(2,1)S(1)}, u32[]{:S(2)}, u32[]{:S(2)}) collective-permute-start(bf16[2,512,256]{2,1,0:T(8,128)(2,1)S(1)} %renorm.3.up_ref), channel_id=1, source_target_pairs={{0,4},{4,0},{8,12},{12,8},{16,20},{20,16},{24,28},{28,24},{1,5},{5... | collective-permute-start | bytes 1572872 | tf_op jit(solution)/shard_map/ppermute | solution.py:32
  71.7 6.1 %copy-start = (bf16[1024,512]{1,0:T(8,128)(2,1)S(1)}, bf16[1024,512]{1,0:T(8,128)(2,1)}, u32[]{:S(2)}) copy-start(bf16[1024,512]{1,0:T(8,128)(2,1)} %q_ref.7) | copy-start | bytes 3145732
  71.7 6.0 %collective-permute-start.7 = (bf16[1,512,256]{2,1,0:T(8,128)(2,1)S(1)}, bf16[1,512,256]{2,1,0:T(8,128)(2,1)S(1)}, u32[]{:S(2)}, u32[]{:S(2)}) collective-permute-start(bf16[1,512,256]{2,1,0:T(8,128)(2,1)S(1)} %renorm.2.down_ref), channel_id=1, source_target_pairs={{0,4},{4,0},{8,12},{12,8},{16,20},{20,16},{24,28},{28,24},{1,5},{5... | collective-permute-start | bytes 786440 | tf_op jit(solution)/shard_map/ppermute | solution.py:32
  72.8 23.3 %collective-permute-start.15 = (bf16[256,1024]{1,0:T(8,128)(2,1)S(1)}, bf16[256,1024]{1,0:T(8,128)(2,1)S(1)}, u32[]{:S(2)}, u32[]{:S(2)}) collective-permute-start(bf16[256,1024]{1,0:T(8,128)(2,1)S(1)} %collective-permute-done.14.near), channel_id=1, source_target_pairs={{0,4},{4,0},{8,12},{12,8},{16,20},{20,16},{24,28},{28,24},{1,5},{5... | collective-permute-start | bytes 1572872 | tf_op jit(solution)/shard_map/ppermute | solution.py:32
  72.9 23.2 %collective-permute-start.17 = (bf16[256,1024]{1,0:T(8,128)(2,1)S(1)}, bf16[256,1024]{1,0:T(8,128)(2,1)S(1)}, u32[]{:S(2)}, u32[]{:S(2)}) collective-permute-start(bf16[256,1024]{1,0:T(8,128)(2,1)S(1)} %collective-permute-done.16.far), channel_id=1, source_target_pairs={{0,4},{4,0},{8,12},{12,8},{16,20},{20,16},{24,28},{28,24},{1,5},{5... | collective-permute-start | bytes 1572872 | tf_op jit(solution)/shard_map/ppermute | solution.py:32
  78.3 11.2 %collective-permute-start.11 = (bf16[256,512]{1,0:T(8,128)(2,1)S(1)}, bf16[256,512]{1,0:T(8,128)(2,1)S(1)}, u32[]{:S(2)}, u32[]{:S(2)}) collective-permute-start(bf16[256,512]{1,0:T(8,128)(2,1)S(1)} %apply.6), channel_id=1, source_target_pairs={{0,3},{1,2},{2,1},{3,0},{4,7},{5,6},{6,5},{7,4},{8,11},{9,10},{10,... | collective-permute-start | bytes 786440 | tf_op jit(solution)/shard_map/ppermute | solution.py:32
  82.9 14.0 %collective-permute-start.10 = (bf16[256,512]{1,0:T(8,128)(2,1)S(1)}, bf16[256,512]{1,0:T(8,128)(2,1)S(1)}, u32[]{:S(2)}, u32[]{:S(2)}) collective-permute-start(bf16[256,512]{1,0:T(8,128)(2,1)S(1)} %apply.5), channel_id=1, source_target_pairs={{0,1},{1,0},{2,3},{3,2},{4,5},{5,4},{6,7},{7,6},{8,9},{9,8},{10,11... | collective-permute-start | bytes 786440 | tf_op jit(solution)/shard_map/ppermute | solution.py:32
  83.5 11.8 %copy-start.3 = (bf16[512,2048]{1,0:T(8,128)(2,1)S(1)}, bf16[512,2048]{1,0:T(8,128)(2,1)}, u32[]{:S(2)}) copy-start(bf16[512,2048]{1,0:T(8,128)(2,1)} %w_ref.1) | copy-start | bytes 6291460
  83.6 11.8 %copy-start.7 = (bf16[512]{0:T(512)(128)(2,1)S(1)}, bf16[512]{0:T(512)(128)(2,1)}, u32[]{:S(2)}) copy-start(bf16[512]{0:T(512)(128)(2,1)} %gain_ref.1) | copy-start | bytes 3076
  89.5 16.5 %collective-permute-start.9 = (bf16[256,512]{1,0:T(8,128)(2,1)S(1)}, bf16[256,512]{1,0:T(8,128)(2,1)S(1)}, u32[]{:S(2)}, u32[]{:S(2)}) collective-permute-start(bf16[256,512]{1,0:T(8,128)(2,1)S(1)} %apply.4), channel_id=1, source_target_pairs={{0,2},{1,3},{2,0},{3,1},{4,6},{5,7},{6,4},{7,5},{8,10},{9,11},{10,... | collective-permute-start | bytes 786440 | tf_op jit(solution)/shard_map/ppermute | solution.py:32

commit v2 on v1

--- a/solution.py
+++ b/solution.py
@@ -329,8 +329,7 @@
     )(*near_core(early, early_c))
 
 
-def project_kernel(holder, scale_by, x_ref, base_ref, squares_ref, near, near_c, far, far_c,
-                   out_ref, *rest):
+def project_kernel(holder, scale_by, x_ref, base_ref, squares_ref, near, near_c, far, far_c, out_ref, *rest):
     rows = near.shape[0]
     columns = out_ref.shape[1] // 2
     core, half = place()
@@ -341,19 +340,18 @@
     x = jnp.concatenate([x_ref[:, mine], x_ref[:, theirs]], axis=1)
     scale = lax.rsqrt(squares * scale_by + EPSILON) if scale_by else None
     block = columns // 2
+    split = far.shape[1] == columns
     stores = []
     for side in range(2):
         for j in range(2):
-            if holder is None:
-                w_near, w_far = ((near, far), (near_c, far_c))[side]
-                start = core if side == 0 else 1 - core
-                here = slice(j * block, (j + 1) * block)
-                w = jnp.concatenate([w_near[:, here], w_far[:, here]], axis=0)
-                at = pl.ds(pl.multiple_of(start * columns + j * block, block), block)
+            here = slice(j * block, (j + 1) * block)
+            start = (core if side == 0 else 1 - core) if split else side
+            at = pl.ds(pl.multiple_of(start * columns + j * block, block), block)
+            if split:
+                w_far = (far, far_c)[side][:, here]
             else:
-                at = slice(side * columns + j * block, side * columns + (j + 1) * block)
-                w = [jnp.where(core == holder, a[:, at], b[:, at]) for a, b in ((near, near_c), (far, far_c))]
-                w = jnp.concatenate(w, axis=0)
+                w_far = jnp.where(core == holder, far[:, at], far_c[:, at])
+            w = jnp.concatenate([jnp.where(core == holder, near[:, at], near_c[:, at]), w_far], axis=0)
             total = base_ref[:, at] + dot(x, w)
             if scale_by:
                 ready_ref, sem = rest
@@ -398,19 +396,23 @@
     tail, piece = load(keys, values, norm_gain, out_weight)
     tail = lax.ppermute(tail, "ctx", [(i, i + 1) for i in range(ctx_count - 1)])
 
-    over = [(i, i ^ (2 if i // heads & 1 else 1)) for i in range(ctx_count * heads)]
+    every = range(ctx_count * heads)
+    over = [(i, i ^ (2 if i // heads & 1 else 1)) for i in every]
     early = lax.ppermute(piece, ("ctx", "head"), over)
+    over = [(i, i ^ (1 if i // heads & 1 else 4 * heads)) for i in every]
+    relay = lax.ppermute(early, ("ctx", "head"), over)
+    early_far = lax.ppermute(early, "ctx", [(i, i ^ 2) for i in range(1, ctx_count, 2)])
     early_c = swap(early, "ctx", 1)
-    late = pick(early, early_c)
-    late = swap(late, "head", 1)
-    cross = [(i, i ^ (2 if i & 1 else 4)) for i in range(ctx_count)]
-    early_far = lax.ppermute(early, "ctx", cross)
-    late_far = lax.ppermute(late, "ctx", cross)
-    late_c = swap(late, "ctx", 1)
+    relay_c = swap(relay, "ctx", 1)
+    late = pick(relay, relay_c)
+    late_far = lax.ppermute(late, "ctx", [(i, i ^ (2 if i & 1 else 4)) for i in range(ctx_count)])
     early_far_c = swap(early_far, "ctx", 1)
     late_far_c = swap(late_far, "ctx", 1)
-    early_pieces = (early, early_c, early_far, early_far_c)
-    late_pieces = (late, late_c, late_far, late_far_c)
+    pieces = {
+        1: (0, (early, early_c, relay, relay_c)),
+        2: (1, (early, early_c, early_far, early_far_c)),
+        3: (1, (relay, relay_c, late_far, late_far_c)),
+    }
 
     give_a, act, scaled, g1, g3 = pushes(keys, values, rates, fast_w1, fast_w2, fast_w3)
     give_b = contract(False, act, scaled)
@@ -442,9 +444,9 @@
         blocks[k] = swap(combined, "head", k) if k else combined
     base, squares = own_project(blocks[0], norm_gain, out_weight)
     for k in send_order(heads):
-        holder, pieces = (None, late_pieces) if k == heads - 1 else (k - 1, early_pieces)
         scale_by = 1.0 / (heads * width) if k == send_order(heads)[-1] else None
-        result = project(holder, scale_by, blocks[k], base, squares, pieces)
+        holder, brought = pieces[k]
+        result = project(holder, scale_by, blocks[k], base, squares, brought)
         if scale_by is None:
             base, squares = result
     return result

time: 108 us -> 121 us (1.12)
  starting transfers between devices: 28.3 us -> 46.4 us
  waiting for transfers between devices: 61 us -> 55.8 us
    ppermute x4, waiting for transfers between devices: 26.6 us -> 4.8 us  [step(): got = lax.ppermute(send, 'ctx', pairs)]
    ppermute x12 -> x11, starting transfers between devices: 14.5 us -> 32.6 us  [swap(): lax.ppermute(value, axis, [(i, i ^ mask) for i in range(lax.axis_size(axi...]
    ppermute x2 -> x3, waiting for transfers between devices: 0.01 us -> 11.2 us  [the longest x1 11.1 us: step(): relay = lax.ppermute(early, ('ctx', 'head'), over)]
    ppermute x1, waiting for transfers between devices: 19.9 us -> 23.7 us  [step(): early = lax.ppermute(piece, ('ctx', 'head'), over)]
    ppermute x12 -> x11, waiting for transfers between devices: 14.4 us -> 16.2 us  [swap(): lax.ppermute(value, axis, [(i, i ^ mask) for i in range(lax.axis_size(axi...]
    ppermute x4, starting transfers between devices: 7.62 us -> 6.06 us  [step(): got = lax.ppermute(send, 'ctx', pairs)]
    ppermute x2 -> x3, starting transfers between devices: 1.6 us -> 2.84 us  [the longest x1 1.92 us: step(): relay = lax.ppermute(early, ('ctx', 'head'), over)]
  transfers between devices with their start and end apart: 20 -> 20, of which waited for: 6 -> 8; matrix products, arithmetic and copies ran while one was open for 0% -> 0% of each run, Pallas kernels for 14% -> 12%
where the time goes in v2:
time: 121 us
  waiting for transfers between devices  55.8 us (46%)
  starting transfers between devices  46.4 us (38%)
  Pallas kernels  18.2 us (15%)
    ppermute x11, starting transfers between devices, swap(): lax.ppermute(value, axis, [(i, i ^ mask) for i in range(lax.axis_size(axi...  32.6 us
    ppermute x1, waiting for transfers between devices, step(): early = lax.ppermute(piece, ('ctx', 'head'), over)  23.7 us
    ppermute x11, waiting for transfers between devices, swap(): lax.ppermute(value, axis, [(i, i ^ mask) for i in range(lax.axis_size(axi...  16.2 us
    ppermute x1, waiting for transfers between devices, step(): relay = lax.ppermute(early, ('ctx', 'head'), over)  11.1 us
    ppermute x4, starting transfers between devices, step(): got = lax.ppermute(send, 'ctx', pairs)  6.06 us
    ppermute x4, waiting for transfers between devices, step(): got = lax.ppermute(send, 'ctx', pairs)  4.8 us
    pallas_call x1, Pallas kernels, window(): pl.pallas_call(window_kernel, out_shape=pltpu.VMEM(queries.shape, jnp.flo...  4.36 us
    pallas_call x3, Pallas kernels, project(): pl.pallas_call(functools.partial(project_kernel, holder, scale_by), out_s...  3.15 us
  transfers between devices with their start and end apart: 20, of which 8 were waited for; matrix products, arithmetic and copies ran while one was open for 0% of the time, Pallas kernels for 12%

profile of v2, /device:TPU:0, one launch (start us, length us, event | category | flops | bytes accessed | tf_op | source)
XLA Modules:
  0.0 120.9 jit_solution(2843851405859887813)
XLA Ops:
  0.0 1.6 %load.1 = (bf16[512,512]{1,0:T(8,128)(2,1)S(1)}, bf16[256,2048]{1,0:T(8,128)(2,1)S(1)}) custom-call(bf16[1024,512]{1,0:T(8,128)(2,1)} %left_ref.1, bf16[1024,512]{1,0:T(8,128)(2,1)} %v_ref.1, bf16[512]{0:T(512)(128)(2,1)} %gain_ref.1, bf16[512,2048]{1,0:T(8,128)(2,1)} %w_ref.1), custom_call_target="tpu_custom_call" | custom-call | tf_op jit(solution)/shard_map/load/pallas_call | solution.py:82
  1.6 3.1 %collective-permute-start.12 = (bf16[256,2048]{1,0:T(8,128)(2,1)S(1)}, bf16[256,2048]{1,0:T(8,128)(2,1)S(1)}, u32[]{:S(2)}, u32[]{:S(2)}) collective-permute-start(bf16[256,2048]{1,0:T(8,128)(2,1)S(1)} %get-tuple-element.42), channel_id=1, source_target_pairs={{0,1},{1,0},{2,3},{3,2},{4,6},{5,7},{6,4},{7,5},{8,9},{9,8},{10,11... | collective-permute-start | bytes 3145736 | tf_op jit(solution)/shard_map/ppermute | solution.py:401
  4.7 23.7 %collective-permute-done.12.near = bf16[256,2048]{1,0:T(8,128)(2,1)S(1)} collective-permute-done((bf16[256,2048]{1,0:T(8,128)(2,1)S(1)}, bf16[256,2048]{1,0:T(8,128)(2,1)S(1)}, u32[]{:S(2)}, u32[]{:S(2)}) %collective-permute-start.12) | collective-permute-done | bytes 1048608 | tf_op jit(solution)/shard_map/ppermute | solution.py:401
  28.4 1.9 %collective-permute-start.13 = (bf16[256,2048]{1,0:T(8,128)(2,1)S(1)}, bf16[256,2048]{1,0:T(8,128)(2,1)S(1)}, u32[]{:S(2)}, u32[]{:S(2)}) collective-permute-start(bf16[256,2048]{1,0:T(8,128)(2,1)S(1)} %collective-permute-done.12.near), channel_id=1, source_target_pairs={{0,16},{1,17},{2,18},{3,19},{4,5},{5,4},{6,7},{7,6},{8,24},{9,25},... | collective-permute-start | bytes 3145736 | tf_op jit(solution)/shard_map/ppermute | solution.py:403
  30.4 3.1 %pushes.1 = (bf16[2,512,256]{2,1,0:T(8,128)(2,1)S(1)}, bf16[1024,512]{1,0:T(8,128)(2,1)S(1)}, bf16[1024,512]{1,0:T(8,128)(2,1)S(1)}, bf16[1024,512]{1,0:T(8,128)(2,1)S(1)}, bf16[1024,512]{1,0:T(8,128)(2,1)S(1)}) custom-call(bf16[1024,512]{1,0:T(8,128)(2,1)S(1)} %copy-done.1, bf16[1024,512]{1,0:T(8,128)(2,1)S(1)} %copy-done.2, f32[1,1024]{1,0:T(1,128)S(1)} %bitcast.1, ...), custom_call_target="tpu_custom_call" | custom-call | tf_op jit(solution)/shard_map/pushes/pallas_call | solution.py:127
  33.5 0.7 contract.5.keep_ref
  34.3 1.1 collective-permute-done.4.got_ref
  35.6 1.5 %collective-permute-start.5 = (bf16[2,512,256]{2,1,0:T(8,128)(2,1)S(1)}, bf16[2,512,256]{2,1,0:T(8,128)(2,1)S(1)}, u32[]{:S(2)}, u32[]{:S(2)}) collective-permute-start(bf16[2,512,256]{2,1,0:T(8,128)(2,1)S(1)} %get-tuple-element.37), channel_id=1, source_target_pairs={{0,8},{4,20},{8,0},{12,28},{16,24},{20,4},{24,16},{28,12},{1,9},{5... | collective-permute-start | bytes 1572872 | tf_op jit(solution)/shard_map/ppermute | solution.py:432
  37.1 11.1 %collective-permute-done.13.early_ref.near.far = bf16[256,2048]{1,0:T(8,128)(2,1)S(1)} collective-permute-done((bf16[256,2048]{1,0:T(8,128)(2,1)S(1)}, bf16[256,2048]{1,0:T(8,128)(2,1)S(1)}, u32[]{:S(2)}, u32[]{:S(2)}) %collective-permute-start.13) | collective-permute-done | bytes 1048608 | tf_op jit(solution)/shard_map/ppermute | solution.py:403
  48.3 0.7 collective-permute-start.18
  49.5 3.5 %collective-permute-start.1 = (bf16[1,512,256]{2,1,0:T(8,128)(2,1)S(1)}, bf16[1,512,256]{2,1,0:T(8,128)(2,1)S(1)}, u32[]{:S(2)}, u32[]{:S(2)}) collective-permute-start(bf16[1,512,256]{2,1,0:T(8,128)(2,1)S(1)} %contract.4), channel_id=1, source_target_pairs={{0,4},{4,0},{8,12},{12,8},{16,20},{20,16},{24,28},{28,24},{1,5},{5... | collective-permute-start | bytes 786440 | tf_op jit(solution)/shard_map/ppermute | solution.py:32
  53.5 0.7 collective-permute-done.1.got_ref
  54.8 2.2 %collective-permute-start.6 = (bf16[2,512,256]{2,1,0:T(8,128)(2,1)S(1)}, bf16[2,512,256]{2,1,0:T(8,128)(2,1)S(1)}, u32[]{:S(2)}, u32[]{:S(2)}) collective-permute-start(bf16[2,512,256]{2,1,0:T(8,128)(2,1)S(1)} %get-tuple-element.39), channel_id=1, source_target_pairs={{0,16},{4,12},{8,24},{12,4},{16,0},{20,28},{24,8},{28,20},{1,17},{... | collective-permute-start | bytes 1572872 | tf_op jit(solution)/shard_map/ppermute | solution.py:432
  57.0 1.7 %collective-permute-start = (bf16[512,512]{1,0:T(8,128)(2,1)S(1)}, bf16[512,512]{1,0:T(8,128)(2,1)S(1)}, u32[]{:S(2)}, u32[]{:S(2)}) collective-permute-start(bf16[512,512]{1,0:T(8,128)(2,1)S(1)} %get-tuple-element.26), channel_id=1, source_target_pairs={{0,4},{4,8},{8,12},{12,16},{16,20},{20,24},{24,28},{1,5},{5,9},{9,... | collective-permute-start | bytes 1572872 | tf_op jit(solution)/shard_map/ppermute | solution.py:397
  58.7 4.8 %collective-permute-done.2.got_ref = bf16[1,512,256]{2,1,0:T(8,128)(2,1)S(1)} collective-permute-done((bf16[1,512,256]{2,1,0:T(8,128)(2,1)S(1)}, bf16[1,512,256]{2,1,0:T(8,128)(2,1)S(1)}, u32[]{:S(2)}, u32[]{:S(2)}) %collective-permute-start.2) | collective-permute-done | bytes 262176 | tf_op jit(solution)/shard_map/ppermute | solution.py:432
  63.6 2.0 %collective-permute-start.3 = (bf16[1,512,256]{2,1,0:T(8,128)(2,1)S(1)}, bf16[1,512,256]{2,1,0:T(8,128)(2,1)S(1)}, u32[]{:S(2)}, u32[]{:S(2)}) collective-permute-start(bf16[1,512,256]{2,1,0:T(8,128)(2,1)S(1)} %get-tuple-element.32), channel_id=1, source_target_pairs={{0,16},{4,12},{8,24},{12,4},{16,0},{20,28},{24,8},{28,20},{1,17},{... | collective-permute-start | bytes 786440 | tf_op jit(solution)/shard_map/ppermute | solution.py:432
  66.0 7.4 %collective-permute-start.17 = (bf16[256,2048]{1,0:T(8,128)(2,1)S(1)}, bf16[256,2048]{1,0:T(8,128)(2,1)S(1)}, u32[]{:S(2)}, u32[]{:S(2)}) collective-permute-start(bf16[256,2048]{1,0:T(8,128)(2,1)S(1)} %collective-permute-done.12.near), channel_id=1, source_target_pairs={{0,4},{4,0},{8,12},{12,8},{16,20},{20,16},{24,28},{28,24},{1,5},{5... | collective-permute-start | bytes 3145736 | tf_op jit(solution)/shard_map/ppermute | solution.py:32
  73.8 7.8 %collective-permute-start.8 = (bf16[2,512,256]{2,1,0:T(8,128)(2,1)S(1)}, bf16[2,512,256]{2,1,0:T(8,128)(2,1)S(1)}, u32[]{:S(2)}, u32[]{:S(2)}) collective-permute-start(bf16[2,512,256]{2,1,0:T(8,128)(2,1)S(1)} %renorm.3.up_ref), channel_id=1, source_target_pairs={{0,4},{4,0},{8,12},{12,8},{16,20},{20,16},{24,28},{28,24},{1,5},{5... | collective-permute-start | bytes 1572872 | tf_op jit(solution)/shard_map/ppermute | solution.py:32
  82.4 4.8 %collective-permute-start.16 = (bf16[256,1024]{1,0:T(8,128)(2,1)S(1)}, bf16[256,1024]{1,0:T(8,128)(2,1)S(1)}, u32[]{:S(2)}, u32[]{:S(2)}) collective-permute-start(bf16[256,1024]{1,0:T(8,128)(2,1)S(1)} %collective-permute-done.15.far), channel_id=1, source_target_pairs={{0,4},{4,0},{8,12},{12,8},{16,20},{20,16},{24,28},{28,24},{1,5},{5... | collective-permute-start | bytes 1572872 | tf_op jit(solution)/shard_map/ppermute | solution.py:32
  87.2 4.4 %window.1.seen_ref = f32[1024,512]{1,0:T(8,128)S(1)} custom-call(bf16[1024,512]{1,0:T(8,128)(2,1)} %q_ref.7, bf16[1024,512]{1,0:T(8,128)(2,1)} %left_ref.1, bf16[1024,512]{1,0:T(8,128)(2,1)} %v_ref.1, bf16[512,512]{1,0:T(8,128)(2,1)S(1)} %collective-permute-done.tail_ref), custom_call_target="tpu_custom_call" | custom-call | tf_op jit(solution)/shard_map/window/pallas_call | solution.py:240
  91.6 0.6 apply.6
  92.2 4.2 %collective-permute-start.11 = (bf16[256,512]{1,0:T(8,128)(2,1)S(1)}, bf16[256,512]{1,0:T(8,128)(2,1)S(1)}, u32[]{:S(2)}, u32[]{:S(2)}) collective-permute-start(bf16[256,512]{1,0:T(8,128)(2,1)S(1)} %apply.6), channel_id=1, source_target_pairs={{0,3},{1,2},{2,1},{3,0},{4,7},{5,6},{6,5},{7,4},{8,11},{9,10},{10,... | collective-permute-start | bytes 786440 | tf_op jit(solution)/shard_map/ppermute | solution.py:32
  97.0 0.6 apply.4
  97.6 6.0 %collective-permute-done.11.x_ref = bf16[256,512]{1,0:T(8,128)(2,1)S(1)} collective-permute-done((bf16[256,512]{1,0:T(8,128)(2,1)S(1)}, bf16[256,512]{1,0:T(8,128)(2,1)S(1)}, u32[]{:S(2)}, u32[]{:S(2)}) %collective-permute-start.11) | collective-permute-done | bytes 262176 | tf_op jit(solution)/shard_map/ppermute | solution.py:32
  103.6 4.3 %collective-permute-start.9 = (bf16[256,512]{1,0:T(8,128)(2,1)S(1)}, bf16[256,512]{1,0:T(8,128)(2,1)S(1)}, u32[]{:S(2)}, u32[]{:S(2)}) collective-permute-start(bf16[256,512]{1,0:T(8,128)(2,1)S(1)} %apply.4), channel_id=1, source_target_pairs={{0,2},{1,3},{2,0},{3,1},{4,6},{5,7},{6,4},{7,5},{8,10},{9,11},{10,... | collective-permute-start | bytes 786440 | tf_op jit(solution)/shard_map/ppermute | solution.py:32
  107.9 0.6 apply.7.x_ref
  108.5 0.7 own_project.1
  109.2 0.8 project.3
  110.0 0.9 collective-permute-done.10.x_ref
  110.9 0.8 project.4
  111.7 7.4 %collective-permute-done.9.x_ref = bf16[256,512]{1,0:T(8,128)(2,1)S(1)} collective-permute-done((bf16[256,512]{1,0:T(8,128)(2,1)S(1)}, bf16[256,512]{1,0:T(8,128)(2,1)S(1)}, u32[]{:S(2)}, u32[]{:S(2)}) %collective-permute-start.9) | collective-permute-done | bytes 262176 | tf_op jit(solution)/shard_map/ppermute | solution.py:32
  119.2 1.6 %project.5 = bf16[256,2048]{1,0:T(8,128)(2,1)} custom-call(bf16[256,512]{1,0:T(8,128)(2,1)S(1)} %collective-permute-done.9.x_ref, f32[256,2048]{1,0:T(8,128)S(1)} %get-tuple-element.45.base_ref, f32[256,1]{1,0:T(8,128)S(1)} %get-tuple-element.46.squares_ref, bf16[256,2048]{1,0:T(8,128)(2,1)S(1)} %collective-permute-done.12.near, ...), custom_call_target="tpu_custom_call" | custom-call | tf_op jit(solution)/shard_map/project/pallas_call | solution.py:378
  (47 shorter events, 4.2 us)
Async XLA Ops:
  0.0 30.3 %copy-start.1 = (bf16[1024,512]{1,0:T(8,128)(2,1)S(1)}, bf16[1024,512]{1,0:T(8,128)(2,1)}, u32[]{:S(2)}) copy-start(bf16[1024,512]{1,0:T(8,128)(2,1)} %left_ref.1) | copy-start | bytes 3145732
  0.0 30.3 %copy-start.2 = (bf16[1024,512]{1,0:T(8,128)(2,1)S(1)}, bf16[1024,512]{1,0:T(8,128)(2,1)}, u32[]{:S(2)}) copy-start(bf16[1024,512]{1,0:T(8,128)(2,1)} %v_ref.1) | copy-start | bytes 3145732
  0.0 30.3 %copy-start.8 = (f32[1024,1]{0,1:T(1,128)S(1)}, f32[1024,1]{0,1:T(1,128)}, u32[]{:S(2)}) copy-start(f32[1024,1]{0,1:T(1,128)} %param.12) | copy-start | bytes 12292
  0.0 30.3 %copy-start.5 = (bf16[1,512,512]{2,1,0:T(8,128)(2,1)S(1)}, bf16[1,512,512]{2,1,0:T(8,128)(2,1)}, u32[]{:S(2)}) copy-start(bf16[1,512,512]{2,1,0:T(8,128)(2,1)} %refs_0_.3) | copy-start | bytes 1572868
  0.0 30.3 %copy-start.4 = (bf16[1,512,512]{2,1,0:T(8,128)(2,1)S(1)}, bf16[1,512,512]{2,1,0:T(8,128)(2,1)}, u32[]{:S(2)}) copy-start(bf16[1,512,512]{2,1,0:T(8,128)(2,1)} %refs_0_.2) | copy-start | bytes 1572868
  0.0 30.3 %copy-start.6 = (bf16[1,512,512]{2,1,0:T(8,128)(2,1)S(1)}, bf16[1,512,512]{2,1,0:T(8,128)(2,1)}, u32[]{:S(2)}) copy-start(bf16[1,512,512]{2,1,0:T(8,128)(2,1)} %refs_1_.1) | copy-start | bytes 1572868
  1.6 26.8 %collective-permute-start.12 = (bf16[256,2048]{1,0:T(8,128)(2,1)S(1)}, bf16[256,2048]{1,0:T(8,128)(2,1)S(1)}, u32[]{:S(2)}, u32[]{:S(2)}) collective-permute-start(bf16[256,2048]{1,0:T(8,128)(2,1)S(1)} %get-tuple-element.42), channel_id=1, source_target_pairs={{0,1},{1,0},{2,3},{3,2},{4,6},{5,7},{6,4},{7,5},{8,9},{9,8},{10,11... | collective-permute-start | bytes 3145736 | tf_op jit(solution)/shard_map/ppermute | solution.py:401
  28.4 19.9 %collective-permute-start.13 = (bf16[256,2048]{1,0:T(8,128)(2,1)S(1)}, bf16[256,2048]{1,0:T(8,128)(2,1)S(1)}, u32[]{:S(2)}, u32[]{:S(2)}) collective-permute-start(bf16[256,2048]{1,0:T(8,128)(2,1)S(1)} %collective-permute-done.12.near), channel_id=1, source_target_pairs={{0,16},{1,17},{2,18},{3,19},{4,5},{5,4},{6,7},{7,6},{8,24},{9,25},... | collective-permute-start | bytes 3145736 | tf_op jit(solution)/shard_map/ppermute | solution.py:403
  33.4 2.0 %collective-permute-start.4 = (bf16[2,512,256]{2,1,0:T(8,128)(2,1)S(1)}, bf16[2,512,256]{2,1,0:T(8,128)(2,1)S(1)}, u32[]{:S(2)}, u32[]{:S(2)}) collective-permute-start(bf16[2,512,256]{2,1,0:T(8,128)(2,1)S(1)} %get-tuple-element.35), channel_id=1, source_target_pairs={{0,4},{4,0},{8,12},{12,8},{16,20},{20,16},{24,28},{28,24},{1,5},{5... | collective-permute-start | bytes 1572872 | tf_op jit(solution)/shard_map/ppermute | solution.py:32
  35.6 19.1 %collective-permute-start.5 = (bf16[2,512,256]{2,1,0:T(8,128)(2,1)S(1)}, bf16[2,512,256]{2,1,0:T(8,128)(2,1)S(1)}, u32[]{:S(2)}, u32[]{:S(2)}) collective-permute-start(bf16[2,512,256]{2,1,0:T(8,128)(2,1)S(1)} %get-tuple-element.37), channel_id=1, source_target_pairs={{0,8},{4,20},{8,0},{12,28},{16,24},{20,4},{24,16},{28,12},{1,9},{5... | collective-permute-start | bytes 1572872 | tf_op jit(solution)/shard_map/ppermute | solution.py:432
  48.3 17.3 %collective-permute-start.14 = (bf16[256,2048]{1,0:T(8,128)(2,1)S(1)}, bf16[256,2048]{1,0:T(8,128)(2,1)S(1)}, u32[]{:S(2)}, u32[]{:S(2)}) collective-permute-start(bf16[256,2048]{1,0:T(8,128)(2,1)S(1)} %collective-permute-done.13.early_ref.near.far), channel_id=1, source_target_pairs={{0,4},{4,0},{8,12},{12,8},{16,20},{20,16},{24,28},{28,24},{1,5},{5... | collective-permute-start | bytes 3145736 | tf_op jit(solution)/shard_map/ppermute | solution.py:32
  48.3 33.3 %collective-permute-start.18 = (bf16[256,2048]{1,0:T(8,128)(2,1)S(1)}, bf16[256,2048]{1,0:T(8,128)(2,1)S(1)}, u32[]{:S(2)}, u32[]{:S(2)}) collective-permute-start(bf16[256,2048]{1,0:T(8,128)(2,1)S(1)} %collective-permute-done.12.near), channel_id=1, source_target_pairs={{4,12},{12,4},{20,28},{28,20},{5,13},{13,5},{21,29},{29,21},{6,14}... | collective-permute-start | bytes 3145736 | tf_op jit(solution)/shard_map/ppermute | solution.py:404
  49.5 4.7 %collective-permute-start.1 = (bf16[1,512,256]{2,1,0:T(8,128)(2,1)S(1)}, bf16[1,512,256]{2,1,0:T(8,128)(2,1)S(1)}, u32[]{:S(2)}, u32[]{:S(2)}) collective-permute-start(bf16[1,512,256]{2,1,0:T(8,128)(2,1)S(1)} %contract.4), channel_id=1, source_target_pairs={{0,4},{4,0},{8,12},{12,8},{16,20},{20,16},{24,28},{28,24},{1,5},{5... | collective-permute-start | bytes 786440 | tf_op jit(solution)/shard_map/ppermute | solution.py:32
  54.3 9.2 %collective-permute-start.2 = (bf16[1,512,256]{2,1,0:T(8,128)(2,1)S(1)}, bf16[1,512,256]{2,1,0:T(8,128)(2,1)S(1)}, u32[]{:S(2)}, u32[]{:S(2)}) collective-permute-start(bf16[1,512,256]{2,1,0:T(8,128)(2,1)S(1)} %get-tuple-element.30), channel_id=1, source_target_pairs={{0,8},{4,20},{8,0},{12,28},{16,24},{20,4},{24,16},{28,12},{1,9},{5... | collective-permute-start | bytes 786440 | tf_op jit(solution)/shard_map/ppermute | solution.py:432
  54.8 11.2 %collective-permute-start.6 = (bf16[2,512,256]{2,1,0:T(8,128)(2,1)S(1)}, bf16[2,512,256]{2,1,0:T(8,128)(2,1)S(1)}, u32[]{:S(2)}, u32[]{:S(2)}) collective-permute-start(bf16[2,512,256]{2,1,0:T(8,128)(2,1)S(1)} %get-tuple-element.39), channel_id=1, source_target_pairs={{0,16},{4,12},{8,24},{12,4},{16,0},{20,28},{24,8},{28,20},{1,17},{... | collective-permute-start | bytes 1572872 | tf_op jit(solution)/shard_map/ppermute | solution.py:432
  57.0 24.8 %collective-permute-start = (bf16[512,512]{1,0:T(8,128)(2,1)S(1)}, bf16[512,512]{1,0:T(8,128)(2,1)S(1)}, u32[]{:S(2)}, u32[]{:S(2)}) collective-permute-start(bf16[512,512]{1,0:T(8,128)(2,1)S(1)} %get-tuple-element.26), channel_id=1, source_target_pairs={{0,4},{4,8},{8,12},{12,16},{16,20},{20,24},{24,28},{1,5},{5,9},{9,... | collective-permute-start | bytes 1572872 | tf_op jit(solution)/shard_map/ppermute | solution.py:397
  63.6 10.2 %collective-permute-start.3 = (bf16[1,512,256]{2,1,0:T(8,128)(2,1)S(1)}, bf16[1,512,256]{2,1,0:T(8,128)(2,1)S(1)}, u32[]{:S(2)}, u32[]{:S(2)}) collective-permute-start(bf16[1,512,256]{2,1,0:T(8,128)(2,1)S(1)} %get-tuple-element.32), channel_id=1, source_target_pairs={{0,16},{4,12},{8,24},{12,4},{16,0},{20,28},{24,8},{28,20},{1,17},{... | collective-permute-start | bytes 786440 | tf_op jit(solution)/shard_map/ppermute | solution.py:432
  65.8 16.6 %collective-permute-start.15 = (bf16[256,1024]{1,0:T(8,128)(2,1)S(1)}, bf16[256,1024]{1,0:T(8,128)(2,1)S(1)}, u32[]{:S(2)}, u32[]{:S(2)}) collective-permute-start(bf16[256,1024]{1,0:T(8,128)(2,1)S(1)} %pick.1), channel_id=1, source_target_pairs={{0,16},{4,12},{8,24},{12,4},{16,0},{20,28},{24,8},{28,20},{1,17},{... | collective-permute-start | bytes 1572872 | tf_op jit(solution)/shard_map/ppermute | solution.py:408
  66.0 44.0 %collective-permute-start.17 = (bf16[256,2048]{1,0:T(8,128)(2,1)S(1)}, bf16[256,2048]{1,0:T(8,128)(2,1)S(1)}, u32[]{:S(2)}, u32[]{:S(2)}) collective-permute-start(bf16[256,2048]{1,0:T(8,128)(2,1)S(1)} %collective-permute-done.12.near), channel_id=1, source_target_pairs={{0,4},{4,0},{8,12},{12,8},{16,20},{20,16},{24,28},{28,24},{1,5},{5... | collective-permute-start | bytes 3145736 | tf_op jit(solution)/shard_map/ppermute | solution.py:32
  73.8 17.8 %collective-permute-start.8 = (bf16[2,512,256]{2,1,0:T(8,128)(2,1)S(1)}, bf16[2,512,256]{2,1,0:T(8,128)(2,1)S(1)}, u32[]{:S(2)}, u32[]{:S(2)}) collective-permute-start(bf16[2,512,256]{2,1,0:T(8,128)(2,1)S(1)} %renorm.3.up_ref), channel_id=1, source_target_pairs={{0,4},{4,0},{8,12},{12,8},{16,20},{20,16},{24,28},{28,24},{1,5},{5... | collective-permute-start | bytes 1572872 | tf_op jit(solution)/shard_map/ppermute | solution.py:32
  81.6 37.6 %collective-permute-start.19 = (bf16[256,2048]{1,0:T(8,128)(2,1)S(1)}, bf16[256,2048]{1,0:T(8,128)(2,1)S(1)}, u32[]{:S(2)}, u32[]{:S(2)}) collective-permute-start(bf16[256,2048]{1,0:T(8,128)(2,1)S(1)} %collective-permute-done.18.far), channel_id=1, source_target_pairs={{0,4},{4,0},{8,12},{12,8},{16,20},{20,16},{24,28},{28,24},{1,5},{5... | collective-permute-start | bytes 3145736 | tf_op jit(solution)/shard_map/ppermute | solution.py:32
  81.8 9.8 %copy-start = (bf16[1024,512]{1,0:T(8,128)(2,1)S(1)}, bf16[1024,512]{1,0:T(8,128)(2,1)}, u32[]{:S(2)}) copy-start(bf16[1024,512]{1,0:T(8,128)(2,1)} %q_ref.7) | copy-start | bytes 3145732
  81.8 9.7 %collective-permute-start.7 = (bf16[1,512,256]{2,1,0:T(8,128)(2,1)S(1)}, bf16[1,512,256]{2,1,0:T(8,128)(2,1)S(1)}, u32[]{:S(2)}, u32[]{:S(2)}) collective-permute-start(bf16[1,512,256]{2,1,0:T(8,128)(2,1)S(1)} %renorm.2.down_ref), channel_id=1, source_target_pairs={{0,4},{4,0},{8,12},{12,8},{16,20},{20,16},{24,28},{28,24},{1,5},{5... | collective-permute-start | bytes 786440 | tf_op jit(solution)/shard_map/ppermute | solution.py:32
  82.4 26.8 %collective-permute-start.16 = (bf16[256,1024]{1,0:T(8,128)(2,1)S(1)}, bf16[256,1024]{1,0:T(8,128)(2,1)S(1)}, u32[]{:S(2)}, u32[]{:S(2)}) collective-permute-start(bf16[256,1024]{1,0:T(8,128)(2,1)S(1)} %collective-permute-done.15.far), channel_id=1, source_target_pairs={{0,4},{4,0},{8,12},{12,8},{16,20},{20,16},{24,28},{28,24},{1,5},{5... | collective-permute-start | bytes 1572872 | tf_op jit(solution)/shard_map/ppermute | solution.py:32
  92.2 11.4 %collective-permute-start.11 = (bf16[256,512]{1,0:T(8,128)(2,1)S(1)}, bf16[256,512]{1,0:T(8,128)(2,1)S(1)}, u32[]{:S(2)}, u32[]{:S(2)}) collective-permute-start(bf16[256,512]{1,0:T(8,128)(2,1)S(1)} %apply.6), channel_id=1, source_target_pairs={{0,3},{1,2},{2,1},{3,0},{4,7},{5,6},{6,5},{7,4},{8,11},{9,10},{10,... | collective-permute-start | bytes 786440 | tf_op jit(solution)/shard_map/ppermute | solution.py:32
  96.9 14.0 %collective-permute-start.10 = (bf16[256,512]{1,0:T(8,128)(2,1)S(1)}, bf16[256,512]{1,0:T(8,128)(2,1)S(1)}, u32[]{:S(2)}, u32[]{:S(2)}) collective-permute-start(bf16[256,512]{1,0:T(8,128)(2,1)S(1)} %apply.5), channel_id=1, source_target_pairs={{0,1},{1,0},{2,3},{3,2},{4,5},{5,4},{6,7},{7,6},{8,9},{9,8},{10,11... | collective-permute-start | bytes 786440 | tf_op jit(solution)/shard_map/ppermute | solution.py:32
  97.6 10.9 %copy-start.3 = (bf16[512,2048]{1,0:T(8,128)(2,1)S(1)}, bf16[512,2048]{1,0:T(8,128)(2,1)}, u32[]{:S(2)}) copy-start(bf16[512,2048]{1,0:T(8,128)(2,1)} %w_ref.1) | copy-start | bytes 6291460
  97.6 10.9 %copy-start.7 = (bf16[512]{0:T(512)(128)(2,1)S(1)}, bf16[512]{0:T(512)(128)(2,1)}, u32[]{:S(2)}) copy-start(bf16[512]{0:T(512)(128)(2,1)} %gain_ref.1) | copy-start | bytes 3076
  103.6 15.6 %collective-permute-start.9 = (bf16[256,512]{1,0:T(8,128)(2,1)S(1)}, bf16[256,512]{1,0:T(8,128)(2,1)S(1)}, u32[]{:S(2)}, u32[]{:S(2)}) collective-permute-start(bf16[256,512]{1,0:T(8,128)(2,1)S(1)} %apply.4), channel_id=1, source_target_pairs={{0,2},{1,3},{2,0},{3,1},{4,6},{5,7},{6,4},{7,5},{8,10},{9,11},{10,... | collective-permute-start | bytes 786440 | tf_op jit(solution)/shard_map/ppermute | solution.py:32

commit v3 on v2

--- a/solution.py
+++ b/solution.py
@@ -299,39 +299,36 @@
     )(*near_core(x, gain, weight))
 
 
-def pick_kernel(early_ref, early_c_ref, out_ref, sem):
-    columns = out_ref.shape[1]
-    core, _ = place()
-    here = pl.ds(pl.multiple_of(core * columns, columns), columns)
-
-    @pl.when(core == 1)
-    def _():
-        copy = pltpu.make_async_copy(early_ref.at[:, here], out_ref, sem)
+def split_kernel(whole_ref, left_ref, right_ref, sem):
+    columns = left_ref.shape[1]
+    copies = [
+        pltpu.make_async_copy(whole_ref.at[:, pl.ds(j * columns, columns)], out, sem.at[j])
+        for j, out in enumerate((left_ref, right_ref))
+    ]
+    for copy in copies:
         copy.start()
+    for copy in copies:
         copy.wait()
 
-    @pl.when(core == 0)
-    def _():
-        copy = pltpu.make_async_copy(early_c_ref.at[:, here], out_ref, sem)
-        copy.start()
-        copy.wait()
-
-
-def pick(early, early_c):
-    return pl.pallas_call(
-        pick_kernel,
-        out_shape=pltpu.VMEM((early.shape[0], early.shape[1] // 2), early.dtype),
+
+def split(whole):
+    half = pltpu.VMEM((whole.shape[0], whole.shape[1] // 2), whole.dtype)
+    return pl.pallas_call(
+        split_kernel,
+        out_shape=(half, half),
         compiler_params=grant(4),
-        in_specs=[VMEM] * 2,
-        out_specs=VMEM,
-        scratch_shapes=[pltpu.SemaphoreType.DMA],
-        name="pick",
-    )(*near_core(early, early_c))
-
-
-def project_kernel(holder, scale_by, x_ref, base_ref, squares_ref, near, near_c, far, far_c, out_ref, *rest):
-    rows = near.shape[0]
-    columns = out_ref.shape[1] // 2
+        in_specs=[VMEM],
+        out_specs=(VMEM, VMEM),
+        scratch_shapes=[pltpu.SemaphoreType.DMA((2,))],
+        name="split",
+    )(*near_core(whole))
+
+
+def project_kernel(holder, scale_by, x_ref, base_ref, squares_ref, *refs):
+    count = (len(refs) - (3 if scale_by else 2)) // 2
+    brought, copied = refs[:count], refs[count : 2 * count]
+    out_ref, *rest = refs[2 * count :]
+    rows, columns = brought[0].shape
     core, half = place()
     wide = x_ref[...].astype(jnp.float32)
     squares = squares_ref[...] + jnp.sum(wide * wide, axis=1, keepdims=True)
@@ -339,28 +336,22 @@
     theirs = pl.ds(pl.multiple_of((1 - half) * rows, rows), rows)
     x = jnp.concatenate([x_ref[:, mine], x_ref[:, theirs]], axis=1)
     scale = lax.rsqrt(squares * scale_by + EPSILON) if scale_by else None
-    block = columns // 2
-    split = far.shape[1] == columns
+    block = columns // 4
     stores = []
-    for side in range(2):
-        for j in range(2):
-            here = slice(j * block, (j + 1) * block)
-            start = (core if side == 0 else 1 - core) if split else side
-            at = pl.ds(pl.multiple_of(start * columns + j * block, block), block)
-            if split:
-                w_far = (far, far_c)[side][:, here]
-            else:
-                w_far = jnp.where(core == holder, far[:, at], far_c[:, at])
-            w = jnp.concatenate([jnp.where(core == holder, near[:, at], near_c[:, at]), w_far], axis=0)
-            total = base_ref[:, at] + dot(x, w)
-            if scale_by:
-                ready_ref, sem = rest
-                ready_ref[2 * side + j] = (total * scale).astype(jnp.bfloat16)
-                store = pltpu.make_async_copy(ready_ref.at[2 * side + j], out_ref.at[:, at], sem.at[2 * side + j])
-                store.start()
-                stores.append(store)
-            else:
-                out_ref[:, at] = total
+    for j in range(4):
+        at = slice(j * block, (j + 1) * block)
+        far, here = (1, at) if count == 2 else (1 + j // 2, slice(j % 2 * block, (j % 2 + 1) * block))
+        w_near = jnp.where(core == holder, brought[0][:, at], copied[0][:, at])
+        w_far = jnp.where(core == holder, brought[far][:, here], copied[far][:, here])
+        total = base_ref[:, at] + dot(x, jnp.concatenate([w_near, w_far], axis=0))
+        if scale_by:
+            ready_ref, sem = rest
+            ready_ref[j] = (total * scale).astype(jnp.bfloat16)
+            store = pltpu.make_async_copy(ready_ref.at[j], out_ref.at[:, pl.ds(j * block, block)], sem.at[j])
+            store.start()
+            stores.append(store)
+        else:
+            out_ref[:, at] = total
     if not scale_by:
         rest[0][...] = squares
     for store in stores:
@@ -378,7 +369,7 @@
     return pl.pallas_call(
         functools.partial(project_kernel, holder, scale_by),
         out_shape=shape,
-        in_specs=[VMEM] * 7,
+        in_specs=[VMEM] * (3 + len(pieces)),
         out_specs=HBM if scale_by else (VMEM, VMEM),
         scratch_shapes=scratch,
         compiler_params=grant(16),
@@ -404,14 +395,16 @@
     early_far = lax.ppermute(early, "ctx", [(i, i ^ 2) for i in range(1, ctx_count, 2)])
     early_c = swap(early, "ctx", 1)
     relay_c = swap(relay, "ctx", 1)
-    late = pick(relay, relay_c)
-    late_far = lax.ppermute(late, "ctx", [(i, i ^ (2 if i & 1 else 4)) for i in range(ctx_count)])
+    left, right = split(relay)
+    late_x = lax.ppermute(left, "ctx", [(i, i ^ 2) for i in range(1, ctx_count, 2)])
+    late_y = lax.ppermute(right, "ctx", [(i, i ^ 4) for i in range(1, ctx_count, 2)])
     early_far_c = swap(early_far, "ctx", 1)
-    late_far_c = swap(late_far, "ctx", 1)
+    late_x_c = swap(late_x, "ctx", 1)
+    late_y_c = swap(late_y, "ctx", 1)
     pieces = {
-        1: (0, (early, early_c, relay, relay_c)),
-        2: (1, (early, early_c, early_far, early_far_c)),
-        3: (1, (relay, relay_c, late_far, late_far_c)),
+        1: (0, (early, relay, early_c, relay_c)),
+        2: (1, (early, early_far, early_c, early_far_c)),
+        3: (1, (relay, late_x, late_y, relay_c, late_x_c, late_y_c)),
     }
 
     give_a, act, scaled, g1, g3 = pushes(keys, values, rates, fast_w1, fast_w2, fast_w3)
@@ -443,8 +436,8 @@
         combined = apply_fast(k, queries, seen, weights, rows)
         blocks[k] = swap(combined, "head", k) if k else combined
     base, squares = own_project(blocks[0], norm_gain, out_weight)
-    for k in send_order(heads):
-        scale_by = 1.0 / (heads * width) if k == send_order(heads)[-1] else None
+    for k in (1, 3, 2):
+        scale_by = 1.0 / (heads * width) if k == 2 else None
         holder, brought = pieces[k]
         result = project(holder, scale_by, blocks[k], base, squares, brought)
         if scale_by is None:

time: 121 us -> 111 us (0.917)
  starting transfers between devices: 46.4 us -> 28.9 us
  waiting for transfers between devices: 55.8 us -> 62.2 us
    ppermute x11 -> x12, starting transfers between devices: 32.6 us -> 12.9 us  [swap(): lax.ppermute(value, axis, [(i, i ^ mask) for i in range(lax.axis_size(axi...]
    ppermute x4, waiting for transfers between devices: 4.8 us -> 20.2 us  [step(): got = lax.ppermute(send, 'ctx', pairs)]
    ppermute x1, waiting for transfers between devices: 11.1 us -> 0.01 us  [step(): relay = lax.ppermute(early, ('ctx', 'head'), over)]
    ppermute x11 -> x12, waiting for transfers between devices: 16.2 us -> 26 us  [swap(): lax.ppermute(value, axis, [(i, i ^ mask) for i in range(lax.axis_size(axi...]
    ppermute x1, waiting for transfers between devices: 23.7 us -> 16 us  [step(): early = lax.ppermute(piece, ('ctx', 'head'), over)]
    ppermute x1 -> x2, starting transfers between devices: 0.2 us -> 1.69 us  [the longest x1 1.01 us: step(): lax.ppermute(right, 'ctx', [(i, i ^ 4) for i in range(1, ctx_count, 2)])]
  transfers between devices with their start and end apart: 20 -> 22, of which waited for: 8 -> 9; matrix products, arithmetic and copies ran while one was open for 0% -> 0% of each run, Pallas kernels for 12% -> 14%
where the time goes in v3:
time: 111 us; the launch traced here: 110 us
  waiting for transfers between devices  62.2 us (56%)
  starting transfers between devices  28.9 us (26%)
  Pallas kernels  18.1 us (16%)
    ppermute x12, waiting for transfers between devices, swap(): lax.ppermute(value, axis, [(i, i ^ mask) for i in range(lax.axis_size(axi...  26 us
    ppermute x4, waiting for transfers between devices, step(): got = lax.ppermute(send, 'ctx', pairs)  20.2 us
    ppermute x1, waiting for transfers between devices, step(): early = lax.ppermute(piece, ('ctx', 'head'), over)  16 us
    ppermute x12, starting transfers between devices, swap(): lax.ppermute(value, axis, [(i, i ^ mask) for i in range(lax.axis_size(axi...  12.9 us
    ppermute x4, starting transfers between devices, step(): got = lax.ppermute(send, 'ctx', pairs)  5.61 us
    pallas_call x1, Pallas kernels, window(): pl.pallas_call(window_kernel, out_shape=pltpu.VMEM(queries.shape, jnp.flo...  4.37 us
    pallas_call x3, Pallas kernels, project(): pl.pallas_call(functools.partial(project_kernel, holder, scale_by), out_s...  3.14 us
    ppermute x1, starting transfers between devices, step(): early = lax.ppermute(piece, ('ctx', 'head'), over)  3.13 us
  transfers between devices with their start and end apart: 22, of which 9 were waited for; matrix products, arithmetic and copies ran while one was open for 0% of the time, Pallas kernels for 14%

profile of v3, /device:TPU:0, one launch (start us, length us, event | category | flops | bytes accessed | tf_op | source)
XLA Modules:
  0.0 110.4 jit_solution(7873554296391121482)
XLA Ops:
  0.0 1.6 %load.1 = (bf16[512,512]{1,0:T(8,128)(2,1)S(1)}, bf16[256,2048]{1,0:T(8,128)(2,1)S(1)}) custom-call(bf16[1024,512]{1,0:T(8,128)(2,1)} %left_ref.1, bf16[1024,512]{1,0:T(8,128)(2,1)} %v_ref.1, bf16[512]{0:T(512)(128)(2,1)} %gain_ref.1, bf16[512,2048]{1,0:T(8,128)(2,1)} %w_ref.1), custom_call_target="tpu_custom_call" | custom-call | tf_op jit(solution)/shard_map/load/pallas_call | solution.py:82
  1.6 3.1 %collective-permute-start.12 = (bf16[256,2048]{1,0:T(8,128)(2,1)S(1)}, bf16[256,2048]{1,0:T(8,128)(2,1)S(1)}, u32[]{:S(2)}, u32[]{:S(2)}) collective-permute-start(bf16[256,2048]{1,0:T(8,128)(2,1)S(1)} %get-tuple-element.44), channel_id=1, source_target_pairs={{0,1},{1,0},{2,3},{3,2},{4,6},{5,7},{6,4},{7,5},{8,9},{9,8},{10,11... | collective-permute-start | bytes 3145736 | tf_op jit(solution)/shard_map/ppermute | solution.py:392
  4.8 3.1 %pushes.1 = (bf16[2,512,256]{2,1,0:T(8,128)(2,1)S(1)}, bf16[1024,512]{1,0:T(8,128)(2,1)S(1)}, bf16[1024,512]{1,0:T(8,128)(2,1)S(1)}, bf16[1024,512]{1,0:T(8,128)(2,1)S(1)}, bf16[1024,512]{1,0:T(8,128)(2,1)S(1)}) custom-call(bf16[1024,512]{1,0:T(8,128)(2,1)S(1)} %copy-done.1, bf16[1024,512]{1,0:T(8,128)(2,1)S(1)} %copy-done.2, f32[1,1024]{1,0:T(1,128)S(1)} %bitcast.1, ...), custom_call_target="tpu_custom_call" | custom-call | tf_op jit(solution)/shard_map/pushes/pallas_call | solution.py:127
  7.9 0.6 collective-permute-start.4
  8.5 0.7 contract.5.keep_ref
  9.2 0.8 collective-permute-done.4.got_ref
  10.2 1.6 %collective-permute-start.5 = (bf16[2,512,256]{2,1,0:T(8,128)(2,1)S(1)}, bf16[2,512,256]{2,1,0:T(8,128)(2,1)S(1)}, u32[]{:S(2)}, u32[]{:S(2)}) collective-permute-start(bf16[2,512,256]{2,1,0:T(8,128)(2,1)S(1)} %get-tuple-element.39), channel_id=1, source_target_pairs={{0,8},{4,20},{8,0},{12,28},{16,24},{20,4},{24,16},{28,12},{1,9},{5... | collective-permute-start | bytes 1572872 | tf_op jit(solution)/shard_map/ppermute | solution.py:425
  12.4 16.0 %collective-permute-done.12.refs_0_ = bf16[256,2048]{1,0:T(8,128)(2,1)S(1)} collective-permute-done((bf16[256,2048]{1,0:T(8,128)(2,1)S(1)}, bf16[256,2048]{1,0:T(8,128)(2,1)S(1)}, u32[]{:S(2)}, u32[]{:S(2)}) %collective-permute-start.12) | collective-permute-done | bytes 1048608 | tf_op jit(solution)/shard_map/ppermute | solution.py:392
  28.4 1.9 %collective-permute-start.13 = (bf16[256,2048]{1,0:T(8,128)(2,1)S(1)}, bf16[256,2048]{1,0:T(8,128)(2,1)S(1)}, u32[]{:S(2)}, u32[]{:S(2)}) collective-permute-start(bf16[256,2048]{1,0:T(8,128)(2,1)S(1)} %collective-permute-done.12.refs_0_), channel_id=1, source_target_pairs={{0,16},{1,17},{2,18},{3,19},{4,5},{5,4},{6,7},{7,6},{8,24},{9,25},... | collective-permute-start | bytes 3145736 | tf_op jit(solution)/shard_map/ppermute | solution.py:394
  31.2 1.9 %collective-permute-start.2 = (bf16[1,512,256]{2,1,0:T(8,128)(2,1)S(1)}, bf16[1,512,256]{2,1,0:T(8,128)(2,1)S(1)}, u32[]{:S(2)}, u32[]{:S(2)}) collective-permute-start(bf16[1,512,256]{2,1,0:T(8,128)(2,1)S(1)} %get-tuple-element.32), channel_id=1, source_target_pairs={{0,8},{4,20},{8,0},{12,28},{16,24},{20,4},{24,16},{28,12},{1,9},{5... | collective-permute-start | bytes 786440 | tf_op jit(solution)/shard_map/ppermute | solution.py:425
  33.1 0.7 collective-permute-start.20
  33.9 2.9 %collective-permute-start = (bf16[512,512]{1,0:T(8,128)(2,1)S(1)}, bf16[512,512]{1,0:T(8,128)(2,1)S(1)}, u32[]{:S(2)}, u32[]{:S(2)}) collective-permute-start(bf16[512,512]{1,0:T(8,128)(2,1)S(1)} %get-tuple-element.28), channel_id=1, source_target_pairs={{0,4},{4,8},{8,12},{12,16},{16,20},{20,24},{24,28},{1,5},{5,9},{9,... | collective-permute-start | bytes 1572872 | tf_op jit(solution)/shard_map/ppermute | solution.py:388
  36.8 3.6 %collective-permute-done.2.got_ref = bf16[1,512,256]{2,1,0:T(8,128)(2,1)S(1)} collective-permute-done((bf16[1,512,256]{2,1,0:T(8,128)(2,1)S(1)}, bf16[1,512,256]{2,1,0:T(8,128)(2,1)S(1)}, u32[]{:S(2)}, u32[]{:S(2)}) %collective-permute-start.2) | collective-permute-done | bytes 262176 | tf_op jit(solution)/shard_map/ppermute | solution.py:425
  40.5 2.0 %collective-permute-start.3 = (bf16[1,512,256]{2,1,0:T(8,128)(2,1)S(1)}, bf16[1,512,256]{2,1,0:T(8,128)(2,1)S(1)}, u32[]{:S(2)}, u32[]{:S(2)}) collective-permute-start(bf16[1,512,256]{2,1,0:T(8,128)(2,1)S(1)} %get-tuple-element.34), channel_id=1, source_target_pairs={{0,16},{4,12},{8,24},{12,4},{16,0},{20,28},{24,8},{28,20},{1,17},{... | collective-permute-start | bytes 786440 | tf_op jit(solution)/shard_map/ppermute | solution.py:425
  42.5 9.1 %collective-permute-done.6.got_ref = bf16[2,512,256]{2,1,0:T(8,128)(2,1)S(1)} collective-permute-done((bf16[2,512,256]{2,1,0:T(8,128)(2,1)S(1)}, bf16[2,512,256]{2,1,0:T(8,128)(2,1)S(1)}, u32[]{:S(2)}, u32[]{:S(2)}) %collective-permute-start.6) | collective-permute-done | bytes 524320 | tf_op jit(solution)/shard_map/ppermute | solution.py:425
  52.1 7.4 %collective-permute-done.3.got_ref = bf16[1,512,256]{2,1,0:T(8,128)(2,1)S(1)} collective-permute-done((bf16[1,512,256]{2,1,0:T(8,128)(2,1)S(1)}, bf16[1,512,256]{2,1,0:T(8,128)(2,1)S(1)}, u32[]{:S(2)}, u32[]{:S(2)}) %collective-permute-start.3) | collective-permute-done | bytes 262176 | tf_op jit(solution)/shard_map/ppermute | solution.py:425
  59.5 1.3 %collective-permute-start.8 = (bf16[2,512,256]{2,1,0:T(8,128)(2,1)S(1)}, bf16[2,512,256]{2,1,0:T(8,128)(2,1)S(1)}, u32[]{:S(2)}, u32[]{:S(2)}) collective-permute-start(bf16[2,512,256]{2,1,0:T(8,128)(2,1)S(1)} %renorm.3.up_ref), channel_id=1, source_target_pairs={{0,4},{4,0},{8,12},{12,8},{16,20},{20,16},{24,28},{28,24},{1,5},{5... | collective-permute-start | bytes 1572872 | tf_op jit(solution)/shard_map/ppermute | solution.py:32
  61.7 1.0 collective-permute-done.7.down_c_ref
  62.7 0.7 collective-permute-start.16
  63.4 1.0 collective-permute-start.17
  64.5 5.3 %collective-permute-start.21 = (bf16[256,2048]{1,0:T(8,128)(2,1)S(1)}, bf16[256,2048]{1,0:T(8,128)(2,1)S(1)}, u32[]{:S(2)}, u32[]{:S(2)}) collective-permute-start(bf16[256,2048]{1,0:T(8,128)(2,1)S(1)} %collective-permute-done.20.refs_1_), channel_id=1, source_target_pairs={{0,4},{4,0},{8,12},{12,8},{16,20},{20,16},{24,28},{28,24},{1,5},{5... | collective-permute-start | bytes 3145736 | tf_op jit(solution)/shard_map/ppermute | solution.py:32
  69.7 4.4 %window.1.seen_ref = f32[1024,512]{1,0:T(8,128)S(1)} custom-call(bf16[1024,512]{1,0:T(8,128)(2,1)} %q_ref.7, bf16[1024,512]{1,0:T(8,128)(2,1)} %left_ref.1, bf16[1024,512]{1,0:T(8,128)(2,1)} %v_ref.1, bf16[512,512]{1,0:T(8,128)(2,1)S(1)} %collective-permute-done.tail_ref), custom_call_target="tpu_custom_call" | custom-call | tf_op jit(solution)/shard_map/window/pallas_call | solution.py:240
  74.7 1.1 %collective-permute-start.11 = (bf16[256,512]{1,0:T(8,128)(2,1)S(1)}, bf16[256,512]{1,0:T(8,128)(2,1)S(1)}, u32[]{:S(2)}, u32[]{:S(2)}) collective-permute-start(bf16[256,512]{1,0:T(8,128)(2,1)S(1)} %apply.6), channel_id=1, source_target_pairs={{0,1},{1,0},{2,3},{3,2},{4,5},{5,4},{6,7},{7,6},{8,9},{9,8},{10,11... | collective-permute-start | bytes 786440 | tf_op jit(solution)/shard_map/ppermute | solution.py:32
  77.0 6.0 %collective-permute-done.11.x_ref = bf16[256,512]{1,0:T(8,128)(2,1)S(1)} collective-permute-done((bf16[256,512]{1,0:T(8,128)(2,1)S(1)}, bf16[256,512]{1,0:T(8,128)(2,1)S(1)}, u32[]{:S(2)}, u32[]{:S(2)}) %collective-permute-start.11) | collective-permute-done | bytes 262176 | tf_op jit(solution)/shard_map/ppermute | solution.py:32
  83.0 3.0 %collective-permute-start.10 = (bf16[256,512]{1,0:T(8,128)(2,1)S(1)}, bf16[256,512]{1,0:T(8,128)(2,1)S(1)}, u32[]{:S(2)}, u32[]{:S(2)}) collective-permute-start(bf16[256,512]{1,0:T(8,128)(2,1)S(1)} %apply.5), channel_id=1, source_target_pairs={{0,3},{1,2},{2,1},{3,0},{4,7},{5,6},{6,5},{7,4},{8,11},{9,10},{10,... | collective-permute-start | bytes 786440 | tf_op jit(solution)/shard_map/ppermute | solution.py:32
  87.5 0.7 copy-done.3
  88.2 0.7 own_project.1
  88.9 0.8 project.3
  89.7 4.3 %collective-permute-done.10.x_ref = bf16[256,512]{1,0:T(8,128)(2,1)S(1)} collective-permute-done((bf16[256,512]{1,0:T(8,128)(2,1)S(1)}, bf16[256,512]{1,0:T(8,128)(2,1)S(1)}, u32[]{:S(2)}, u32[]{:S(2)}) %collective-permute-start.10) | collective-permute-done | bytes 262176 | tf_op jit(solution)/shard_map/ppermute | solution.py:32
  94.0 0.8 project.4
  94.8 13.9 %collective-permute-done.9.x_ref = bf16[256,512]{1,0:T(8,128)(2,1)S(1)} collective-permute-done((bf16[256,512]{1,0:T(8,128)(2,1)S(1)}, bf16[256,512]{1,0:T(8,128)(2,1)S(1)}, u32[]{:S(2)}, u32[]{:S(2)}) %collective-permute-start.9) | collective-permute-done | bytes 262176 | tf_op jit(solution)/shard_map/ppermute | solution.py:32
  108.7 1.6 %project.5 = bf16[256,2048]{1,0:T(8,128)(2,1)} custom-call(bf16[256,512]{1,0:T(8,128)(2,1)S(1)} %collective-permute-done.9.x_ref, f32[256,2048]{1,0:T(8,128)S(1)} %get-tuple-element.49.base_ref, f32[256,1]{1,0:T(8,128)S(1)} %get-tuple-element.50.squares_ref, bf16[256,2048]{1,0:T(8,128)(2,1)S(1)} %collective-permute-done.12.refs_0_, ...), custom_call_target="tpu_custom_call" | custom-call | tf_op jit(solution)/shard_map/project/pallas_call | solution.py:369
  (51 shorter events, 6.2 us)
Async XLA Ops:
  0.0 4.7 %copy-start.1 = (bf16[1024,512]{1,0:T(8,128)(2,1)S(1)}, bf16[1024,512]{1,0:T(8,128)(2,1)}, u32[]{:S(2)}) copy-start(bf16[1024,512]{1,0:T(8,128)(2,1)} %left_ref.1) | copy-start | bytes 3145732
  0.0 4.7 %copy-start.2 = (bf16[1024,512]{1,0:T(8,128)(2,1)S(1)}, bf16[1024,512]{1,0:T(8,128)(2,1)}, u32[]{:S(2)}) copy-start(bf16[1024,512]{1,0:T(8,128)(2,1)} %v_ref.1) | copy-start | bytes 3145732
  0.0 4.7 %copy-start.8 = (f32[1024,1]{0,1:T(1,128)S(1)}, f32[1024,1]{0,1:T(1,128)}, u32[]{:S(2)}) copy-start(f32[1024,1]{0,1:T(1,128)} %param.12) | copy-start | bytes 12292
  0.0 4.7 %copy-start.5 = (bf16[1,512,512]{2,1,0:T(8,128)(2,1)S(1)}, bf16[1,512,512]{2,1,0:T(8,128)(2,1)}, u32[]{:S(2)}) copy-start(bf16[1,512,512]{2,1,0:T(8,128)(2,1)} %refs_0_.3) | copy-start | bytes 1572868
  0.0 4.7 %copy-start.4 = (bf16[1,512,512]{2,1,0:T(8,128)(2,1)S(1)}, bf16[1,512,512]{2,1,0:T(8,128)(2,1)}, u32[]{:S(2)}) copy-start(bf16[1,512,512]{2,1,0:T(8,128)(2,1)} %refs_0_.2) | copy-start | bytes 1572868
  0.0 4.8 %copy-start.6 = (bf16[1,512,512]{2,1,0:T(8,128)(2,1)S(1)}, bf16[1,512,512]{2,1,0:T(8,128)(2,1)}, u32[]{:S(2)}) copy-start(bf16[1,512,512]{2,1,0:T(8,128)(2,1)} %refs_1_.1) | copy-start | bytes 1572868
  1.6 26.8 %collective-permute-start.12 = (bf16[256,2048]{1,0:T(8,128)(2,1)S(1)}, bf16[256,2048]{1,0:T(8,128)(2,1)S(1)}, u32[]{:S(2)}, u32[]{:S(2)}) collective-permute-start(bf16[256,2048]{1,0:T(8,128)(2,1)S(1)} %get-tuple-element.44), channel_id=1, source_target_pairs={{0,1},{1,0},{2,3},{3,2},{4,6},{5,7},{6,4},{7,5},{8,9},{9,8},{10,11... | collective-permute-start | bytes 3145736 | tf_op jit(solution)/shard_map/ppermute | solution.py:392
  7.9 2.2 %collective-permute-start.4 = (bf16[2,512,256]{2,1,0:T(8,128)(2,1)S(1)}, bf16[2,512,256]{2,1,0:T(8,128)(2,1)S(1)}, u32[]{:S(2)}, u32[]{:S(2)}) collective-permute-start(bf16[2,512,256]{2,1,0:T(8,128)(2,1)S(1)} %get-tuple-element.37), channel_id=1, source_target_pairs={{0,4},{4,0},{8,12},{12,8},{16,20},{20,16},{24,28},{28,24},{1,5},{5... | collective-permute-start | bytes 1572872 | tf_op jit(solution)/shard_map/ppermute | solution.py:32
  10.2 20.8 %collective-permute-start.5 = (bf16[2,512,256]{2,1,0:T(8,128)(2,1)S(1)}, bf16[2,512,256]{2,1,0:T(8,128)(2,1)S(1)}, u32[]{:S(2)}, u32[]{:S(2)}) collective-permute-start(bf16[2,512,256]{2,1,0:T(8,128)(2,1)S(1)} %get-tuple-element.39), channel_id=1, source_target_pairs={{0,8},{4,20},{8,0},{12,28},{16,24},{20,4},{24,16},{28,12},{1,9},{5... | collective-permute-start | bytes 1572872 | tf_op jit(solution)/shard_map/ppermute | solution.py:425
  12.2 18.6 %collective-permute-start.1 = (bf16[1,512,256]{2,1,0:T(8,128)(2,1)S(1)}, bf16[1,512,256]{2,1,0:T(8,128)(2,1)S(1)}, u32[]{:S(2)}, u32[]{:S(2)}) collective-permute-start(bf16[1,512,256]{2,1,0:T(8,128)(2,1)S(1)} %contract.4), channel_id=1, source_target_pairs={{0,4},{4,0},{8,12},{12,8},{16,20},{20,16},{24,28},{28,24},{1,5},{5... | collective-permute-start | bytes 786440 | tf_op jit(solution)/shard_map/ppermute | solution.py:32
  28.4 32.7 %collective-permute-start.13 = (bf16[256,2048]{1,0:T(8,128)(2,1)S(1)}, bf16[256,2048]{1,0:T(8,128)(2,1)S(1)}, u32[]{:S(2)}, u32[]{:S(2)}) collective-permute-start(bf16[256,2048]{1,0:T(8,128)(2,1)S(1)} %collective-permute-done.12.refs_0_), channel_id=1, source_target_pairs={{0,16},{1,17},{2,18},{3,19},{4,5},{5,4},{6,7},{7,6},{8,24},{9,25},... | collective-permute-start | bytes 3145736 | tf_op jit(solution)/shard_map/ppermute | solution.py:394
  31.1 20.6 %collective-permute-start.6 = (bf16[2,512,256]{2,1,0:T(8,128)(2,1)S(1)}, bf16[2,512,256]{2,1,0:T(8,128)(2,1)S(1)}, u32[]{:S(2)}, u32[]{:S(2)}) collective-permute-start(bf16[2,512,256]{2,1,0:T(8,128)(2,1)S(1)} %get-tuple-element.41), channel_id=1, source_target_pairs={{0,16},{4,12},{8,24},{12,4},{16,0},{20,28},{24,8},{28,20},{1,17},{... | collective-permute-start | bytes 1572872 | tf_op jit(solution)/shard_map/ppermute | solution.py:425
  31.2 9.2 %collective-permute-start.2 = (bf16[1,512,256]{2,1,0:T(8,128)(2,1)S(1)}, bf16[1,512,256]{2,1,0:T(8,128)(2,1)S(1)}, u32[]{:S(2)}, u32[]{:S(2)}) collective-permute-start(bf16[1,512,256]{2,1,0:T(8,128)(2,1)S(1)} %get-tuple-element.32), channel_id=1, source_target_pairs={{0,8},{4,20},{8,0},{12,28},{16,24},{20,4},{24,16},{28,12},{1,9},{5... | collective-permute-start | bytes 786440 | tf_op jit(solution)/shard_map/ppermute | solution.py:425
  33.1 31.3 %collective-permute-start.20 = (bf16[256,2048]{1,0:T(8,128)(2,1)S(1)}, bf16[256,2048]{1,0:T(8,128)(2,1)S(1)}, u32[]{:S(2)}, u32[]{:S(2)}) collective-permute-start(bf16[256,2048]{1,0:T(8,128)(2,1)S(1)} %collective-permute-done.12.refs_0_), channel_id=1, source_target_pairs={{4,12},{12,4},{20,28},{28,20},{5,13},{13,5},{21,29},{29,21},{6,14}... | collective-permute-start | bytes 3145736 | tf_op jit(solution)/shard_map/ppermute | solution.py:395
  33.9 27.2 %collective-permute-start = (bf16[512,512]{1,0:T(8,128)(2,1)S(1)}, bf16[512,512]{1,0:T(8,128)(2,1)S(1)}, u32[]{:S(2)}, u32[]{:S(2)}) collective-permute-start(bf16[512,512]{1,0:T(8,128)(2,1)S(1)} %get-tuple-element.28), channel_id=1, source_target_pairs={{0,4},{4,8},{8,12},{12,16},{16,20},{20,24},{24,28},{1,5},{5,9},{9,... | collective-permute-start | bytes 1572872 | tf_op jit(solution)/shard_map/ppermute | solution.py:388
  40.5 19.0 %collective-permute-start.3 = (bf16[1,512,256]{2,1,0:T(8,128)(2,1)S(1)}, bf16[1,512,256]{2,1,0:T(8,128)(2,1)S(1)}, u32[]{:S(2)}, u32[]{:S(2)}) collective-permute-start(bf16[1,512,256]{2,1,0:T(8,128)(2,1)S(1)} %get-tuple-element.34), channel_id=1, source_target_pairs={{0,16},{4,12},{8,24},{12,4},{16,0},{20,28},{24,8},{28,20},{1,17},{... | collective-permute-start | bytes 786440 | tf_op jit(solution)/shard_map/ppermute | solution.py:425
  51.6 23.1 %collective-permute-start.14 = (bf16[256,2048]{1,0:T(8,128)(2,1)S(1)}, bf16[256,2048]{1,0:T(8,128)(2,1)S(1)}, u32[]{:S(2)}, u32[]{:S(2)}) collective-permute-start(bf16[256,2048]{1,0:T(8,128)(2,1)S(1)} %collective-permute-done.12.refs_0_), channel_id=1, source_target_pairs={{0,4},{4,0},{8,12},{12,8},{16,20},{20,16},{24,28},{28,24},{1,5},{5... | collective-permute-start | bytes 3145736 | tf_op jit(solution)/shard_map/ppermute | solution.py:32
  59.5 3.9 %collective-permute-start.8 = (bf16[2,512,256]{2,1,0:T(8,128)(2,1)S(1)}, bf16[2,512,256]{2,1,0:T(8,128)(2,1)S(1)}, u32[]{:S(2)}, u32[]{:S(2)}) collective-permute-start(bf16[2,512,256]{2,1,0:T(8,128)(2,1)S(1)} %renorm.3.up_ref), channel_id=1, source_target_pairs={{0,4},{4,0},{8,12},{12,8},{16,20},{20,16},{24,28},{28,24},{1,5},{5... | collective-permute-start | bytes 1572872 | tf_op jit(solution)/shard_map/ppermute | solution.py:32
  61.0 1.7 %collective-permute-start.7 = (bf16[1,512,256]{2,1,0:T(8,128)(2,1)S(1)}, bf16[1,512,256]{2,1,0:T(8,128)(2,1)S(1)}, u32[]{:S(2)}, u32[]{:S(2)}) collective-permute-start(bf16[1,512,256]{2,1,0:T(8,128)(2,1)S(1)} %renorm.2.down_ref), channel_id=1, source_target_pairs={{0,4},{4,0},{8,12},{12,8},{16,20},{20,16},{24,28},{28,24},{1,5},{5... | collective-permute-start | bytes 786440 | tf_op jit(solution)/shard_map/ppermute | solution.py:32
  61.1 25.5 %collective-permute-start.15 = (bf16[256,2048]{1,0:T(8,128)(2,1)S(1)}, bf16[256,2048]{1,0:T(8,128)(2,1)S(1)}, u32[]{:S(2)}, u32[]{:S(2)}) collective-permute-start(bf16[256,2048]{1,0:T(8,128)(2,1)S(1)} %collective-permute-done.13.refs_1_.whole_ref.refs_0_), channel_id=1, source_target_pairs={{0,4},{4,0},{8,12},{12,8},{16,20},{20,16},{24,28},{28,24},{1,5},{5... | collective-permute-start | bytes 3145736 | tf_op jit(solution)/shard_map/ppermute | solution.py:32
  62.7 13.1 %collective-permute-start.16 = (bf16[256,1024]{1,0:T(8,128)(2,1)S(1)}, bf16[256,1024]{1,0:T(8,128)(2,1)S(1)}, u32[]{:S(2)}, u32[]{:S(2)}) collective-permute-start(bf16[256,1024]{1,0:T(8,128)(2,1)S(1)} %get-tuple-element.47), channel_id=1, source_target_pairs={{4,12},{12,4},{20,28},{28,20},{5,13},{13,5},{21,29},{29,21},{6,14}... | collective-permute-start | bytes 1572872 | tf_op jit(solution)/shard_map/ppermute | solution.py:399
  63.4 10.7 %copy-start = (bf16[1024,512]{1,0:T(8,128)(2,1)S(1)}, bf16[1024,512]{1,0:T(8,128)(2,1)}, u32[]{:S(2)}) copy-start(bf16[1024,512]{1,0:T(8,128)(2,1)} %q_ref.7) | copy-start | bytes 3145732
  63.4 12.4 %collective-permute-start.17 = (bf16[256,1024]{1,0:T(8,128)(2,1)S(1)}, bf16[256,1024]{1,0:T(8,128)(2,1)S(1)}, u32[]{:S(2)}, u32[]{:S(2)}) collective-permute-start(bf16[256,1024]{1,0:T(8,128)(2,1)S(1)} %get-tuple-element.48), channel_id=1, source_target_pairs={{4,20},{12,28},{20,4},{28,12},{5,21},{13,29},{21,5},{29,13},{6,22}... | collective-permute-start | bytes 1572872 | tf_op jit(solution)/shard_map/ppermute | solution.py:400
  64.5 44.2 %collective-permute-start.21 = (bf16[256,2048]{1,0:T(8,128)(2,1)S(1)}, bf16[256,2048]{1,0:T(8,128)(2,1)S(1)}, u32[]{:S(2)}, u32[]{:S(2)}) collective-permute-start(bf16[256,2048]{1,0:T(8,128)(2,1)S(1)} %collective-permute-done.20.refs_1_), channel_id=1, source_target_pairs={{0,4},{4,0},{8,12},{12,8},{16,20},{20,16},{24,28},{28,24},{1,5},{5... | collective-permute-start | bytes 3145736 | tf_op jit(solution)/shard_map/ppermute | solution.py:32
  74.7 8.3 %collective-permute-start.11 = (bf16[256,512]{1,0:T(8,128)(2,1)S(1)}, bf16[256,512]{1,0:T(8,128)(2,1)S(1)}, u32[]{:S(2)}, u32[]{:S(2)}) collective-permute-start(bf16[256,512]{1,0:T(8,128)(2,1)S(1)} %apply.6), channel_id=1, source_target_pairs={{0,1},{1,0},{2,3},{3,2},{4,5},{5,4},{6,7},{7,6},{8,9},{9,8},{10,11... | collective-permute-start | bytes 786440 | tf_op jit(solution)/shard_map/ppermute | solution.py:32
  75.9 18.2 %collective-permute-start.18 = (bf16[256,1024]{1,0:T(8,128)(2,1)S(1)}, bf16[256,1024]{1,0:T(8,128)(2,1)S(1)}, u32[]{:S(2)}, u32[]{:S(2)}) collective-permute-start(bf16[256,1024]{1,0:T(8,128)(2,1)S(1)} %collective-permute-done.16.refs_1_), channel_id=1, source_target_pairs={{0,4},{4,0},{8,12},{12,8},{16,20},{20,16},{24,28},{28,24},{1,5},{5... | collective-permute-start | bytes 1572872 | tf_op jit(solution)/shard_map/ppermute | solution.py:32
  75.9 18.2 %collective-permute-start.19 = (bf16[256,1024]{1,0:T(8,128)(2,1)S(1)}, bf16[256,1024]{1,0:T(8,128)(2,1)S(1)}, u32[]{:S(2)}, u32[]{:S(2)}) collective-permute-start(bf16[256,1024]{1,0:T(8,128)(2,1)S(1)} %collective-permute-done.17.refs_2_), channel_id=1, source_target_pairs={{0,4},{4,0},{8,12},{12,8},{16,20},{20,16},{24,28},{28,24},{1,5},{5... | collective-permute-start | bytes 1572872 | tf_op jit(solution)/shard_map/ppermute | solution.py:32
  83.0 11.0 %collective-permute-start.10 = (bf16[256,512]{1,0:T(8,128)(2,1)S(1)}, bf16[256,512]{1,0:T(8,128)(2,1)S(1)}, u32[]{:S(2)}, u32[]{:S(2)}) collective-permute-start(bf16[256,512]{1,0:T(8,128)(2,1)S(1)} %apply.5), channel_id=1, source_target_pairs={{0,3},{1,2},{2,1},{3,0},{4,7},{5,6},{6,5},{7,4},{8,11},{9,10},{10,... | collective-permute-start | bytes 786440 | tf_op jit(solution)/shard_map/ppermute | solution.py:32
  86.6 1.6 %copy-start.3 = (bf16[512,2048]{1,0:T(8,128)(2,1)S(1)}, bf16[512,2048]{1,0:T(8,128)(2,1)}, u32[]{:S(2)}) copy-start(bf16[512,2048]{1,0:T(8,128)(2,1)} %w_ref.1) | copy-start | bytes 6291460
  86.6 1.6 %copy-start.7 = (bf16[512]{0:T(512)(128)(2,1)S(1)}, bf16[512]{0:T(512)(128)(2,1)}, u32[]{:S(2)}) copy-start(bf16[512]{0:T(512)(128)(2,1)} %gain_ref.1) | copy-start | bytes 3076
  86.6 22.1 %collective-permute-start.9 = (bf16[256,512]{1,0:T(8,128)(2,1)S(1)}, bf16[256,512]{1,0:T(8,128)(2,1)S(1)}, u32[]{:S(2)}, u32[]{:S(2)}) collective-permute-start(bf16[256,512]{1,0:T(8,128)(2,1)S(1)} %apply.4), channel_id=1, source_target_pairs={{0,2},{1,3},{2,0},{3,1},{4,6},{5,7},{6,4},{7,5},{8,10},{9,11},{10,... | collective-permute-start | bytes 786440 | tf_op jit(solution)/shard_map/ppermute | solution.py:32

commit v4 on v3

--- a/solution.py
+++ b/solution.py
@@ -48,8 +48,8 @@
     return jnp.concatenate([tall] * (width // 128), axis=1)
 
 
-def load_kernel(k_hbm, v_hbm, gain_hbm, w_hbm, tail_ref, piece_ref, w_ref, gain_ref, sem):
-    rows, columns = piece_ref.shape
+def load_kernel(k_hbm, v_hbm, gain_hbm, w_hbm, tail_ref, low_ref, high_ref, w_ref, gain_ref, sem):
+    rows, columns = w_ref.shape
     _, side = place()
     first = pl.multiple_of(side * rows, rows)
     last = pl.ds(k_hbm.shape[0] - WINDOW, WINDOW)
@@ -70,21 +70,23 @@
     for i in range(steps):
         at = slice(i * block, (i + 1) * block)
         copies[1 + i].wait()
+        to_ref, to = (low_ref, at) if i < steps // 2 else (high_ref, slice((i - 2) * block, (i - 1) * block))
         for left in range(0, columns, 128):
             here = slice(left, left + 128)
-            piece_ref[at, here] = (w_ref[at, here].astype(jnp.float32) * gain[at, :]).astype(jnp.bfloat16)
+            to_ref[to, here] = (w_ref[at, here].astype(jnp.float32) * gain[at, :]).astype(jnp.bfloat16)
     for copy in copies[1 + steps :]:
         copy.wait()
 
 
 def load(keys, values, gain, weight):
     piece = pltpu.VMEM((weight.shape[0] // 2, weight.shape[1]), jnp.bfloat16)
+    chunk = pltpu.VMEM((weight.shape[0] // 4, weight.shape[1]), jnp.bfloat16)
     return pl.pallas_call(
         load_kernel,
-        out_shape=[pltpu.VMEM((2 * WINDOW, keys.shape[1]), jnp.bfloat16), piece],
+        out_shape=[pltpu.VMEM((2 * WINDOW, keys.shape[1]), jnp.bfloat16), chunk, chunk],
         compiler_params=grant(8),
         in_specs=[HBM] * 4,
-        out_specs=[VMEM] * 2,
+        out_specs=[VMEM] * 3,
         scratch_shapes=[piece, pltpu.VMEM(gain.shape, gain.dtype), pltpu.SemaphoreType.DMA((7,))],
         name="load",
     )(*far_core(keys, values, gain, weight))
@@ -299,51 +301,24 @@
     )(*near_core(x, gain, weight))
 
 
-def split_kernel(whole_ref, left_ref, right_ref, sem):
-    columns = left_ref.shape[1]
-    copies = [
-        pltpu.make_async_copy(whole_ref.at[:, pl.ds(j * columns, columns)], out, sem.at[j])
-        for j, out in enumerate((left_ref, right_ref))
-    ]
-    for copy in copies:
-        copy.start()
-    for copy in copies:
-        copy.wait()
-
-
-def split(whole):
-    half = pltpu.VMEM((whole.shape[0], whole.shape[1] // 2), whole.dtype)
-    return pl.pallas_call(
-        split_kernel,
-        out_shape=(half, half),
-        compiler_params=grant(4),
-        in_specs=[VMEM],
-        out_specs=(VMEM, VMEM),
-        scratch_shapes=[pltpu.SemaphoreType.DMA((2,))],
-        name="split",
-    )(*near_core(whole))
-
-
 def project_kernel(holder, scale_by, x_ref, base_ref, squares_ref, *refs):
     count = (len(refs) - (3 if scale_by else 2)) // 2
     brought, copied = refs[:count], refs[count : 2 * count]
     out_ref, *rest = refs[2 * count :]
-    rows, columns = brought[0].shape
     core, half = place()
     wide = x_ref[...].astype(jnp.float32)
     squares = squares_ref[...] + jnp.sum(wide * wide, axis=1, keepdims=True)
+    rows = wide.shape[1] // 2
     mine = pl.ds(pl.multiple_of(half * rows, rows), rows)
     theirs = pl.ds(pl.multiple_of((1 - half) * rows, rows), rows)
     x = jnp.concatenate([x_ref[:, mine], x_ref[:, theirs]], axis=1)
     scale = lax.rsqrt(squares * scale_by + EPSILON) if scale_by else None
-    block = columns // 4
+    block = brought[0].shape[1] // 4
     stores = []
     for j in range(4):
         at = slice(j * block, (j + 1) * block)
-        far, here = (1, at) if count == 2 else (1 + j // 2, slice(j % 2 * block, (j % 2 + 1) * block))
-        w_near = jnp.where(core == holder, brought[0][:, at], copied[0][:, at])
-        w_far = jnp.where(core == holder, brought[far][:, here], copied[far][:, here])
-        total = base_ref[:, at] + dot(x, jnp.concatenate([w_near, w_far], axis=0))
+        w = [jnp.where(core == holder, a[:, at], b[:, at]) for a, b in zip(brought, copied)]
+        total = base_ref[:, at] + dot(x, jnp.concatenate(w, axis=0))
         if scale_by:
             ready_ref, sem = rest
             ready_ref[j] = (total * scale).astype(jnp.bfloat16)
@@ -384,27 +359,31 @@
     bits = ctx_count.bit_length() - 1
     assert ctx_count == 1 << bits and bits >= 3 and heads == 4
 
-    tail, piece = load(keys, values, norm_gain, out_weight)
+    tail, *chunks = load(keys, values, norm_gain, out_weight)
     tail = lax.ppermute(tail, "ctx", [(i, i + 1) for i in range(ctx_count - 1)])
 
-    every = range(ctx_count * heads)
-    over = [(i, i ^ (2 if i // heads & 1 else 1)) for i in every]
-    early = lax.ppermute(piece, ("ctx", "head"), over)
-    over = [(i, i ^ (1 if i // heads & 1 else 4 * heads)) for i in every]
-    relay = lax.ppermute(early, ("ctx", "head"), over)
-    early_far = lax.ppermute(early, "ctx", [(i, i ^ 2) for i in range(1, ctx_count, 2)])
-    early_c = swap(early, "ctx", 1)
-    relay_c = swap(relay, "ctx", 1)
-    left, right = split(relay)
-    late_x = lax.ppermute(left, "ctx", [(i, i ^ 2) for i in range(1, ctx_count, 2)])
-    late_y = lax.ppermute(right, "ctx", [(i, i ^ 4) for i in range(1, ctx_count, 2)])
-    early_far_c = swap(early_far, "ctx", 1)
-    late_x_c = swap(late_x, "ctx", 1)
-    late_y_c = swap(late_y, "ctx", 1)
+    over = [(i, i ^ (2 if i // heads & 1 else 1)) for i in range(ctx_count * heads)]
+    again = [(i, i ^ 1) for i in range(ctx_count * heads) if i // heads & 1]
+    cross = [(i, i ^ (2 if i & 1 else 4)) for i in range(ctx_count)]
+    early, relay, far, late = [], [], [], []
+    for j, chunk in enumerate(chunks):
+        early.append(lax.ppermute(chunk, ("ctx", "head"), over))
+        relay.append(lax.ppermute(early[j], ("ctx", "head"), again))
+        far.append(lax.ppermute(early[j], "ctx", cross))
+        late.append(lax.ppermute(relay[j], "ctx", [(i, i ^ (2 << j)) for i in range(1, ctx_count, 2)]))
+
+    def shared(arrays):
+        copies = []
+        for array in arrays:
+            copies.append(swap(array, "ctx", 1))
+        return copies
+
+    early_c, relay_c = shared(early), shared(relay)
+    far_c, late_c = shared(far), shared(late)
     pieces = {
-        1: (0, (early, relay, early_c, relay_c)),
-        2: (1, (early, early_far, early_c, early_far_c)),
-        3: (1, (relay, late_x, late_y, relay_c, late_x_c, late_y_c)),
+        1: (0, early + far + early_c + far_c),
+        2: (1, early + far + early_c + far_c),
+        3: (1, relay + late + relay_c + late_c),
     }
 
     give_a, act, scaled, g1, g3 = pushes(keys, values, rates, fast_w1, fast_w2, fast_w3)

time: 111 us -> 104 us (0.937)
  waiting for transfers between devices: 62.2 us -> 36.7 us
  starting transfers between devices: 28.9 us -> 42.4 us
  local copies, waits for them, and re-layouts: 0.73 us -> 6.28 us
    ppermute x12 -> x15, starting transfers between devices: 12.9 us -> 25.2 us  [swap(): lax.ppermute(value, axis, [(i, i ^ mask) for i in range(lax.axis_size(axi...]
    ppermute x4, waiting for transfers between devices: 20.2 us -> 8.45 us  [step(): got = lax.ppermute(send, 'ctx', pairs)]
    ppermute x12 -> x15, waiting for transfers between devices: 26 us -> 17.4 us  [swap(): lax.ppermute(value, axis, [(i, i ^ mask) for i in range(lax.axis_size(axi...]
    unnamed x18 -> x20, local copies, waits for them, and re-layouts: 0.73 us -> 6.28 us
    ppermute x5 -> x8, waiting for transfers between devices: 16 us -> 10.9 us  [the longest x2 10.9 us: step(): early.append(lax.ppermute(chunk, ('ctx', 'head'), over))]
    ppermute x5 -> x8, starting transfers between devices: 7.46 us -> 10.8 us  [the longest x2 4.57 us: step(): far.append(lax.ppermute(early[j], 'ctx', cross))]
    ppermute x1, starting transfers between devices: 2.95 us -> 1.31 us  [step(): tail = lax.ppermute(tail, 'ctx', [(i, i + 1) for i in range(ctx_count - 1)])]
  transfers between devices with their start and end apart: 22 -> 28, of which waited for: 9 -> 7; matrix products, arithmetic and copies ran while one was open for 0% -> 0% of each run, Pallas kernels for 14% -> 13%
where the time goes in v4:
time: 104 us
  starting transfers between devices  42.4 us (41%)
  waiting for transfers between devices  36.7 us (35%)
  Pallas kernels  17.8 us (17%)
  local copies, waits for them, and re-layouts  6.28 us (6%)
    ppermute x15, starting transfers between devices, swap(): lax.ppermute(value, axis, [(i, i ^ mask) for i in range(lax.axis_size(axi...  25.2 us
    ppermute x15, waiting for transfers between devices, swap(): lax.ppermute(value, axis, [(i, i ^ mask) for i in range(lax.axis_size(axi...  17.4 us
    ppermute x2, waiting for transfers between devices, step(): early.append(lax.ppermute(chunk, ('ctx', 'head'), over))  10.9 us
    ppermute x4, waiting for transfers between devices, step(): got = lax.ppermute(send, 'ctx', pairs)  8.45 us
    unnamed x20, local copies, waits for them, and re-layouts  6.28 us
    ppermute x4, starting transfers between devices, step(): got = lax.ppermute(send, 'ctx', pairs)  5.14 us
    ppermute x2, starting transfers between devices, step(): far.append(lax.ppermute(early[j], 'ctx', cross))  4.57 us
    pallas_call x1, Pallas kernels, window(): pl.pallas_call(window_kernel, out_shape=pltpu.VMEM(queries.shape, jnp.flo...  4.37 us
  transfers between devices with their start and end apart: 28, of which 7 were waited for; matrix products, arithmetic and copies ran while one was open for 0% of the time, Pallas kernels for 13%

profile of v4, /device:TPU:0, one launch (start us, length us, event | category | flops | bytes accessed | tf_op | source)
XLA Modules:
  0.0 103.8 jit_solution(7409741416901181212)
XLA Ops:
  0.0 1.2 %copy-done.1 = bf16[1024,512]{1,0:T(8,128)(2,1)S(1)} copy-done((bf16[1024,512]{1,0:T(8,128)(2,1)S(1)}, bf16[1024,512]{1,0:T(8,128)(2,1)}, u32[]{:S(2)}) %copy-start.1) | copy-done | bytes 1048600
  1.2 1.2 %copy-done.3 = bf16[1024,512]{1,0:T(8,128)(2,1)S(1)} copy-done((bf16[1024,512]{1,0:T(8,128)(2,1)S(1)}, bf16[1024,512]{1,0:T(8,128)(2,1)}, u32[]{:S(2)}) %copy-start.3) | copy-done | bytes 1048600
  2.5 1.0 %copy-done.5 = bf16[1,512,512]{2,1,0:T(8,128)(2,1)S(1)} copy-done((bf16[1,512,512]{2,1,0:T(8,128)(2,1)S(1)}, bf16[1,512,512]{2,1,0:T(8,128)(2,1)}, u32[]{:S(2)}) %copy-start.5) | copy-done | bytes 524312
  3.5 1.0 %copy-done.6 = bf16[1,512,512]{2,1,0:T(8,128)(2,1)S(1)} copy-done((bf16[1,512,512]{2,1,0:T(8,128)(2,1)S(1)}, bf16[1,512,512]{2,1,0:T(8,128)(2,1)}, u32[]{:S(2)}) %copy-start.6) | copy-done | bytes 524312
  4.5 1.0 %copy-done.7 = bf16[1,512,512]{2,1,0:T(8,128)(2,1)S(1)} copy-done((bf16[1,512,512]{2,1,0:T(8,128)(2,1)S(1)}, bf16[1,512,512]{2,1,0:T(8,128)(2,1)}, u32[]{:S(2)}) %copy-start.7) | copy-done | bytes 524312
  6.3 3.1 %pushes.1 = (bf16[2,512,256]{2,1,0:T(8,128)(2,1)S(1)}, bf16[1024,512]{1,0:T(8,128)(2,1)S(1)}, bf16[1024,512]{1,0:T(8,128)(2,1)S(1)}, bf16[1024,512]{1,0:T(8,128)(2,1)S(1)}, bf16[1024,512]{1,0:T(8,128)(2,1)S(1)}) custom-call(bf16[1024,512]{1,0:T(8,128)(2,1)S(1)} %copy-done.1, bf16[1024,512]{1,0:T(8,128)(2,1)S(1)} %copy-done.3, f32[1,1024]{1,0:T(1,128)S(1)} %bitcast.1, ...), custom_call_target="tpu_custom_call" | custom-call | tf_op jit(solution)/shard_map/pushes/pallas_call | solution.py:129
  10.5 1.4 %load.1 = (bf16[512,512]{1,0:T(8,128)(2,1)S(1)}, bf16[128,2048]{1,0:T(8,128)(2,1)S(1)}, bf16[128,2048]{1,0:T(8,128)(2,1)S(1)}) custom-call(bf16[1024,512]{1,0:T(8,128)(2,1)} %left_ref.1, bf16[1024,512]{1,0:T(8,128)(2,1)} %v_ref.1, bf16[512]{0:T(512)(128)(2,1)} %gain_ref.1, bf16[512,2048]{1,0:T(8,128)(2,1)} %w_ref.1), custom_call_target="tpu_custom_call" | custom-call | tf_op jit(solution)/shard_map/load/pallas_call | solution.py:84
  11.9 3.1 %collective-permute-start.12 = (bf16[128,2048]{1,0:T(8,128)(2,1)S(1)}, bf16[128,2048]{1,0:T(8,128)(2,1)S(1)}, u32[]{:S(2)}, u32[]{:S(2)}) collective-permute-start(bf16[128,2048]{1,0:T(8,128)(2,1)S(1)} %get-tuple-element.43), channel_id=1, source_target_pairs={{0,1},{1,0},{2,3},{3,2},{4,6},{5,7},{6,4},{7,5},{8,9},{9,8},{10,11... | collective-permute-start | bytes 1572872 | tf_op jit(solution)/shard_map/ppermute | solution.py:370
  15.7 1.9 %collective-permute-start.2 = (bf16[1,512,256]{2,1,0:T(8,128)(2,1)S(1)}, bf16[1,512,256]{2,1,0:T(8,128)(2,1)S(1)}, u32[]{:S(2)}, u32[]{:S(2)}) collective-permute-start(bf16[1,512,256]{2,1,0:T(8,128)(2,1)S(1)} %get-tuple-element.31), channel_id=1, source_target_pairs={{0,8},{4,20},{8,0},{12,28},{16,24},{20,4},{24,16},{28,12},{1,9},{5... | collective-permute-start | bytes 786440 | tf_op jit(solution)/shard_map/ppermute | solution.py:404
  18.8 3.4 %collective-permute-done.2.got_ref = bf16[1,512,256]{2,1,0:T(8,128)(2,1)S(1)} collective-permute-done((bf16[1,512,256]{2,1,0:T(8,128)(2,1)S(1)}, bf16[1,512,256]{2,1,0:T(8,128)(2,1)S(1)}, u32[]{:S(2)}, u32[]{:S(2)}) %collective-permute-start.2) | collective-permute-done | bytes 262176 | tf_op jit(solution)/shard_map/ppermute | solution.py:404
  22.2 2.0 %collective-permute-start.3 = (bf16[1,512,256]{2,1,0:T(8,128)(2,1)S(1)}, bf16[1,512,256]{2,1,0:T(8,128)(2,1)S(1)}, u32[]{:S(2)}, u32[]{:S(2)}) collective-permute-start(bf16[1,512,256]{2,1,0:T(8,128)(2,1)S(1)} %get-tuple-element.33), channel_id=1, source_target_pairs={{0,16},{4,12},{8,24},{12,4},{16,0},{20,28},{24,8},{28,20},{1,17},{... | collective-permute-start | bytes 786440 | tf_op jit(solution)/shard_map/ppermute | solution.py:404
  24.2 1.3 %collective-permute-start = (bf16[512,512]{1,0:T(8,128)(2,1)S(1)}, bf16[512,512]{1,0:T(8,128)(2,1)S(1)}, u32[]{:S(2)}, u32[]{:S(2)}) collective-permute-start(bf16[512,512]{1,0:T(8,128)(2,1)S(1)} %get-tuple-element.27), channel_id=1, source_target_pairs={{0,4},{4,8},{8,12},{12,16},{16,20},{20,24},{24,28},{1,5},{5,9},{9,... | collective-permute-start | bytes 1572872 | tf_op jit(solution)/shard_map/ppermute | solution.py:363
  25.5 2.0 %collective-permute-done.12.refs_0_ = bf16[128,2048]{1,0:T(8,128)(2,1)S(1)} collective-permute-done((bf16[128,2048]{1,0:T(8,128)(2,1)S(1)}, bf16[128,2048]{1,0:T(8,128)(2,1)S(1)}, u32[]{:S(2)}, u32[]{:S(2)}) %collective-permute-start.12) | collective-permute-done | bytes 524320 | tf_op jit(solution)/shard_map/ppermute | solution.py:370
  27.4 2.3 %collective-permute-start.14 = (bf16[128,2048]{1,0:T(8,128)(2,1)S(1)}, bf16[128,2048]{1,0:T(8,128)(2,1)S(1)}, u32[]{:S(2)}, u32[]{:S(2)}) collective-permute-start(bf16[128,2048]{1,0:T(8,128)(2,1)S(1)} %collective-permute-done.12.refs_0_), channel_id=1, source_target_pairs={{0,16},{4,12},{8,24},{12,4},{16,0},{20,28},{24,8},{28,20},{1,17},{... | collective-permute-start | bytes 1572872 | tf_op jit(solution)/shard_map/ppermute | solution.py:372
  29.8 8.9 %collective-permute-done.13.refs_1_ = bf16[128,2048]{1,0:T(8,128)(2,1)S(1)} collective-permute-done((bf16[128,2048]{1,0:T(8,128)(2,1)S(1)}, bf16[128,2048]{1,0:T(8,128)(2,1)S(1)}, u32[]{:S(2)}, u32[]{:S(2)}) %collective-permute-start.13) | collective-permute-done | bytes 524320 | tf_op jit(solution)/shard_map/ppermute | solution.py:370
  38.7 2.3 %collective-permute-start.15 = (bf16[128,2048]{1,0:T(8,128)(2,1)S(1)}, bf16[128,2048]{1,0:T(8,128)(2,1)S(1)}, u32[]{:S(2)}, u32[]{:S(2)}) collective-permute-start(bf16[128,2048]{1,0:T(8,128)(2,1)S(1)} %collective-permute-done.13.refs_1_), channel_id=1, source_target_pairs={{0,16},{4,12},{8,24},{12,4},{16,0},{20,28},{24,8},{28,20},{1,17},{... | collective-permute-start | bytes 1572872 | tf_op jit(solution)/shard_map/ppermute | solution.py:372
  41.4 1.0 collective-permute-start.6
  43.9 4.7 %collective-permute-start.16 = (bf16[128,2048]{1,0:T(8,128)(2,1)S(1)}, bf16[128,2048]{1,0:T(8,128)(2,1)S(1)}, u32[]{:S(2)}, u32[]{:S(2)}) collective-permute-start(bf16[128,2048]{1,0:T(8,128)(2,1)S(1)} %collective-permute-done.12.refs_0_), channel_id=1, source_target_pairs={{0,4},{4,0},{8,12},{12,8},{16,20},{20,16},{24,28},{28,24},{1,5},{5... | collective-permute-start | bytes 1572872 | tf_op jit(solution)/shard_map/ppermute | solution.py:32
  48.6 5.1 %collective-permute-done.6.got_ref = bf16[2,512,256]{2,1,0:T(8,128)(2,1)S(1)} collective-permute-done((bf16[2,512,256]{2,1,0:T(8,128)(2,1)S(1)}, bf16[2,512,256]{2,1,0:T(8,128)(2,1)S(1)}, u32[]{:S(2)}, u32[]{:S(2)}) %collective-permute-start.6) | collective-permute-done | bytes 524320 | tf_op jit(solution)/shard_map/ppermute | solution.py:404
  54.2 0.8 collective-permute-start.22
  55.0 0.9 collective-permute-start.23
  55.9 6.0 %collective-permute-start.8 = (bf16[2,512,256]{2,1,0:T(8,128)(2,1)S(1)}, bf16[2,512,256]{2,1,0:T(8,128)(2,1)S(1)}, u32[]{:S(2)}, u32[]{:S(2)}) collective-permute-start(bf16[2,512,256]{2,1,0:T(8,128)(2,1)S(1)} %renorm.3.up_ref), channel_id=1, source_target_pairs={{0,4},{4,0},{8,12},{12,8},{16,20},{20,16},{24,28},{28,24},{1,5},{5... | collective-permute-start | bytes 1572872 | tf_op jit(solution)/shard_map/ppermute | solution.py:32
  62.4 2.6 %collective-permute-start.25 = (bf16[128,2048]{1,0:T(8,128)(2,1)S(1)}, bf16[128,2048]{1,0:T(8,128)(2,1)S(1)}, u32[]{:S(2)}, u32[]{:S(2)}) collective-permute-start(bf16[128,2048]{1,0:T(8,128)(2,1)S(1)} %collective-permute-done.21.refs_1_), channel_id=1, source_target_pairs={{0,4},{4,0},{8,12},{12,8},{16,20},{20,16},{24,28},{28,24},{1,5},{5... | collective-permute-start | bytes 1572872 | tf_op jit(solution)/shard_map/ppermute | solution.py:32
  65.0 3.6 %collective-permute-start.26 = (bf16[128,2048]{1,0:T(8,128)(2,1)S(1)}, bf16[128,2048]{1,0:T(8,128)(2,1)S(1)}, u32[]{:S(2)}, u32[]{:S(2)}) collective-permute-start(bf16[128,2048]{1,0:T(8,128)(2,1)S(1)} %collective-permute-done.22.refs_2_), channel_id=1, source_target_pairs={{0,4},{4,0},{8,12},{12,8},{16,20},{20,16},{24,28},{28,24},{1,5},{5... | collective-permute-start | bytes 1572872 | tf_op jit(solution)/shard_map/ppermute | solution.py:32
  68.6 4.4 %window.1.seen_ref = f32[1024,512]{1,0:T(8,128)S(1)} custom-call(bf16[1024,512]{1,0:T(8,128)(2,1)} %q_ref.7, bf16[1024,512]{1,0:T(8,128)(2,1)} %left_ref.1, bf16[1024,512]{1,0:T(8,128)(2,1)} %v_ref.1, bf16[512,512]{1,0:T(8,128)(2,1)S(1)} %collective-permute-done.tail_ref), custom_call_target="tpu_custom_call" | custom-call | tf_op jit(solution)/shard_map/window/pallas_call | solution.py:242
  73.6 1.6 %collective-permute-start.11 = (bf16[256,512]{1,0:T(8,128)(2,1)S(1)}, bf16[256,512]{1,0:T(8,128)(2,1)S(1)}, u32[]{:S(2)}, u32[]{:S(2)}) collective-permute-start(bf16[256,512]{1,0:T(8,128)(2,1)S(1)} %apply.6), channel_id=1, source_target_pairs={{0,1},{1,0},{2,3},{3,2},{4,5},{5,4},{6,7},{7,6},{8,9},{9,8},{10,11... | collective-permute-start | bytes 786440 | tf_op jit(solution)/shard_map/ppermute | solution.py:32
  75.8 2.4 %collective-permute-start.10 = (bf16[256,512]{1,0:T(8,128)(2,1)S(1)}, bf16[256,512]{1,0:T(8,128)(2,1)S(1)}, u32[]{:S(2)}, u32[]{:S(2)}) collective-permute-start(bf16[256,512]{1,0:T(8,128)(2,1)S(1)} %apply.5), channel_id=1, source_target_pairs={{0,3},{1,2},{2,1},{3,0},{4,7},{5,6},{6,5},{7,4},{8,11},{9,10},{10,... | collective-permute-start | bytes 786440 | tf_op jit(solution)/shard_map/ppermute | solution.py:32
  78.9 3.5 %collective-permute-done.11.x_ref = bf16[256,512]{1,0:T(8,128)(2,1)S(1)} collective-permute-done((bf16[256,512]{1,0:T(8,128)(2,1)S(1)}, bf16[256,512]{1,0:T(8,128)(2,1)S(1)}, u32[]{:S(2)}, u32[]{:S(2)}) %collective-permute-start.11) | collective-permute-done | bytes 262176 | tf_op jit(solution)/shard_map/ppermute | solution.py:32
  82.4 2.9 %collective-permute-start.9 = (bf16[256,512]{1,0:T(8,128)(2,1)S(1)}, bf16[256,512]{1,0:T(8,128)(2,1)S(1)}, u32[]{:S(2)}, u32[]{:S(2)}) collective-permute-start(bf16[256,512]{1,0:T(8,128)(2,1)S(1)} %apply.4), channel_id=1, source_target_pairs={{0,2},{1,3},{2,0},{3,1},{4,6},{5,7},{6,4},{7,5},{8,10},{9,11},{10,... | collective-permute-start | bytes 786440 | tf_op jit(solution)/shard_map/ppermute | solution.py:32
  87.5 3.0 %collective-permute-done.10.x_ref = bf16[256,512]{1,0:T(8,128)(2,1)S(1)} collective-permute-done((bf16[256,512]{1,0:T(8,128)(2,1)S(1)}, bf16[256,512]{1,0:T(8,128)(2,1)S(1)}, u32[]{:S(2)}, u32[]{:S(2)}) %collective-permute-start.10) | collective-permute-done | bytes 262176 | tf_op jit(solution)/shard_map/ppermute | solution.py:32
  91.2 10.8 %collective-permute-done.9.x_ref = bf16[256,512]{1,0:T(8,128)(2,1)S(1)} collective-permute-done((bf16[256,512]{1,0:T(8,128)(2,1)S(1)}, bf16[256,512]{1,0:T(8,128)(2,1)S(1)}, u32[]{:S(2)}, u32[]{:S(2)}) %collective-permute-start.9) | collective-permute-done | bytes 262176 | tf_op jit(solution)/shard_map/ppermute | solution.py:32
  102.1 1.6 %project.5 = bf16[256,2048]{1,0:T(8,128)(2,1)} custom-call(bf16[256,512]{1,0:T(8,128)(2,1)S(1)} %collective-permute-done.9.x_ref, f32[256,2048]{1,0:T(8,128)S(1)} %get-tuple-element.47.base_ref, f32[256,1]{1,0:T(8,128)S(1)} %get-tuple-element.48.squares_ref, bf16[128,2048]{1,0:T(8,128)(2,1)S(1)} %collective-permute-done.12.refs_0_, ...), custom_call_target="tpu_custom_call" | custom-call | tf_op jit(solution)/shard_map/project/pallas_call | solution.py:344
  (64 shorter events, 11.2 us)
Async XLA Ops:
  9.3 9.0 %collective-permute-start.4 = (bf16[2,512,256]{2,1,0:T(8,128)(2,1)S(1)}, bf16[2,512,256]{2,1,0:T(8,128)(2,1)S(1)}, u32[]{:S(2)}, u32[]{:S(2)}) collective-permute-start(bf16[2,512,256]{2,1,0:T(8,128)(2,1)S(1)} %get-tuple-element.36), channel_id=1, source_target_pairs={{0,4},{4,0},{8,12},{12,8},{16,20},{20,16},{24,28},{28,24},{1,5},{5... | collective-permute-start | bytes 1572872 | tf_op jit(solution)/shard_map/ppermute | solution.py:32
  10.4 5.2 %collective-permute-start.1 = (bf16[1,512,256]{2,1,0:T(8,128)(2,1)S(1)}, bf16[1,512,256]{2,1,0:T(8,128)(2,1)S(1)}, u32[]{:S(2)}, u32[]{:S(2)}) collective-permute-start(bf16[1,512,256]{2,1,0:T(8,128)(2,1)S(1)} %contract.4), channel_id=1, source_target_pairs={{0,4},{4,0},{8,12},{12,8},{16,20},{20,16},{24,28},{28,24},{1,5},{5... | collective-permute-start | bytes 786440 | tf_op jit(solution)/shard_map/ppermute | solution.py:32
  11.9 5.7 %copy-start.2 = (bf16[1024,512]{1,0:T(8,128)(2,1)S(1)}, bf16[1024,512]{1,0:T(8,128)(2,1)}, u32[]{:S(2)}) copy-start(bf16[1024,512]{1,0:T(8,128)(2,1)} %left_ref.1) | copy-start | bytes 3145732
  11.9 15.5 %collective-permute-start.12 = (bf16[128,2048]{1,0:T(8,128)(2,1)S(1)}, bf16[128,2048]{1,0:T(8,128)(2,1)S(1)}, u32[]{:S(2)}, u32[]{:S(2)}) collective-permute-start(bf16[128,2048]{1,0:T(8,128)(2,1)S(1)} %get-tuple-element.43), channel_id=1, source_target_pairs={{0,1},{1,0},{2,3},{3,2},{4,6},{5,7},{6,4},{7,5},{8,9},{9,8},{10,11... | collective-permute-start | bytes 1572872 | tf_op jit(solution)/shard_map/ppermute | solution.py:370
  15.0 23.7 %collective-permute-start.13 = (bf16[128,2048]{1,0:T(8,128)(2,1)S(1)}, bf16[128,2048]{1,0:T(8,128)(2,1)S(1)}, u32[]{:S(2)}, u32[]{:S(2)}) collective-permute-start(bf16[128,2048]{1,0:T(8,128)(2,1)S(1)} %get-tuple-element.44), channel_id=1, source_target_pairs={{0,1},{1,0},{2,3},{3,2},{4,6},{5,7},{6,4},{7,5},{8,9},{9,8},{10,11... | collective-permute-start | bytes 1572872 | tf_op jit(solution)/shard_map/ppermute | solution.py:370
  15.7 6.4 %collective-permute-start.2 = (bf16[1,512,256]{2,1,0:T(8,128)(2,1)S(1)}, bf16[1,512,256]{2,1,0:T(8,128)(2,1)S(1)}, u32[]{:S(2)}, u32[]{:S(2)}) collective-permute-start(bf16[1,512,256]{2,1,0:T(8,128)(2,1)S(1)} %get-tuple-element.31), channel_id=1, source_target_pairs={{0,8},{4,20},{8,0},{12,28},{16,24},{20,4},{24,16},{28,12},{1,9},{5... | collective-permute-start | bytes 786440 | tf_op jit(solution)/shard_map/ppermute | solution.py:404
  18.5 22.7 %collective-permute-start.5 = (bf16[2,512,256]{2,1,0:T(8,128)(2,1)S(1)}, bf16[2,512,256]{2,1,0:T(8,128)(2,1)S(1)}, u32[]{:S(2)}, u32[]{:S(2)}) collective-permute-start(bf16[2,512,256]{2,1,0:T(8,128)(2,1)S(1)} %get-tuple-element.38), channel_id=1, source_target_pairs={{0,8},{4,20},{8,0},{12,28},{16,24},{20,4},{24,16},{28,12},{1,9},{5... | collective-permute-start | bytes 1572872 | tf_op jit(solution)/shard_map/ppermute | solution.py:404
  22.2 18.7 %collective-permute-start.3 = (bf16[1,512,256]{2,1,0:T(8,128)(2,1)S(1)}, bf16[1,512,256]{2,1,0:T(8,128)(2,1)S(1)}, u32[]{:S(2)}, u32[]{:S(2)}) collective-permute-start(bf16[1,512,256]{2,1,0:T(8,128)(2,1)S(1)} %get-tuple-element.33), channel_id=1, source_target_pairs={{0,16},{4,12},{8,24},{12,4},{16,0},{20,28},{24,8},{28,20},{1,17},{... | collective-permute-start | bytes 786440 | tf_op jit(solution)/shard_map/ppermute | solution.py:404
  24.2 18.3 %collective-permute-start = (bf16[512,512]{1,0:T(8,128)(2,1)S(1)}, bf16[512,512]{1,0:T(8,128)(2,1)S(1)}, u32[]{:S(2)}, u32[]{:S(2)}) collective-permute-start(bf16[512,512]{1,0:T(8,128)(2,1)S(1)} %get-tuple-element.27), channel_id=1, source_target_pairs={{0,4},{4,8},{8,12},{12,16},{16,20},{20,24},{24,28},{1,5},{5,9},{9,... | collective-permute-start | bytes 1572872 | tf_op jit(solution)/shard_map/ppermute | solution.py:363
  27.4 16.4 %collective-permute-start.14 = (bf16[128,2048]{1,0:T(8,128)(2,1)S(1)}, bf16[128,2048]{1,0:T(8,128)(2,1)S(1)}, u32[]{:S(2)}, u32[]{:S(2)}) collective-permute-start(bf16[128,2048]{1,0:T(8,128)(2,1)S(1)} %collective-permute-done.12.refs_0_), channel_id=1, source_target_pairs={{0,16},{4,12},{8,24},{12,4},{16,0},{20,28},{24,8},{28,20},{1,17},{... | collective-permute-start | bytes 1572872 | tf_op jit(solution)/shard_map/ppermute | solution.py:372
  38.7 9.9 %collective-permute-start.15 = (bf16[128,2048]{1,0:T(8,128)(2,1)S(1)}, bf16[128,2048]{1,0:T(8,128)(2,1)S(1)}, u32[]{:S(2)}, u32[]{:S(2)}) collective-permute-start(bf16[128,2048]{1,0:T(8,128)(2,1)S(1)} %collective-permute-done.13.refs_1_), channel_id=1, source_target_pairs={{0,16},{4,12},{8,24},{12,4},{16,0},{20,28},{24,8},{28,20},{1,17},{... | collective-permute-start | bytes 1572872 | tf_op jit(solution)/shard_map/ppermute | solution.py:372
  41.2 2.0 %collective-permute-start.7 = (bf16[1,512,256]{2,1,0:T(8,128)(2,1)S(1)}, bf16[1,512,256]{2,1,0:T(8,128)(2,1)S(1)}, u32[]{:S(2)}, u32[]{:S(2)}) collective-permute-start(bf16[1,512,256]{2,1,0:T(8,128)(2,1)S(1)} %renorm.2.down_ref), channel_id=1, source_target_pairs={{0,4},{4,0},{8,12},{12,8},{16,20},{20,16},{24,28},{28,24},{1,5},{5... | collective-permute-start | bytes 786440 | tf_op jit(solution)/shard_map/ppermute | solution.py:32
  41.4 12.3 %collective-permute-start.6 = (bf16[2,512,256]{2,1,0:T(8,128)(2,1)S(1)}, bf16[2,512,256]{2,1,0:T(8,128)(2,1)S(1)}, u32[]{:S(2)}, u32[]{:S(2)}) collective-permute-start(bf16[2,512,256]{2,1,0:T(8,128)(2,1)S(1)} %get-tuple-element.40), channel_id=1, source_target_pairs={{0,16},{4,12},{8,24},{12,4},{16,0},{20,28},{24,8},{28,20},{1,17},{... | collective-permute-start | bytes 1572872 | tf_op jit(solution)/shard_map/ppermute | solution.py:404
  42.4 11.7 %collective-permute-start.20 = (bf16[128,2048]{1,0:T(8,128)(2,1)S(1)}, bf16[128,2048]{1,0:T(8,128)(2,1)S(1)}, u32[]{:S(2)}, u32[]{:S(2)}) collective-permute-start(bf16[128,2048]{1,0:T(8,128)(2,1)S(1)} %collective-permute-done.12.refs_0_), channel_id=1, source_target_pairs={{4,5},{5,4},{6,7},{7,6},{12,13},{13,12},{14,15},{15,14},{20,21},{2... | collective-permute-start | bytes 1572872 | tf_op jit(solution)/shard_map/ppermute | solution.py:371
  43.1 11.9 %collective-permute-start.21 = (bf16[128,2048]{1,0:T(8,128)(2,1)S(1)}, bf16[128,2048]{1,0:T(8,128)(2,1)S(1)}, u32[]{:S(2)}, u32[]{:S(2)}) collective-permute-start(bf16[128,2048]{1,0:T(8,128)(2,1)S(1)} %collective-permute-done.13.refs_1_), channel_id=1, source_target_pairs={{4,5},{5,4},{6,7},{7,6},{12,13},{13,12},{14,15},{15,14},{20,21},{2... | collective-permute-start | bytes 1572872 | tf_op jit(solution)/shard_map/ppermute | solution.py:371
  43.9 12.0 %collective-permute-start.16 = (bf16[128,2048]{1,0:T(8,128)(2,1)S(1)}, bf16[128,2048]{1,0:T(8,128)(2,1)S(1)}, u32[]{:S(2)}, u32[]{:S(2)}) collective-permute-start(bf16[128,2048]{1,0:T(8,128)(2,1)S(1)} %collective-permute-done.12.refs_0_), channel_id=1, source_target_pairs={{0,4},{4,0},{8,12},{12,8},{16,20},{20,16},{24,28},{28,24},{1,5},{5... | collective-permute-start | bytes 1572872 | tf_op jit(solution)/shard_map/ppermute | solution.py:32
  48.6 13.3 %collective-permute-start.17 = (bf16[128,2048]{1,0:T(8,128)(2,1)S(1)}, bf16[128,2048]{1,0:T(8,128)(2,1)S(1)}, u32[]{:S(2)}, u32[]{:S(2)}) collective-permute-start(bf16[128,2048]{1,0:T(8,128)(2,1)S(1)} %collective-permute-done.13.refs_1_), channel_id=1, source_target_pairs={{0,4},{4,0},{8,12},{12,8},{16,20},{20,16},{24,28},{28,24},{1,5},{5... | collective-permute-start | bytes 1572872 | tf_op jit(solution)/shard_map/ppermute | solution.py:32
  53.7 8.2 %collective-permute-start.18 = (bf16[128,2048]{1,0:T(8,128)(2,1)S(1)}, bf16[128,2048]{1,0:T(8,128)(2,1)S(1)}, u32[]{:S(2)}, u32[]{:S(2)}) collective-permute-start(bf16[128,2048]{1,0:T(8,128)(2,1)S(1)} %collective-permute-done.14.refs_2_), channel_id=1, source_target_pairs={{0,4},{4,0},{8,12},{12,8},{16,20},{20,16},{24,28},{28,24},{1,5},{5... | collective-permute-start | bytes 1572872 | tf_op jit(solution)/shard_map/ppermute | solution.py:32
  54.1 18.9 %copy-start = (bf16[1024,512]{1,0:T(8,128)(2,1)S(1)}, bf16[1024,512]{1,0:T(8,128)(2,1)}, u32[]{:S(2)}) copy-start(bf16[1024,512]{1,0:T(8,128)(2,1)} %q_ref.7) | copy-start | bytes 3145732
  54.2 8.2 %collective-permute-start.22 = (bf16[128,2048]{1,0:T(8,128)(2,1)S(1)}, bf16[128,2048]{1,0:T(8,128)(2,1)S(1)}, u32[]{:S(2)}, u32[]{:S(2)}) collective-permute-start(bf16[128,2048]{1,0:T(8,128)(2,1)S(1)} %collective-permute-done.20.refs_0_), channel_id=1, source_target_pairs={{4,12},{12,4},{20,28},{28,20},{5,13},{13,5},{21,29},{29,21},{6,14}... | collective-permute-start | bytes 1572872 | tf_op jit(solution)/shard_map/ppermute | solution.py:373
  55.0 10.0 %collective-permute-start.23 = (bf16[128,2048]{1,0:T(8,128)(2,1)S(1)}, bf16[128,2048]{1,0:T(8,128)(2,1)S(1)}, u32[]{:S(2)}, u32[]{:S(2)}) collective-permute-start(bf16[128,2048]{1,0:T(8,128)(2,1)S(1)} %collective-permute-done.21.refs_1_), channel_id=1, source_target_pairs={{4,20},{12,28},{20,4},{28,12},{5,21},{13,29},{21,5},{29,13},{6,22}... | collective-permute-start | bytes 1572872 | tf_op jit(solution)/shard_map/ppermute | solution.py:373
  55.9 12.7 %collective-permute-start.8 = (bf16[2,512,256]{2,1,0:T(8,128)(2,1)S(1)}, bf16[2,512,256]{2,1,0:T(8,128)(2,1)S(1)}, u32[]{:S(2)}, u32[]{:S(2)}) collective-permute-start(bf16[2,512,256]{2,1,0:T(8,128)(2,1)S(1)} %renorm.3.up_ref), channel_id=1, source_target_pairs={{0,4},{4,0},{8,12},{12,8},{16,20},{20,16},{24,28},{28,24},{1,5},{5... | collective-permute-start | bytes 1572872 | tf_op jit(solution)/shard_map/ppermute | solution.py:32
  61.9 11.7 %collective-permute-start.19 = (bf16[128,2048]{1,0:T(8,128)(2,1)S(1)}, bf16[128,2048]{1,0:T(8,128)(2,1)S(1)}, u32[]{:S(2)}, u32[]{:S(2)}) collective-permute-start(bf16[128,2048]{1,0:T(8,128)(2,1)S(1)} %collective-permute-done.15.refs_3_), channel_id=1, source_target_pairs={{0,4},{4,0},{8,12},{12,8},{16,20},{20,16},{24,28},{28,24},{1,5},{5... | collective-permute-start | bytes 1572872 | tf_op jit(solution)/shard_map/ppermute | solution.py:32
  61.9 13.9 %collective-permute-start.24 = (bf16[128,2048]{1,0:T(8,128)(2,1)S(1)}, bf16[128,2048]{1,0:T(8,128)(2,1)S(1)}, u32[]{:S(2)}, u32[]{:S(2)}) collective-permute-start(bf16[128,2048]{1,0:T(8,128)(2,1)S(1)} %collective-permute-done.20.refs_0_), channel_id=1, source_target_pairs={{0,4},{4,0},{8,12},{12,8},{16,20},{20,16},{24,28},{28,24},{1,5},{5... | collective-permute-start | bytes 1572872 | tf_op jit(solution)/shard_map/ppermute | solution.py:32
  62.4 25.0 %collective-permute-start.25 = (bf16[128,2048]{1,0:T(8,128)(2,1)S(1)}, bf16[128,2048]{1,0:T(8,128)(2,1)S(1)}, u32[]{:S(2)}, u32[]{:S(2)}) collective-permute-start(bf16[128,2048]{1,0:T(8,128)(2,1)S(1)} %collective-permute-done.21.refs_1_), channel_id=1, source_target_pairs={{0,4},{4,0},{8,12},{12,8},{16,20},{20,16},{24,28},{28,24},{1,5},{5... | collective-permute-start | bytes 1572872 | tf_op jit(solution)/shard_map/ppermute | solution.py:32
  65.0 22.4 %collective-permute-start.26 = (bf16[128,2048]{1,0:T(8,128)(2,1)S(1)}, bf16[128,2048]{1,0:T(8,128)(2,1)S(1)}, u32[]{:S(2)}, u32[]{:S(2)}) collective-permute-start(bf16[128,2048]{1,0:T(8,128)(2,1)S(1)} %collective-permute-done.22.refs_2_), channel_id=1, source_target_pairs={{0,4},{4,0},{8,12},{12,8},{16,20},{20,16},{24,28},{28,24},{1,5},{5... | collective-permute-start | bytes 1572872 | tf_op jit(solution)/shard_map/ppermute | solution.py:32
  68.6 18.8 %collective-permute-start.27 = (bf16[128,2048]{1,0:T(8,128)(2,1)S(1)}, bf16[128,2048]{1,0:T(8,128)(2,1)S(1)}, u32[]{:S(2)}, u32[]{:S(2)}) collective-permute-start(bf16[128,2048]{1,0:T(8,128)(2,1)S(1)} %collective-permute-done.23.refs_3_), channel_id=1, source_target_pairs={{0,4},{4,0},{8,12},{12,8},{16,20},{20,16},{24,28},{28,24},{1,5},{5... | collective-permute-start | bytes 1572872 | tf_op jit(solution)/shard_map/ppermute | solution.py:32
  73.6 8.8 %collective-permute-start.11 = (bf16[256,512]{1,0:T(8,128)(2,1)S(1)}, bf16[256,512]{1,0:T(8,128)(2,1)S(1)}, u32[]{:S(2)}, u32[]{:S(2)}) collective-permute-start(bf16[256,512]{1,0:T(8,128)(2,1)S(1)} %apply.6), channel_id=1, source_target_pairs={{0,1},{1,0},{2,3},{3,2},{4,5},{5,4},{6,7},{7,6},{8,9},{9,8},{10,11... | collective-permute-start | bytes 786440 | tf_op jit(solution)/shard_map/ppermute | solution.py:32
  75.8 14.6 %collective-permute-start.10 = (bf16[256,512]{1,0:T(8,128)(2,1)S(1)}, bf16[256,512]{1,0:T(8,128)(2,1)S(1)}, u32[]{:S(2)}, u32[]{:S(2)}) collective-permute-start(bf16[256,512]{1,0:T(8,128)(2,1)S(1)} %apply.5), channel_id=1, source_target_pairs={{0,3},{1,2},{2,1},{3,0},{4,7},{5,6},{6,5},{7,4},{8,11},{9,10},{10,... | collective-permute-start | bytes 786440 | tf_op jit(solution)/shard_map/ppermute | solution.py:32
  78.8 7.1 %copy-start.4 = (bf16[512,2048]{1,0:T(8,128)(2,1)S(1)}, bf16[512,2048]{1,0:T(8,128)(2,1)}, u32[]{:S(2)}) copy-start(bf16[512,2048]{1,0:T(8,128)(2,1)} %w_ref.1) | copy-start | bytes 6291460
  78.8 7.1 %copy-start.8 = (bf16[512]{0:T(512)(128)(2,1)S(1)}, bf16[512]{0:T(512)(128)(2,1)}, u32[]{:S(2)}) copy-start(bf16[512]{0:T(512)(128)(2,1)} %gain_ref.1) | copy-start | bytes 3076
  82.4 19.7 %collective-permute-start.9 = (bf16[256,512]{1,0:T(8,128)(2,1)S(1)}, bf16[256,512]{1,0:T(8,128)(2,1)S(1)}, u32[]{:S(2)}, u32[]{:S(2)}) collective-permute-start(bf16[256,512]{1,0:T(8,128)(2,1)S(1)} %apply.4), channel_id=1, source_target_pairs={{0,2},{1,3},{2,0},{3,1},{4,6},{5,7},{6,4},{7,5},{8,10},{9,11},{10,... | collective-permute-start | bytes 786440 | tf_op jit(solution)/shard_map/ppermute | solution.py:32
  (6 other events, 6.3 us)

commit v5 on v4

--- a/solution.py
+++ b/solution.py
@@ -48,46 +48,43 @@
     return jnp.concatenate([tall] * (width // 128), axis=1)
 
 
-def load_kernel(k_hbm, v_hbm, gain_hbm, w_hbm, tail_ref, low_ref, high_ref, w_ref, gain_ref, sem):
-    rows, columns = w_ref.shape
+def load_kernel(chunk, k_hbm, v_hbm, gain_hbm, w_hbm, *refs):
+    *tail_ref, piece_ref, w_ref, gain_ref, sem = refs
+    rows, columns = piece_ref.shape
     _, side = place()
-    first = pl.multiple_of(side * rows, rows)
-    last = pl.ds(k_hbm.shape[0] - WINDOW, WINDOW)
-    steps = 4
-    block = rows // steps
-    moves = [(gain_hbm, gain_ref)]
-    for i in range(steps):
-        at = pl.ds(i * block, block)
-        moves.append((w_hbm.at[pl.ds(first + i * block, block), :], w_ref.at[at, :]))
-    moves += [(k_hbm.at[last, :], tail_ref.at[pl.ds(0, WINDOW), :])]
-    moves += [(v_hbm.at[last, :], tail_ref.at[pl.ds(WINDOW, WINDOW), :])]
+    first = pl.multiple_of((2 * side + chunk) * rows, rows)
+    moves = [(gain_hbm, gain_ref), (w_hbm.at[pl.ds(first, rows), :], w_ref)]
+    if tail_ref:
+        last = pl.ds(k_hbm.shape[0] - WINDOW, WINDOW)
+        moves += [
+            (src.at[last, :], tail_ref[0].at[pl.ds(j * WINDOW, WINDOW), :])
+            for j, src in enumerate((k_hbm, v_hbm))
+        ]
     copies = [pltpu.make_async_copy(src, dst, sem.at[j]) for j, (src, dst) in enumerate(moves)]
     for copy in copies:
         copy.start()
     copies[0].wait()
-    gain = gain_ref[...].reshape(1, 2 * rows).astype(jnp.float32)
-    gain = jnp.transpose(jnp.broadcast_to(jnp.where(side == 0, gain[:, :rows], gain[:, rows:]), (128, rows)))
-    for i in range(steps):
-        at = slice(i * block, (i + 1) * block)
-        copies[1 + i].wait()
-        to_ref, to = (low_ref, at) if i < steps // 2 else (high_ref, slice((i - 2) * block, (i - 1) * block))
-        for left in range(0, columns, 128):
-            here = slice(left, left + 128)
-            to_ref[to, here] = (w_ref[at, here].astype(jnp.float32) * gain[at, :]).astype(jnp.bfloat16)
-    for copy in copies[1 + steps :]:
+    gain = gain_ref[...].reshape(1, gain_ref.shape[0]).astype(jnp.float32)
+    low, high = (gain[:, (2 * j + chunk) * rows : (2 * j + chunk + 1) * rows] for j in range(2))
+    gain = jnp.transpose(jnp.broadcast_to(jnp.where(side == 0, low, high), (128, rows)))
+    copies[1].wait()
+    for left in range(0, columns, 128):
+        here = slice(left, left + 128)
+        piece_ref[:, here] = (w_ref[:, here].astype(jnp.float32) * gain).astype(jnp.bfloat16)
+    for copy in copies[2:]:
         copy.wait()
 
 
-def load(keys, values, gain, weight):
-    piece = pltpu.VMEM((weight.shape[0] // 2, weight.shape[1]), jnp.bfloat16)
-    chunk = pltpu.VMEM((weight.shape[0] // 4, weight.shape[1]), jnp.bfloat16)
-    return pl.pallas_call(
-        load_kernel,
-        out_shape=[pltpu.VMEM((2 * WINDOW, keys.shape[1]), jnp.bfloat16), chunk, chunk],
+def load(chunk, keys, values, gain, weight):
+    piece = pltpu.VMEM((weight.shape[0] // 4, weight.shape[1]), jnp.bfloat16)
+    shapes = [pltpu.VMEM((2 * WINDOW, keys.shape[1]), jnp.bfloat16)] if chunk == 0 else []
+    return pl.pallas_call(
+        functools.partial(load_kernel, chunk),
+        out_shape=shapes + [piece],
         compiler_params=grant(8),
         in_specs=[HBM] * 4,
-        out_specs=[VMEM] * 3,
-        scratch_shapes=[piece, pltpu.VMEM(gain.shape, gain.dtype), pltpu.SemaphoreType.DMA((7,))],
+        out_specs=[VMEM] * (len(shapes) + 1),
+        scratch_shapes=[piece, pltpu.VMEM(gain.shape, gain.dtype), pltpu.SemaphoreType.DMA((4,))],
         name="load",
     )(*far_core(keys, values, gain, weight))
 
@@ -252,31 +249,46 @@
     )(*far_core(queries, keys, values), *near_core(tail))
 
 
-def apply_kernel(slot, q_ref, seen_ref, down_ref, up_ref, down_c_ref, up_c_ref, out_ref):
+def mix_kernel(slot, q_ref, up_ref, up_c_ref, out_ref):
+    rows, width = out_ref.shape
+    here = pl.ds(pl.multiple_of((lax.axis_index("head").astype(jnp.int32) ^ slot) * rows, rows), rows)
+    q = q_ref[here, :]
+    half = width // 2
+    for j, ref in enumerate((up_ref, up_c_ref)):
+        gate = dot(q, ref[0])
+        up = dot(q, ref[1])
+        out_ref[:, j * half : (j + 1) * half] = (gate * jax.nn.sigmoid(gate) * up).astype(jnp.bfloat16)
+
+
+def mix(slot, queries, up, up_c, rows):
+    return pl.pallas_call(
+        functools.partial(mix_kernel, slot),
+        out_shape=pltpu.VMEM((rows, queries.shape[1]), jnp.bfloat16),
+        compiler_params=grant(8),
+        in_specs=[VMEM] * 3,
+        out_specs=VMEM,
+        name="mix",
+    )(*near_core(queries, up, up_c))
+
+
+def down_kernel(slot, mixed_ref, seen_ref, down_ref, down_c_ref, out_ref):
     rows, width = out_ref.shape
     own, rest = halves(width)
     here = pl.ds(pl.multiple_of((lax.axis_index("head").astype(jnp.int32) ^ slot) * rows, rows), rows)
-    q = q_ref[here, :]
-    mixed = []
-    for ref in (up_ref, up_c_ref):
-        gate = dot(q, ref[0])
-        up = dot(q, ref[1])
-        mixed.append((gate * jax.nn.sigmoid(gate) * up).astype(jnp.bfloat16))
-    mixed = jnp.concatenate(mixed, axis=1)
     for ref, at in ((down_ref, own), (down_c_ref, rest)):
         down = jnp.concatenate([ref[0, own, :], ref[0, rest, :]], axis=0)
-        out_ref[:, at] = (dot(mixed, down) + seen_ref[here, at]).astype(jnp.bfloat16)
-
-
-def apply_fast(slot, queries, seen, weights, rows):
-    return pl.pallas_call(
-        functools.partial(apply_kernel, slot),
-        out_shape=pltpu.VMEM((rows, queries.shape[1]), jnp.bfloat16),
-        compiler_params=grant(16),
-        in_specs=[VMEM] * 6,
+        out_ref[:, at] = (dot(mixed_ref[...], down) + seen_ref[here, at]).astype(jnp.bfloat16)
+
+
+def combine(slot, mixed, seen, down, down_c):
+    return pl.pallas_call(
+        functools.partial(down_kernel, slot),
+        out_shape=pltpu.VMEM(mixed.shape, jnp.bfloat16),
+        compiler_params=grant(8),
+        in_specs=[VMEM] * 4,
         out_specs=VMEM,
-        name="apply",
-    )(*near_core(queries, seen, *weights))
+        name="combine",
+    )(*near_core(mixed, seen, down, down_c))
 
 
 def own_project_kernel(x_ref, gain_ref, w_ref, out_ref, squares_ref):
@@ -359,7 +371,8 @@
     bits = ctx_count.bit_length() - 1
     assert ctx_count == 1 << bits and bits >= 3 and heads == 4
 
-    tail, *chunks = load(keys, values, norm_gain, out_weight)
+    tail, chunk = load(0, keys, values, norm_gain, out_weight)
+    chunks = [chunk, *load(1, keys, values, norm_gain, out_weight)]
     tail = lax.ppermute(tail, "ctx", [(i, i + 1) for i in range(ctx_count - 1)])
 
     over = [(i, i ^ (2 if i // heads & 1 else 1)) for i in range(ctx_count * heads)]
@@ -412,7 +425,8 @@
     rows = tok_rows // heads
     blocks = {}
     for k in send_order(heads) + [0]:
-        combined = apply_fast(k, queries, seen, weights, rows)
+        mixed = mix(k, queries, weights[1], weights[3], rows)
+        combined = combine(k, mixed, seen, weights[0], weights[2])
         blocks[k] = swap(combined, "head", k) if k else combined
     base, squares = own_project(blocks[0], norm_gain, out_weight)
     for k in (1, 3, 2):

time: 104 us -> 100 us (0.962)
  starting transfers between devices: 42.4 us -> 38.4 us
  waiting for transfers between devices: 36.7 us -> 33.5 us
  Pallas kernels: 17.8 us -> 19.6 us
  local copies, waits for them, and re-layouts: 6.28 us -> 7.53 us
    ppermute x15, starting transfers between devices: 25.2 us -> 21.1 us  [swap(): lax.ppermute(value, axis, [(i, i ^ mask) for i in range(lax.axis_size(axi...]
    pallas_call x5 -> x10, Pallas kernels: 3.72 us -> 5.53 us  [the longest x2 2.49 us: load(): pl.pallas_call(functools.partial(load_kernel, chunk), out_shape=shapes +...]
    ppermute x15, waiting for transfers between devices: 17.4 us -> 15.8 us  [swap(): lax.ppermute(value, axis, [(i, i ^ mask) for i in range(lax.axis_size(axi...]
    ppermute x2, waiting for transfers between devices: 10.9 us -> 9.58 us  [step(): early.append(lax.ppermute(chunk, ('ctx', 'head'), over))]
    unnamed x20, local copies, waits for them, and re-layouts: 6.28 us -> 7.53 us
  transfers between devices with their start and end apart: 28 -> 28, of which waited for: 7 -> 7; matrix products, arithmetic and copies ran while one was open for 0% -> 0% of each run, Pallas kernels for 13% -> 15%
where the time goes in v5:
time: 100 us; the launch traced here: 99.6 us
  starting transfers between devices  38.4 us (38%)
  waiting for transfers between devices  33.5 us (34%)
  Pallas kernels  19.6 us (20%)
  local copies, waits for them, and re-layouts  7.53 us (8%)
    ppermute x15, starting transfers between devices, swap(): lax.ppermute(value, axis, [(i, i ^ mask) for i in range(lax.axis_size(axi...  21.1 us
    ppermute x15, waiting for transfers between devices, swap(): lax.ppermute(value, axis, [(i, i ^ mask) for i in range(lax.axis_size(axi...  15.8 us
    ppermute x2, waiting for transfers between devices, step(): early.append(lax.ppermute(chunk, ('ctx', 'head'), over))  9.58 us
    ppermute x4, waiting for transfers between devices, step(): got = lax.ppermute(send, 'ctx', pairs)  8.17 us
    unnamed x20, local copies, waits for them, and re-layouts  7.53 us
    ppermute x4, starting transfers between devices, step(): got = lax.ppermute(send, 'ctx', pairs)  5.19 us
    ppermute x2, starting transfers between devices, step(): far.append(lax.ppermute(early[j], 'ctx', cross))  4.57 us
    pallas_call x1, Pallas kernels, window(): pl.pallas_call(window_kernel, out_shape=pltpu.VMEM(queries.shape, jnp.flo...  4.37 us
  transfers between devices with their start and end apart: 28, of which 7 were waited for; matrix products, arithmetic and copies ran while one was open for 0% of the time, Pallas kernels for 15%

profile of v5, /device:TPU:0, one launch (start us, length us, event | category | flops | bytes accessed | tf_op | source)
XLA Modules:
  0.0 99.6 jit_solution(9594083608633739910)
XLA Ops:
  0.0 1.2 %copy-done = bf16[1024,512]{1,0:T(8,128)(2,1)S(1)} copy-done((bf16[1024,512]{1,0:T(8,128)(2,1)S(1)}, bf16[1024,512]{1,0:T(8,128)(2,1)}, u32[]{:S(2)}) %copy-start) | copy-done | bytes 1048600
  1.2 1.2 %copy-done.4 = bf16[1024,512]{1,0:T(8,128)(2,1)S(1)} copy-done((bf16[1024,512]{1,0:T(8,128)(2,1)S(1)}, bf16[1024,512]{1,0:T(8,128)(2,1)}, u32[]{:S(2)}) %copy-start.4) | copy-done | bytes 1048600
  2.5 1.0 %copy-done.5 = bf16[1,512,512]{2,1,0:T(8,128)(2,1)S(1)} copy-done((bf16[1,512,512]{2,1,0:T(8,128)(2,1)S(1)}, bf16[1,512,512]{2,1,0:T(8,128)(2,1)}, u32[]{:S(2)}) %copy-start.5) | copy-done | bytes 524312
  3.5 1.0 %copy-done.6 = bf16[1,512,512]{2,1,0:T(8,128)(2,1)S(1)} copy-done((bf16[1,512,512]{2,1,0:T(8,128)(2,1)S(1)}, bf16[1,512,512]{2,1,0:T(8,128)(2,1)}, u32[]{:S(2)}) %copy-start.6) | copy-done | bytes 524312
  4.5 1.0 %copy-done.7 = bf16[1,512,512]{2,1,0:T(8,128)(2,1)S(1)} copy-done((bf16[1,512,512]{2,1,0:T(8,128)(2,1)S(1)}, bf16[1,512,512]{2,1,0:T(8,128)(2,1)}, u32[]{:S(2)}) %copy-start.7) | copy-done | bytes 524312
  6.3 3.1 %pushes.1 = (bf16[2,512,256]{2,1,0:T(8,128)(2,1)S(1)}, bf16[1024,512]{1,0:T(8,128)(2,1)S(1)}, bf16[1024,512]{1,0:T(8,128)(2,1)S(1)}, bf16[1024,512]{1,0:T(8,128)(2,1)S(1)}, bf16[1024,512]{1,0:T(8,128)(2,1)S(1)}) custom-call(bf16[1024,512]{1,0:T(8,128)(2,1)S(1)} %copy-done, bf16[1024,512]{1,0:T(8,128)(2,1)S(1)} %copy-done.4, f32[1,1024]{1,0:T(1,128)S(1)} %bitcast.1, ...), custom_call_target="tpu_custom_call" | custom-call | tf_op jit(solution)/shard_map/pushes/pallas_call | solution.py:126
  10.5 1.3 %load.2 = (bf16[512,512]{1,0:T(8,128)(2,1)S(1)}, bf16[128,2048]{1,0:T(8,128)(2,1)S(1)}) custom-call(bf16[1024,512]{1,0:T(8,128)(2,1)} %k_hbm.5, bf16[1024,512]{1,0:T(8,128)(2,1)} %v_hbm.5, bf16[512]{0:T(512)(128)(2,1)} %gain_hbm.3, bf16[512,2048]{1,0:T(8,128)(2,1)} %w_hbm.3), custom_call_target="tpu_custom_call" | custom-call | tf_op jit(solution)/shard_map/load/pallas_call | solution.py:81
  11.7 3.1 %collective-permute-start.12 = (bf16[128,2048]{1,0:T(8,128)(2,1)S(1)}, bf16[128,2048]{1,0:T(8,128)(2,1)S(1)}, u32[]{:S(2)}, u32[]{:S(2)}) collective-permute-start(bf16[128,2048]{1,0:T(8,128)(2,1)S(1)} %get-tuple-element.42), channel_id=1, source_target_pairs={{0,1},{1,0},{2,3},{3,2},{4,6},{5,7},{6,4},{7,5},{8,9},{9,8},{10,11... | collective-permute-start | bytes 1572872 | tf_op jit(solution)/shard_map/ppermute | solution.py:383
  14.8 1.2 %load.3 = bf16[128,2048]{1,0:T(8,128)(2,1)S(1)} custom-call(bf16[1024,512]{1,0:T(8,128)(2,1)} %k_hbm.5, bf16[1024,512]{1,0:T(8,128)(2,1)} %v_hbm.5, bf16[512]{0:T(512)(128)(2,1)} %gain_hbm.3, bf16[512,2048]{1,0:T(8,128)(2,1)} %w_hbm.3), custom_call_target="tpu_custom_call" | custom-call | tf_op jit(solution)/shard_map/load/pallas_call | solution.py:81
  16.8 2.0 %collective-permute-start.6 = (bf16[1,512,256]{2,1,0:T(8,128)(2,1)S(1)}, bf16[1,512,256]{2,1,0:T(8,128)(2,1)S(1)}, u32[]{:S(2)}, u32[]{:S(2)}) collective-permute-start(bf16[1,512,256]{2,1,0:T(8,128)(2,1)S(1)} %get-tuple-element.37), channel_id=1, source_target_pairs={{0,8},{4,20},{8,0},{12,28},{16,24},{20,4},{24,16},{28,12},{1,9},{5... | collective-permute-start | bytes 786440 | tf_op jit(solution)/shard_map/ppermute | solution.py:417
  19.8 3.4 %collective-permute-done.6.got_ref = bf16[1,512,256]{2,1,0:T(8,128)(2,1)S(1)} collective-permute-done((bf16[1,512,256]{2,1,0:T(8,128)(2,1)S(1)}, bf16[1,512,256]{2,1,0:T(8,128)(2,1)S(1)}, u32[]{:S(2)}, u32[]{:S(2)}) %collective-permute-start.6) | collective-permute-done | bytes 262176 | tf_op jit(solution)/shard_map/ppermute | solution.py:417
  23.3 2.0 %collective-permute-start.7 = (bf16[1,512,256]{2,1,0:T(8,128)(2,1)S(1)}, bf16[1,512,256]{2,1,0:T(8,128)(2,1)S(1)}, u32[]{:S(2)}, u32[]{:S(2)}) collective-permute-start(bf16[1,512,256]{2,1,0:T(8,128)(2,1)S(1)} %get-tuple-element.39), channel_id=1, source_target_pairs={{0,16},{4,12},{8,24},{12,4},{16,0},{20,28},{24,8},{28,20},{1,17},{... | collective-permute-start | bytes 786440 | tf_op jit(solution)/shard_map/ppermute | solution.py:417
  25.3 1.3 %collective-permute-start.4 = (bf16[512,512]{1,0:T(8,128)(2,1)S(1)}, bf16[512,512]{1,0:T(8,128)(2,1)S(1)}, u32[]{:S(2)}, u32[]{:S(2)}) collective-permute-start(bf16[512,512]{1,0:T(8,128)(2,1)S(1)} %get-tuple-element.33), channel_id=1, source_target_pairs={{0,4},{4,8},{8,12},{12,16},{16,20},{20,24},{24,28},{1,5},{5,9},{9,... | collective-permute-start | bytes 1572872 | tf_op jit(solution)/shard_map/ppermute | solution.py:376
  27.3 2.3 %collective-permute-start.14 = (bf16[128,2048]{1,0:T(8,128)(2,1)S(1)}, bf16[128,2048]{1,0:T(8,128)(2,1)S(1)}, u32[]{:S(2)}, u32[]{:S(2)}) collective-permute-start(bf16[128,2048]{1,0:T(8,128)(2,1)S(1)} %collective-permute-done.12.refs_0_), channel_id=1, source_target_pairs={{0,16},{4,12},{8,24},{12,4},{16,0},{20,28},{24,8},{28,20},{1,17},{... | collective-permute-start | bytes 1572872 | tf_op jit(solution)/shard_map/ppermute | solution.py:385
  29.6 8.9 %collective-permute-done.13.refs_1_ = bf16[128,2048]{1,0:T(8,128)(2,1)S(1)} collective-permute-done((bf16[128,2048]{1,0:T(8,128)(2,1)S(1)}, bf16[128,2048]{1,0:T(8,128)(2,1)S(1)}, u32[]{:S(2)}, u32[]{:S(2)}) %collective-permute-start.13) | collective-permute-done | bytes 524320 | tf_op jit(solution)/shard_map/ppermute | solution.py:383
  38.5 2.3 %collective-permute-start.15 = (bf16[128,2048]{1,0:T(8,128)(2,1)S(1)}, bf16[128,2048]{1,0:T(8,128)(2,1)S(1)}, u32[]{:S(2)}, u32[]{:S(2)}) collective-permute-start(bf16[128,2048]{1,0:T(8,128)(2,1)S(1)} %collective-permute-done.13.refs_1_), channel_id=1, source_target_pairs={{0,16},{4,12},{8,24},{12,4},{16,0},{20,28},{24,8},{28,20},{1,17},{... | collective-permute-start | bytes 1572872 | tf_op jit(solution)/shard_map/ppermute | solution.py:385
  41.2 1.0 %collective-permute-start.2 = (bf16[2,512,256]{2,1,0:T(8,128)(2,1)S(1)}, bf16[2,512,256]{2,1,0:T(8,128)(2,1)S(1)}, u32[]{:S(2)}, u32[]{:S(2)}) collective-permute-start(bf16[2,512,256]{2,1,0:T(8,128)(2,1)S(1)} %get-tuple-element.32), channel_id=1, source_target_pairs={{0,16},{4,12},{8,24},{12,4},{16,0},{20,28},{24,8},{28,20},{1,17},{... | collective-permute-start | bytes 1572872 | tf_op jit(solution)/shard_map/ppermute | solution.py:417
  43.7 4.7 %collective-permute-start.16 = (bf16[128,2048]{1,0:T(8,128)(2,1)S(1)}, bf16[128,2048]{1,0:T(8,128)(2,1)S(1)}, u32[]{:S(2)}, u32[]{:S(2)}) collective-permute-start(bf16[128,2048]{1,0:T(8,128)(2,1)S(1)} %collective-permute-done.12.refs_0_), channel_id=1, source_target_pairs={{0,4},{4,0},{8,12},{12,8},{16,20},{20,16},{24,28},{28,24},{1,5},{5... | collective-permute-start | bytes 1572872 | tf_op jit(solution)/shard_map/ppermute | solution.py:32
  48.7 4.8 %collective-permute-done.2.got_ref = bf16[2,512,256]{2,1,0:T(8,128)(2,1)S(1)} collective-permute-done((bf16[2,512,256]{2,1,0:T(8,128)(2,1)S(1)}, bf16[2,512,256]{2,1,0:T(8,128)(2,1)S(1)}, u32[]{:S(2)}, u32[]{:S(2)}) %collective-permute-start.2) | collective-permute-done | bytes 524320 | tf_op jit(solution)/shard_map/ppermute | solution.py:417
  54.5 0.8 collective-permute-start.22
  55.4 0.9 collective-permute-start.23
  56.2 5.4 %collective-permute-start.3 = (bf16[2,512,256]{2,1,0:T(8,128)(2,1)S(1)}, bf16[2,512,256]{2,1,0:T(8,128)(2,1)S(1)}, u32[]{:S(2)}, u32[]{:S(2)}) collective-permute-start(bf16[2,512,256]{2,1,0:T(8,128)(2,1)S(1)} %renorm.2.up_ref), channel_id=1, source_target_pairs={{0,4},{4,0},{8,12},{12,8},{16,20},{20,16},{24,28},{28,24},{1,5},{5... | collective-permute-start | bytes 1572872 | tf_op jit(solution)/shard_map/ppermute | solution.py:32
  62.2 4.4 %window.1.seen_ref = f32[1024,512]{1,0:T(8,128)S(1)} custom-call(bf16[1024,512]{1,0:T(8,128)(2,1)} %q_ref.7, bf16[1024,512]{1,0:T(8,128)(2,1)} %k_hbm.5, bf16[1024,512]{1,0:T(8,128)(2,1)} %v_hbm.5, bf16[512,512]{1,0:T(8,128)(2,1)S(1)} %collective-permute-done.4.tail_ref), custom_call_target="tpu_custom_call" | custom-call | tf_op jit(solution)/shard_map/window/pallas_call | solution.py:239
  66.7 1.7 %collective-permute-start.26 = (bf16[128,2048]{1,0:T(8,128)(2,1)S(1)}, bf16[128,2048]{1,0:T(8,128)(2,1)S(1)}, u32[]{:S(2)}, u32[]{:S(2)}) collective-permute-start(bf16[128,2048]{1,0:T(8,128)(2,1)S(1)} %collective-permute-done.22.refs_2_), channel_id=1, source_target_pairs={{0,4},{4,0},{8,12},{12,8},{16,20},{20,16},{24,28},{28,24},{1,5},{5... | collective-permute-start | bytes 1572872 | tf_op jit(solution)/shard_map/ppermute | solution.py:32
  69.2 1.6 %collective-permute-start.11 = (bf16[256,512]{1,0:T(8,128)(2,1)S(1)}, bf16[256,512]{1,0:T(8,128)(2,1)S(1)}, u32[]{:S(2)}, u32[]{:S(2)}) collective-permute-start(bf16[256,512]{1,0:T(8,128)(2,1)S(1)} %combine.6), channel_id=1, source_target_pairs={{0,1},{1,0},{2,3},{3,2},{4,5},{5,4},{6,7},{7,6},{8,9},{9,8},{10,11... | collective-permute-start | bytes 786440 | tf_op jit(solution)/shard_map/ppermute | solution.py:32
  71.7 2.4 %collective-permute-start.10 = (bf16[256,512]{1,0:T(8,128)(2,1)S(1)}, bf16[256,512]{1,0:T(8,128)(2,1)S(1)}, u32[]{:S(2)}, u32[]{:S(2)}) collective-permute-start(bf16[256,512]{1,0:T(8,128)(2,1)S(1)} %combine.5), channel_id=1, source_target_pairs={{0,3},{1,2},{2,1},{3,0},{4,7},{5,6},{6,5},{7,4},{8,11},{9,10},{10,... | collective-permute-start | bytes 786440 | tf_op jit(solution)/shard_map/ppermute | solution.py:32
  74.9 3.2 %collective-permute-done.11.x_ref = bf16[256,512]{1,0:T(8,128)(2,1)S(1)} collective-permute-done((bf16[256,512]{1,0:T(8,128)(2,1)S(1)}, bf16[256,512]{1,0:T(8,128)(2,1)S(1)}, u32[]{:S(2)}, u32[]{:S(2)}) %collective-permute-start.11) | collective-permute-done | bytes 262176 | tf_op jit(solution)/shard_map/ppermute | solution.py:32
  78.0 2.9 %collective-permute-start.9 = (bf16[256,512]{1,0:T(8,128)(2,1)S(1)}, bf16[256,512]{1,0:T(8,128)(2,1)S(1)}, u32[]{:S(2)}, u32[]{:S(2)}) collective-permute-start(bf16[256,512]{1,0:T(8,128)(2,1)S(1)} %combine.4), channel_id=1, source_target_pairs={{0,2},{1,3},{2,0},{3,1},{4,6},{5,7},{6,4},{7,5},{8,10},{9,11},{10,... | collective-permute-start | bytes 786440 | tf_op jit(solution)/shard_map/ppermute | solution.py:32
  81.7 1.2 %copy-done.3 = bf16[512,2048]{1,0:T(8,128)(2,1)S(1)} copy-done((bf16[512,2048]{1,0:T(8,128)(2,1)S(1)}, bf16[512,2048]{1,0:T(8,128)(2,1)}, u32[]{:S(2)}) %copy-start.3) | copy-done | bytes 2097176
  84.5 1.6 %collective-permute-done.10.x_ref = bf16[256,512]{1,0:T(8,128)(2,1)S(1)} collective-permute-done((bf16[256,512]{1,0:T(8,128)(2,1)S(1)}, bf16[256,512]{1,0:T(8,128)(2,1)S(1)}, u32[]{:S(2)}, u32[]{:S(2)}) %collective-permute-start.10) | collective-permute-done | bytes 262176 | tf_op jit(solution)/shard_map/ppermute | solution.py:32
  86.9 11.0 %collective-permute-done.9.x_ref = bf16[256,512]{1,0:T(8,128)(2,1)S(1)} collective-permute-done((bf16[256,512]{1,0:T(8,128)(2,1)S(1)}, bf16[256,512]{1,0:T(8,128)(2,1)S(1)}, u32[]{:S(2)}, u32[]{:S(2)}) %collective-permute-start.9) | collective-permute-done | bytes 262176 | tf_op jit(solution)/shard_map/ppermute | solution.py:32
  97.9 1.6 %project.5 = bf16[256,2048]{1,0:T(8,128)(2,1)} custom-call(bf16[256,512]{1,0:T(8,128)(2,1)S(1)} %collective-permute-done.9.x_ref, f32[256,2048]{1,0:T(8,128)S(1)} %get-tuple-element.45.base_ref, f32[256,1]{1,0:T(8,128)S(1)} %get-tuple-element.46.squares_ref, bf16[128,2048]{1,0:T(8,128)(2,1)S(1)} %collective-permute-done.12.refs_0_, ...), custom_call_target="tpu_custom_call" | custom-call | tf_op jit(solution)/shard_map/project/pallas_call | solution.py:356
  (69 shorter events, 13.4 us)
Async XLA Ops:
  9.3 10.2 %collective-permute-start = (bf16[2,512,256]{2,1,0:T(8,128)(2,1)S(1)}, bf16[2,512,256]{2,1,0:T(8,128)(2,1)S(1)}, u32[]{:S(2)}, u32[]{:S(2)}) collective-permute-start(bf16[2,512,256]{2,1,0:T(8,128)(2,1)S(1)} %get-tuple-element.28), channel_id=1, source_target_pairs={{0,4},{4,0},{8,12},{12,8},{16,20},{20,16},{24,28},{28,24},{1,5},{5... | collective-permute-start | bytes 1572872 | tf_op jit(solution)/shard_map/ppermute | solution.py:32
  10.4 6.3 %collective-permute-start.5 = (bf16[1,512,256]{2,1,0:T(8,128)(2,1)S(1)}, bf16[1,512,256]{2,1,0:T(8,128)(2,1)S(1)}, u32[]{:S(2)}, u32[]{:S(2)}) collective-permute-start(bf16[1,512,256]{2,1,0:T(8,128)(2,1)S(1)} %contract.5), channel_id=1, source_target_pairs={{0,4},{4,0},{8,12},{12,8},{16,20},{20,16},{24,28},{28,24},{1,5},{5... | collective-permute-start | bytes 786440 | tf_op jit(solution)/shard_map/ppermute | solution.py:32
  11.7 15.5 %collective-permute-start.12 = (bf16[128,2048]{1,0:T(8,128)(2,1)S(1)}, bf16[128,2048]{1,0:T(8,128)(2,1)S(1)}, u32[]{:S(2)}, u32[]{:S(2)}) collective-permute-start(bf16[128,2048]{1,0:T(8,128)(2,1)S(1)} %get-tuple-element.42), channel_id=1, source_target_pairs={{0,1},{1,0},{2,3},{3,2},{4,6},{5,7},{6,4},{7,5},{8,9},{9,8},{10,11... | collective-permute-start | bytes 1572872 | tf_op jit(solution)/shard_map/ppermute | solution.py:383
  16.1 2.7 %copy-start.1 = (bf16[1024,512]{1,0:T(8,128)(2,1)S(1)}, bf16[1024,512]{1,0:T(8,128)(2,1)}, u32[]{:S(2)}) copy-start(bf16[1024,512]{1,0:T(8,128)(2,1)} %k_hbm.5) | copy-start | bytes 3145732
  16.1 22.4 %collective-permute-start.13 = (bf16[128,2048]{1,0:T(8,128)(2,1)S(1)}, bf16[128,2048]{1,0:T(8,128)(2,1)S(1)}, u32[]{:S(2)}, u32[]{:S(2)}) collective-permute-start(bf16[128,2048]{1,0:T(8,128)(2,1)S(1)} %load.3), channel_id=1, source_target_pairs={{0,1},{1,0},{2,3},{3,2},{4,6},{5,7},{6,4},{7,5},{8,9},{9,8},{10,11... | collective-permute-start | bytes 1572872 | tf_op jit(solution)/shard_map/ppermute | solution.py:383
  16.8 6.4 %collective-permute-start.6 = (bf16[1,512,256]{2,1,0:T(8,128)(2,1)S(1)}, bf16[1,512,256]{2,1,0:T(8,128)(2,1)S(1)}, u32[]{:S(2)}, u32[]{:S(2)}) collective-permute-start(bf16[1,512,256]{2,1,0:T(8,128)(2,1)S(1)} %get-tuple-element.37), channel_id=1, source_target_pairs={{0,8},{4,20},{8,0},{12,28},{16,24},{20,4},{24,16},{28,12},{1,9},{5... | collective-permute-start | bytes 786440 | tf_op jit(solution)/shard_map/ppermute | solution.py:417
  19.7 21.4 %collective-permute-start.1 = (bf16[2,512,256]{2,1,0:T(8,128)(2,1)S(1)}, bf16[2,512,256]{2,1,0:T(8,128)(2,1)S(1)}, u32[]{:S(2)}, u32[]{:S(2)}) collective-permute-start(bf16[2,512,256]{2,1,0:T(8,128)(2,1)S(1)} %get-tuple-element.30), channel_id=1, source_target_pairs={{0,8},{4,20},{8,0},{12,28},{16,24},{20,4},{24,16},{28,12},{1,9},{5... | collective-permute-start | bytes 1572872 | tf_op jit(solution)/shard_map/ppermute | solution.py:417
  23.3 17.5 %collective-permute-start.7 = (bf16[1,512,256]{2,1,0:T(8,128)(2,1)S(1)}, bf16[1,512,256]{2,1,0:T(8,128)(2,1)S(1)}, u32[]{:S(2)}, u32[]{:S(2)}) collective-permute-start(bf16[1,512,256]{2,1,0:T(8,128)(2,1)S(1)} %get-tuple-element.39), channel_id=1, source_target_pairs={{0,16},{4,12},{8,24},{12,4},{16,0},{20,28},{24,8},{28,20},{1,17},{... | collective-permute-start | bytes 786440 | tf_op jit(solution)/shard_map/ppermute | solution.py:417
  25.3 17.0 %collective-permute-start.4 = (bf16[512,512]{1,0:T(8,128)(2,1)S(1)}, bf16[512,512]{1,0:T(8,128)(2,1)S(1)}, u32[]{:S(2)}, u32[]{:S(2)}) collective-permute-start(bf16[512,512]{1,0:T(8,128)(2,1)S(1)} %get-tuple-element.33), channel_id=1, source_target_pairs={{0,4},{4,8},{8,12},{12,16},{16,20},{20,24},{24,28},{1,5},{5,9},{9,... | collective-permute-start | bytes 1572872 | tf_op jit(solution)/shard_map/ppermute | solution.py:376
  27.3 16.4 %collective-permute-start.14 = (bf16[128,2048]{1,0:T(8,128)(2,1)S(1)}, bf16[128,2048]{1,0:T(8,128)(2,1)S(1)}, u32[]{:S(2)}, u32[]{:S(2)}) collective-permute-start(bf16[128,2048]{1,0:T(8,128)(2,1)S(1)} %collective-permute-done.12.refs_0_), channel_id=1, source_target_pairs={{0,16},{4,12},{8,24},{12,4},{16,0},{20,28},{24,8},{28,20},{1,17},{... | collective-permute-start | bytes 1572872 | tf_op jit(solution)/shard_map/ppermute | solution.py:385
  38.5 9.9 %collective-permute-start.15 = (bf16[128,2048]{1,0:T(8,128)(2,1)S(1)}, bf16[128,2048]{1,0:T(8,128)(2,1)S(1)}, u32[]{:S(2)}, u32[]{:S(2)}) collective-permute-start(bf16[128,2048]{1,0:T(8,128)(2,1)S(1)} %collective-permute-done.13.refs_1_), channel_id=1, source_target_pairs={{0,16},{4,12},{8,24},{12,4},{16,0},{20,28},{24,8},{28,20},{1,17},{... | collective-permute-start | bytes 1572872 | tf_op jit(solution)/shard_map/ppermute | solution.py:385
  41.0 2.0 %collective-permute-start.8 = (bf16[1,512,256]{2,1,0:T(8,128)(2,1)S(1)}, bf16[1,512,256]{2,1,0:T(8,128)(2,1)S(1)}, u32[]{:S(2)}, u32[]{:S(2)}) collective-permute-start(bf16[1,512,256]{2,1,0:T(8,128)(2,1)S(1)} %renorm.3.down_ref), channel_id=1, source_target_pairs={{0,4},{4,0},{8,12},{12,8},{16,20},{20,16},{24,28},{28,24},{1,5},{5... | collective-permute-start | bytes 786440 | tf_op jit(solution)/shard_map/ppermute | solution.py:32
  41.2 12.3 %collective-permute-start.2 = (bf16[2,512,256]{2,1,0:T(8,128)(2,1)S(1)}, bf16[2,512,256]{2,1,0:T(8,128)(2,1)S(1)}, u32[]{:S(2)}, u32[]{:S(2)}) collective-permute-start(bf16[2,512,256]{2,1,0:T(8,128)(2,1)S(1)} %get-tuple-element.32), channel_id=1, source_target_pairs={{0,16},{4,12},{8,24},{12,4},{16,0},{20,28},{24,8},{28,20},{1,17},{... | collective-permute-start | bytes 1572872 | tf_op jit(solution)/shard_map/ppermute | solution.py:417
  42.3 12.2 %collective-permute-start.20 = (bf16[128,2048]{1,0:T(8,128)(2,1)S(1)}, bf16[128,2048]{1,0:T(8,128)(2,1)S(1)}, u32[]{:S(2)}, u32[]{:S(2)}) collective-permute-start(bf16[128,2048]{1,0:T(8,128)(2,1)S(1)} %collective-permute-done.12.refs_0_), channel_id=1, source_target_pairs={{4,5},{5,4},{6,7},{7,6},{12,13},{13,12},{14,15},{15,14},{20,21},{2... | collective-permute-start | bytes 1572872 | tf_op jit(solution)/shard_map/ppermute | solution.py:384
  43.0 12.4 %collective-permute-start.21 = (bf16[128,2048]{1,0:T(8,128)(2,1)S(1)}, bf16[128,2048]{1,0:T(8,128)(2,1)S(1)}, u32[]{:S(2)}, u32[]{:S(2)}) collective-permute-start(bf16[128,2048]{1,0:T(8,128)(2,1)S(1)} %collective-permute-done.13.refs_1_), channel_id=1, source_target_pairs={{4,5},{5,4},{6,7},{7,6},{12,13},{13,12},{14,15},{15,14},{20,21},{2... | collective-permute-start | bytes 1572872 | tf_op jit(solution)/shard_map/ppermute | solution.py:384
  43.7 12.6 %collective-permute-start.16 = (bf16[128,2048]{1,0:T(8,128)(2,1)S(1)}, bf16[128,2048]{1,0:T(8,128)(2,1)S(1)}, u32[]{:S(2)}, u32[]{:S(2)}) collective-permute-start(bf16[128,2048]{1,0:T(8,128)(2,1)S(1)} %collective-permute-done.12.refs_0_), channel_id=1, source_target_pairs={{0,4},{4,0},{8,12},{12,8},{16,20},{20,16},{24,28},{28,24},{1,5},{5... | collective-permute-start | bytes 1572872 | tf_op jit(solution)/shard_map/ppermute | solution.py:32
  48.4 13.3 %collective-permute-start.17 = (bf16[128,2048]{1,0:T(8,128)(2,1)S(1)}, bf16[128,2048]{1,0:T(8,128)(2,1)S(1)}, u32[]{:S(2)}, u32[]{:S(2)}) collective-permute-start(bf16[128,2048]{1,0:T(8,128)(2,1)S(1)} %collective-permute-done.13.refs_1_), channel_id=1, source_target_pairs={{0,4},{4,0},{8,12},{12,8},{16,20},{20,16},{24,28},{28,24},{1,5},{5... | collective-permute-start | bytes 1572872 | tf_op jit(solution)/shard_map/ppermute | solution.py:32
  53.5 8.2 %collective-permute-start.18 = (bf16[128,2048]{1,0:T(8,128)(2,1)S(1)}, bf16[128,2048]{1,0:T(8,128)(2,1)S(1)}, u32[]{:S(2)}, u32[]{:S(2)}) collective-permute-start(bf16[128,2048]{1,0:T(8,128)(2,1)S(1)} %collective-permute-done.14.refs_2_), channel_id=1, source_target_pairs={{0,4},{4,0},{8,12},{12,8},{16,20},{20,16},{24,28},{28,24},{1,5},{5... | collective-permute-start | bytes 1572872 | tf_op jit(solution)/shard_map/ppermute | solution.py:32
  54.5 14.0 %copy-start.2 = (bf16[1024,512]{1,0:T(8,128)(2,1)S(1)}, bf16[1024,512]{1,0:T(8,128)(2,1)}, u32[]{:S(2)}) copy-start(bf16[1024,512]{1,0:T(8,128)(2,1)} %q_ref.7) | copy-start | bytes 3145732
  54.5 12.1 %collective-permute-start.22 = (bf16[128,2048]{1,0:T(8,128)(2,1)S(1)}, bf16[128,2048]{1,0:T(8,128)(2,1)S(1)}, u32[]{:S(2)}, u32[]{:S(2)}) collective-permute-start(bf16[128,2048]{1,0:T(8,128)(2,1)S(1)} %collective-permute-done.20.refs_0_), channel_id=1, source_target_pairs={{4,12},{12,4},{20,28},{28,20},{5,13},{13,5},{21,29},{29,21},{6,14}... | collective-permute-start | bytes 1572872 | tf_op jit(solution)/shard_map/ppermute | solution.py:386
  55.4 11.4 %collective-permute-start.23 = (bf16[128,2048]{1,0:T(8,128)(2,1)S(1)}, bf16[128,2048]{1,0:T(8,128)(2,1)S(1)}, u32[]{:S(2)}, u32[]{:S(2)}) collective-permute-start(bf16[128,2048]{1,0:T(8,128)(2,1)S(1)} %collective-permute-done.21.refs_1_), channel_id=1, source_target_pairs={{4,20},{12,28},{20,4},{28,12},{5,21},{13,29},{21,5},{29,13},{6,22}... | collective-permute-start | bytes 1572872 | tf_op jit(solution)/shard_map/ppermute | solution.py:386
  56.2 12.2 %collective-permute-start.3 = (bf16[2,512,256]{2,1,0:T(8,128)(2,1)S(1)}, bf16[2,512,256]{2,1,0:T(8,128)(2,1)S(1)}, u32[]{:S(2)}, u32[]{:S(2)}) collective-permute-start(bf16[2,512,256]{2,1,0:T(8,128)(2,1)S(1)} %renorm.2.up_ref), channel_id=1, source_target_pairs={{0,4},{4,0},{8,12},{12,8},{16,20},{20,16},{24,28},{28,24},{1,5},{5... | collective-permute-start | bytes 1572872 | tf_op jit(solution)/shard_map/ppermute | solution.py:32
  61.7 7.6 %collective-permute-start.19 = (bf16[128,2048]{1,0:T(8,128)(2,1)S(1)}, bf16[128,2048]{1,0:T(8,128)(2,1)S(1)}, u32[]{:S(2)}, u32[]{:S(2)}) collective-permute-start(bf16[128,2048]{1,0:T(8,128)(2,1)S(1)} %collective-permute-done.15.refs_3_), channel_id=1, source_target_pairs={{0,4},{4,0},{8,12},{12,8},{16,20},{20,16},{24,28},{28,24},{1,5},{5... | collective-permute-start | bytes 1572872 | tf_op jit(solution)/shard_map/ppermute | solution.py:32
  61.8 9.9 %collective-permute-start.24 = (bf16[128,2048]{1,0:T(8,128)(2,1)S(1)}, bf16[128,2048]{1,0:T(8,128)(2,1)S(1)}, u32[]{:S(2)}, u32[]{:S(2)}) collective-permute-start(bf16[128,2048]{1,0:T(8,128)(2,1)S(1)} %collective-permute-done.20.refs_0_), channel_id=1, source_target_pairs={{0,4},{4,0},{8,12},{12,8},{16,20},{20,16},{24,28},{28,24},{1,5},{5... | collective-permute-start | bytes 1572872 | tf_op jit(solution)/shard_map/ppermute | solution.py:32
  66.6 17.9 %collective-permute-start.25 = (bf16[128,2048]{1,0:T(8,128)(2,1)S(1)}, bf16[128,2048]{1,0:T(8,128)(2,1)S(1)}, u32[]{:S(2)}, u32[]{:S(2)}) collective-permute-start(bf16[128,2048]{1,0:T(8,128)(2,1)S(1)} %collective-permute-done.21.refs_1_), channel_id=1, source_target_pairs={{0,4},{4,0},{8,12},{12,8},{16,20},{20,16},{24,28},{28,24},{1,5},{5... | collective-permute-start | bytes 1572872 | tf_op jit(solution)/shard_map/ppermute | solution.py:32
  66.7 17.8 %collective-permute-start.26 = (bf16[128,2048]{1,0:T(8,128)(2,1)S(1)}, bf16[128,2048]{1,0:T(8,128)(2,1)S(1)}, u32[]{:S(2)}, u32[]{:S(2)}) collective-permute-start(bf16[128,2048]{1,0:T(8,128)(2,1)S(1)} %collective-permute-done.22.refs_2_), channel_id=1, source_target_pairs={{0,4},{4,0},{8,12},{12,8},{16,20},{20,16},{24,28},{28,24},{1,5},{5... | collective-permute-start | bytes 1572872 | tf_op jit(solution)/shard_map/ppermute | solution.py:32
  68.5 16.1 %collective-permute-start.27 = (bf16[128,2048]{1,0:T(8,128)(2,1)S(1)}, bf16[128,2048]{1,0:T(8,128)(2,1)S(1)}, u32[]{:S(2)}, u32[]{:S(2)}) collective-permute-start(bf16[128,2048]{1,0:T(8,128)(2,1)S(1)} %collective-permute-done.23.refs_3_), channel_id=1, source_target_pairs={{0,4},{4,0},{8,12},{12,8},{16,20},{20,16},{24,28},{28,24},{1,5},{5... | collective-permute-start | bytes 1572872 | tf_op jit(solution)/shard_map/ppermute | solution.py:32
  69.2 8.8 %collective-permute-start.11 = (bf16[256,512]{1,0:T(8,128)(2,1)S(1)}, bf16[256,512]{1,0:T(8,128)(2,1)S(1)}, u32[]{:S(2)}, u32[]{:S(2)}) collective-permute-start(bf16[256,512]{1,0:T(8,128)(2,1)S(1)} %combine.6), channel_id=1, source_target_pairs={{0,1},{1,0},{2,3},{3,2},{4,5},{5,4},{6,7},{7,6},{8,9},{9,8},{10,11... | collective-permute-start | bytes 786440 | tf_op jit(solution)/shard_map/ppermute | solution.py:32
  71.7 14.4 %collective-permute-start.10 = (bf16[256,512]{1,0:T(8,128)(2,1)S(1)}, bf16[256,512]{1,0:T(8,128)(2,1)S(1)}, u32[]{:S(2)}, u32[]{:S(2)}) collective-permute-start(bf16[256,512]{1,0:T(8,128)(2,1)S(1)} %combine.5), channel_id=1, source_target_pairs={{0,3},{1,2},{2,1},{3,0},{4,7},{5,6},{6,5},{7,4},{8,11},{9,10},{10,... | collective-permute-start | bytes 786440 | tf_op jit(solution)/shard_map/ppermute | solution.py:32
  78.0 19.9 %collective-permute-start.9 = (bf16[256,512]{1,0:T(8,128)(2,1)S(1)}, bf16[256,512]{1,0:T(8,128)(2,1)S(1)}, u32[]{:S(2)}, u32[]{:S(2)}) collective-permute-start(bf16[256,512]{1,0:T(8,128)(2,1)S(1)} %combine.4), channel_id=1, source_target_pairs={{0,2},{1,3},{2,0},{3,1},{4,6},{5,7},{6,4},{7,5},{8,10},{9,11},{10,... | collective-permute-start | bytes 786440 | tf_op jit(solution)/shard_map/ppermute | solution.py:32
  81.4 1.6 %copy-start.3 = (bf16[512,2048]{1,0:T(8,128)(2,1)S(1)}, bf16[512,2048]{1,0:T(8,128)(2,1)}, u32[]{:S(2)}) copy-start(bf16[512,2048]{1,0:T(8,128)(2,1)} %w_hbm.3) | copy-start | bytes 6291460
  81.4 1.6 %copy-start.8 = (bf16[512]{0:T(512)(128)(2,1)S(1)}, bf16[512]{0:T(512)(128)(2,1)}, u32[]{:S(2)}) copy-start(bf16[512]{0:T(512)(128)(2,1)} %gain_hbm.3) | copy-start | bytes 3076
  (6 other events, 6.3 us)

commit v6 on v4

--- a/solution.py
+++ b/solution.py
@@ -252,31 +252,46 @@
     )(*far_core(queries, keys, values), *near_core(tail))
 
 
-def apply_kernel(slot, q_ref, seen_ref, down_ref, up_ref, down_c_ref, up_c_ref, out_ref):
+def mix_kernel(slot, q_ref, up_ref, up_c_ref, out_ref):
+    rows, width = out_ref.shape
+    here = pl.ds(pl.multiple_of((lax.axis_index("head").astype(jnp.int32) ^ slot) * rows, rows), rows)
+    q = q_ref[here, :]
+    half = width // 2
+    for j, ref in enumerate((up_ref, up_c_ref)):
+        gate = dot(q, ref[0])
+        up = dot(q, ref[1])
+        out_ref[:, j * half : (j + 1) * half] = (gate * jax.nn.sigmoid(gate) * up).astype(jnp.bfloat16)
+
+
+def mix(slot, queries, up, up_c, rows):
+    return pl.pallas_call(
+        functools.partial(mix_kernel, slot),
+        out_shape=pltpu.VMEM((rows, queries.shape[1]), jnp.bfloat16),
+        compiler_params=grant(8),
+        in_specs=[VMEM] * 3,
+        out_specs=VMEM,
+        name="mix",
+    )(*near_core(queries, up, up_c))
+
+
+def down_kernel(slot, mixed_ref, seen_ref, down_ref, down_c_ref, out_ref):
     rows, width = out_ref.shape
     own, rest = halves(width)
     here = pl.ds(pl.multiple_of((lax.axis_index("head").astype(jnp.int32) ^ slot) * rows, rows), rows)
-    q = q_ref[here, :]
-    mixed = []
-    for ref in (up_ref, up_c_ref):
-        gate = dot(q, ref[0])
-        up = dot(q, ref[1])
-        mixed.append((gate * jax.nn.sigmoid(gate) * up).astype(jnp.bfloat16))
-    mixed = jnp.concatenate(mixed, axis=1)
     for ref, at in ((down_ref, own), (down_c_ref, rest)):
         down = jnp.concatenate([ref[0, own, :], ref[0, rest, :]], axis=0)
-        out_ref[:, at] = (dot(mixed, down) + seen_ref[here, at]).astype(jnp.bfloat16)
-
-
-def apply_fast(slot, queries, seen, weights, rows):
-    return pl.pallas_call(
-        functools.partial(apply_kernel, slot),
-        out_shape=pltpu.VMEM((rows, queries.shape[1]), jnp.bfloat16),
-        compiler_params=grant(16),
-        in_specs=[VMEM] * 6,
+        out_ref[:, at] = (dot(mixed_ref[...], down) + seen_ref[here, at]).astype(jnp.bfloat16)
+
+
+def combine(slot, mixed, seen, down, down_c):
+    return pl.pallas_call(
+        functools.partial(down_kernel, slot),
+        out_shape=pltpu.VMEM(mixed.shape, jnp.bfloat16),
+        compiler_params=grant(8),
+        in_specs=[VMEM] * 4,
         out_specs=VMEM,
-        name="apply",
-    )(*near_core(queries, seen, *weights))
+        name="combine",
+    )(*near_core(mixed, seen, down, down_c))
 
 
 def own_project_kernel(x_ref, gain_ref, w_ref, out_ref, squares_ref):
@@ -412,7 +427,8 @@
     rows = tok_rows // heads
     blocks = {}
     for k in send_order(heads) + [0]:
-        combined = apply_fast(k, queries, seen, weights, rows)
+        mixed = mix(k, queries, weights[1], weights[3], rows)
+        combined = combine(k, mixed, seen, weights[0], weights[2])
         blocks[k] = swap(combined, "head", k) if k else combined
     base, squares = own_project(blocks[0], norm_gain, out_weight)
     for k in (1, 3, 2):

time: 104 us -> 100 us (0.962)
  starting transfers between devices: 42.4 us -> 38 us
  waiting for transfers between devices: 36.7 us -> 35.1 us
  local copies, waits for them, and re-layouts: 6.28 us -> 7.53 us
    ppermute x15, starting transfers between devices: 25.2 us -> 20.8 us  [swap(): lax.ppermute(value, axis, [(i, i ^ mask) for i in range(lax.axis_size(axi...]
    ppermute x15, waiting for transfers between devices: 17.4 us -> 15.8 us  [swap(): lax.ppermute(value, axis, [(i, i ^ mask) for i in range(lax.axis_size(axi...]
    unnamed x20, local copies, waits for them, and re-layouts: 6.28 us -> 7.53 us
    pallas_call x4 -> x8, Pallas kernels: 2.3 us -> 3.04 us  [the longest x4 1.78 us: mix(): pl.pallas_call(functools.partial(mix_kernel, slot), out_shape=pltpu.VMEM(...]
  transfers between devices with their start and end apart: 28 -> 28, of which waited for: 7 -> 7; matrix products, arithmetic and copies ran while one was open for 0% -> 0% of each run, Pallas kernels for 13% -> 14%
where the time goes in v6:
time: 100 us; the launch traced here: 99.8 us
  starting transfers between devices  38 us (38%)
  waiting for transfers between devices  35.1 us (35%)
  Pallas kernels  18.6 us (19%)
  local copies, waits for them, and re-layouts  7.53 us (8%)
    ppermute x15, starting transfers between devices, swap(): lax.ppermute(value, axis, [(i, i ^ mask) for i in range(lax.axis_size(axi...  20.8 us
    ppermute x15, waiting for transfers between devices, swap(): lax.ppermute(value, axis, [(i, i ^ mask) for i in range(lax.axis_size(axi...  15.8 us
    ppermute x2, waiting for transfers between devices, step(): early.append(lax.ppermute(chunk, ('ctx', 'head'), over))  10.9 us
    ppermute x4, waiting for transfers between devices, step(): got = lax.ppermute(send, 'ctx', pairs)  8.45 us
    unnamed x20, local copies, waits for them, and re-layouts  7.53 us
    ppermute x4, starting transfers between devices, step(): got = lax.ppermute(send, 'ctx', pairs)  5.14 us
    ppermute x2, starting transfers between devices, step(): far.append(lax.ppermute(early[j], 'ctx', cross))  4.57 us
    pallas_call x1, Pallas kernels, window(): pl.pallas_call(window_kernel, out_shape=pltpu.VMEM(queries.shape, jnp.flo...  4.37 us
  transfers between devices with their start and end apart: 28, of which 7 were waited for; matrix products, arithmetic and copies ran while one was open for 0% of the time, Pallas kernels for 14%

profile of v6, /device:TPU:0, one launch (start us, length us, event | category | flops | bytes accessed | tf_op | source)
XLA Modules:
  0.0 99.8 jit_solution(5204692880967692594)
XLA Ops:
  0.0 1.2 %copy-done.1 = bf16[1024,512]{1,0:T(8,128)(2,1)S(1)} copy-done((bf16[1024,512]{1,0:T(8,128)(2,1)S(1)}, bf16[1024,512]{1,0:T(8,128)(2,1)}, u32[]{:S(2)}) %copy-start.1) | copy-done | bytes 1048600
  1.2 1.2 %copy-done.3 = bf16[1024,512]{1,0:T(8,128)(2,1)S(1)} copy-done((bf16[1024,512]{1,0:T(8,128)(2,1)S(1)}, bf16[1024,512]{1,0:T(8,128)(2,1)}, u32[]{:S(2)}) %copy-start.3) | copy-done | bytes 1048600
  2.5 1.0 %copy-done.5 = bf16[1,512,512]{2,1,0:T(8,128)(2,1)S(1)} copy-done((bf16[1,512,512]{2,1,0:T(8,128)(2,1)S(1)}, bf16[1,512,512]{2,1,0:T(8,128)(2,1)}, u32[]{:S(2)}) %copy-start.5) | copy-done | bytes 524312
  3.5 1.0 %copy-done.6 = bf16[1,512,512]{2,1,0:T(8,128)(2,1)S(1)} copy-done((bf16[1,512,512]{2,1,0:T(8,128)(2,1)S(1)}, bf16[1,512,512]{2,1,0:T(8,128)(2,1)}, u32[]{:S(2)}) %copy-start.6) | copy-done | bytes 524312
  4.5 1.0 %copy-done.7 = bf16[1,512,512]{2,1,0:T(8,128)(2,1)S(1)} copy-done((bf16[1,512,512]{2,1,0:T(8,128)(2,1)S(1)}, bf16[1,512,512]{2,1,0:T(8,128)(2,1)}, u32[]{:S(2)}) %copy-start.7) | copy-done | bytes 524312
  6.3 3.1 %pushes.1 = (bf16[2,512,256]{2,1,0:T(8,128)(2,1)S(1)}, bf16[1024,512]{1,0:T(8,128)(2,1)S(1)}, bf16[1024,512]{1,0:T(8,128)(2,1)S(1)}, bf16[1024,512]{1,0:T(8,128)(2,1)S(1)}, bf16[1024,512]{1,0:T(8,128)(2,1)S(1)}) custom-call(bf16[1024,512]{1,0:T(8,128)(2,1)S(1)} %copy-done.1, bf16[1024,512]{1,0:T(8,128)(2,1)S(1)} %copy-done.3, f32[1,1024]{1,0:T(1,128)S(1)} %bitcast.1, ...), custom_call_target="tpu_custom_call" | custom-call | tf_op jit(solution)/shard_map/pushes/pallas_call | solution.py:129
  10.5 1.4 %load.1 = (bf16[512,512]{1,0:T(8,128)(2,1)S(1)}, bf16[128,2048]{1,0:T(8,128)(2,1)S(1)}, bf16[128,2048]{1,0:T(8,128)(2,1)S(1)}) custom-call(bf16[1024,512]{1,0:T(8,128)(2,1)} %k_hbm.3, bf16[1024,512]{1,0:T(8,128)(2,1)} %v_hbm.3, bf16[512]{0:T(512)(128)(2,1)} %gain_ref.1, bf16[512,2048]{1,0:T(8,128)(2,1)} %w_ref.1), custom_call_target="tpu_custom_call" | custom-call | tf_op jit(solution)/shard_map/load/pallas_call | solution.py:84
  11.9 3.1 %collective-permute-start.12 = (bf16[128,2048]{1,0:T(8,128)(2,1)S(1)}, bf16[128,2048]{1,0:T(8,128)(2,1)S(1)}, u32[]{:S(2)}, u32[]{:S(2)}) collective-permute-start(bf16[128,2048]{1,0:T(8,128)(2,1)S(1)} %get-tuple-element.43), channel_id=1, source_target_pairs={{0,1},{1,0},{2,3},{3,2},{4,6},{5,7},{6,4},{7,5},{8,9},{9,8},{10,11... | collective-permute-start | bytes 1572872 | tf_op jit(solution)/shard_map/ppermute | solution.py:385
  15.7 1.9 %collective-permute-start.6 = (bf16[1,512,256]{2,1,0:T(8,128)(2,1)S(1)}, bf16[1,512,256]{2,1,0:T(8,128)(2,1)S(1)}, u32[]{:S(2)}, u32[]{:S(2)}) collective-permute-start(bf16[1,512,256]{2,1,0:T(8,128)(2,1)S(1)} %get-tuple-element.38), channel_id=1, source_target_pairs={{0,8},{4,20},{8,0},{12,28},{16,24},{20,4},{24,16},{28,12},{1,9},{5... | collective-permute-start | bytes 786440 | tf_op jit(solution)/shard_map/ppermute | solution.py:419
  18.8 3.4 %collective-permute-done.6.got_ref = bf16[1,512,256]{2,1,0:T(8,128)(2,1)S(1)} collective-permute-done((bf16[1,512,256]{2,1,0:T(8,128)(2,1)S(1)}, bf16[1,512,256]{2,1,0:T(8,128)(2,1)S(1)}, u32[]{:S(2)}, u32[]{:S(2)}) %collective-permute-start.6) | collective-permute-done | bytes 262176 | tf_op jit(solution)/shard_map/ppermute | solution.py:419
  22.2 2.0 %collective-permute-start.7 = (bf16[1,512,256]{2,1,0:T(8,128)(2,1)S(1)}, bf16[1,512,256]{2,1,0:T(8,128)(2,1)S(1)}, u32[]{:S(2)}, u32[]{:S(2)}) collective-permute-start(bf16[1,512,256]{2,1,0:T(8,128)(2,1)S(1)} %get-tuple-element.40), channel_id=1, source_target_pairs={{0,16},{4,12},{8,24},{12,4},{16,0},{20,28},{24,8},{28,20},{1,17},{... | collective-permute-start | bytes 786440 | tf_op jit(solution)/shard_map/ppermute | solution.py:419
  24.2 1.3 %collective-permute-start.4 = (bf16[512,512]{1,0:T(8,128)(2,1)S(1)}, bf16[512,512]{1,0:T(8,128)(2,1)S(1)}, u32[]{:S(2)}, u32[]{:S(2)}) collective-permute-start(bf16[512,512]{1,0:T(8,128)(2,1)S(1)} %get-tuple-element.34), channel_id=1, source_target_pairs={{0,4},{4,8},{8,12},{12,16},{16,20},{20,24},{24,28},{1,5},{5,9},{9,... | collective-permute-start | bytes 1572872 | tf_op jit(solution)/shard_map/ppermute | solution.py:378
  25.5 2.0 %collective-permute-done.12.refs_0_ = bf16[128,2048]{1,0:T(8,128)(2,1)S(1)} collective-permute-done((bf16[128,2048]{1,0:T(8,128)(2,1)S(1)}, bf16[128,2048]{1,0:T(8,128)(2,1)S(1)}, u32[]{:S(2)}, u32[]{:S(2)}) %collective-permute-start.12) | collective-permute-done | bytes 524320 | tf_op jit(solution)/shard_map/ppermute | solution.py:385
  27.4 2.3 %collective-permute-start.14 = (bf16[128,2048]{1,0:T(8,128)(2,1)S(1)}, bf16[128,2048]{1,0:T(8,128)(2,1)S(1)}, u32[]{:S(2)}, u32[]{:S(2)}) collective-permute-start(bf16[128,2048]{1,0:T(8,128)(2,1)S(1)} %collective-permute-done.12.refs_0_), channel_id=1, source_target_pairs={{0,16},{4,12},{8,24},{12,4},{16,0},{20,28},{24,8},{28,20},{1,17},{... | collective-permute-start | bytes 1572872 | tf_op jit(solution)/shard_map/ppermute | solution.py:387
  29.8 8.9 %collective-permute-done.13.refs_1_ = bf16[128,2048]{1,0:T(8,128)(2,1)S(1)} collective-permute-done((bf16[128,2048]{1,0:T(8,128)(2,1)S(1)}, bf16[128,2048]{1,0:T(8,128)(2,1)S(1)}, u32[]{:S(2)}, u32[]{:S(2)}) %collective-permute-start.13) | collective-permute-done | bytes 524320 | tf_op jit(solution)/shard_map/ppermute | solution.py:385
  38.7 2.3 %collective-permute-start.15 = (bf16[128,2048]{1,0:T(8,128)(2,1)S(1)}, bf16[128,2048]{1,0:T(8,128)(2,1)S(1)}, u32[]{:S(2)}, u32[]{:S(2)}) collective-permute-start(bf16[128,2048]{1,0:T(8,128)(2,1)S(1)} %collective-permute-done.13.refs_1_), channel_id=1, source_target_pairs={{0,16},{4,12},{8,24},{12,4},{16,0},{20,28},{24,8},{28,20},{1,17},{... | collective-permute-start | bytes 1572872 | tf_op jit(solution)/shard_map/ppermute | solution.py:387
  41.4 1.0 %collective-permute-start.2 = (bf16[2,512,256]{2,1,0:T(8,128)(2,1)S(1)}, bf16[2,512,256]{2,1,0:T(8,128)(2,1)S(1)}, u32[]{:S(2)}, u32[]{:S(2)}) collective-permute-start(bf16[2,512,256]{2,1,0:T(8,128)(2,1)S(1)} %get-tuple-element.33), channel_id=1, source_target_pairs={{0,16},{4,12},{8,24},{12,4},{16,0},{20,28},{24,8},{28,20},{1,17},{... | collective-permute-start | bytes 1572872 | tf_op jit(solution)/shard_map/ppermute | solution.py:419
  43.9 4.7 %collective-permute-start.16 = (bf16[128,2048]{1,0:T(8,128)(2,1)S(1)}, bf16[128,2048]{1,0:T(8,128)(2,1)S(1)}, u32[]{:S(2)}, u32[]{:S(2)}) collective-permute-start(bf16[128,2048]{1,0:T(8,128)(2,1)S(1)} %collective-permute-done.12.refs_0_), channel_id=1, source_target_pairs={{0,4},{4,0},{8,12},{12,8},{16,20},{20,16},{24,28},{28,24},{1,5},{5... | collective-permute-start | bytes 1572872 | tf_op jit(solution)/shard_map/ppermute | solution.py:32
  48.6 5.1 %collective-permute-done.2.got_ref = bf16[2,512,256]{2,1,0:T(8,128)(2,1)S(1)} collective-permute-done((bf16[2,512,256]{2,1,0:T(8,128)(2,1)S(1)}, bf16[2,512,256]{2,1,0:T(8,128)(2,1)S(1)}, u32[]{:S(2)}, u32[]{:S(2)}) %collective-permute-start.2) | collective-permute-done | bytes 524320 | tf_op jit(solution)/shard_map/ppermute | solution.py:419
  54.2 0.8 collective-permute-start.22
  55.0 0.9 collective-permute-start.23
  55.9 6.0 %collective-permute-start.3 = (bf16[2,512,256]{2,1,0:T(8,128)(2,1)S(1)}, bf16[2,512,256]{2,1,0:T(8,128)(2,1)S(1)}, u32[]{:S(2)}, u32[]{:S(2)}) collective-permute-start(bf16[2,512,256]{2,1,0:T(8,128)(2,1)S(1)} %renorm.2.up_ref), channel_id=1, source_target_pairs={{0,4},{4,0},{8,12},{12,8},{16,20},{20,16},{24,28},{28,24},{1,5},{5... | collective-permute-start | bytes 1572872 | tf_op jit(solution)/shard_map/ppermute | solution.py:32
  62.4 4.4 %window.1.seen_ref = f32[1024,512]{1,0:T(8,128)S(1)} custom-call(bf16[1024,512]{1,0:T(8,128)(2,1)} %q_ref.7, bf16[1024,512]{1,0:T(8,128)(2,1)} %k_hbm.3, bf16[1024,512]{1,0:T(8,128)(2,1)} %v_hbm.3, bf16[512,512]{1,0:T(8,128)(2,1)S(1)} %collective-permute-done.4.tail_ref), custom_call_target="tpu_custom_call" | custom-call | tf_op jit(solution)/shard_map/window/pallas_call | solution.py:242
  66.9 1.7 %collective-permute-start.26 = (bf16[128,2048]{1,0:T(8,128)(2,1)S(1)}, bf16[128,2048]{1,0:T(8,128)(2,1)S(1)}, u32[]{:S(2)}, u32[]{:S(2)}) collective-permute-start(bf16[128,2048]{1,0:T(8,128)(2,1)S(1)} %collective-permute-done.22.refs_2_), channel_id=1, source_target_pairs={{0,4},{4,0},{8,12},{12,8},{16,20},{20,16},{24,28},{28,24},{1,5},{5... | collective-permute-start | bytes 1572872 | tf_op jit(solution)/shard_map/ppermute | solution.py:32
  69.4 1.6 %collective-permute-start.11 = (bf16[256,512]{1,0:T(8,128)(2,1)S(1)}, bf16[256,512]{1,0:T(8,128)(2,1)S(1)}, u32[]{:S(2)}, u32[]{:S(2)}) collective-permute-start(bf16[256,512]{1,0:T(8,128)(2,1)S(1)} %combine.6), channel_id=1, source_target_pairs={{0,1},{1,0},{2,3},{3,2},{4,5},{5,4},{6,7},{7,6},{8,9},{9,8},{10,11... | collective-permute-start | bytes 786440 | tf_op jit(solution)/shard_map/ppermute | solution.py:32
  71.8 2.4 %collective-permute-start.10 = (bf16[256,512]{1,0:T(8,128)(2,1)S(1)}, bf16[256,512]{1,0:T(8,128)(2,1)S(1)}, u32[]{:S(2)}, u32[]{:S(2)}) collective-permute-start(bf16[256,512]{1,0:T(8,128)(2,1)S(1)} %combine.5), channel_id=1, source_target_pairs={{0,3},{1,2},{2,1},{3,0},{4,7},{5,6},{6,5},{7,4},{8,11},{9,10},{10,... | collective-permute-start | bytes 786440 | tf_op jit(solution)/shard_map/ppermute | solution.py:32
  75.0 3.2 %collective-permute-done.11.x_ref = bf16[256,512]{1,0:T(8,128)(2,1)S(1)} collective-permute-done((bf16[256,512]{1,0:T(8,128)(2,1)S(1)}, bf16[256,512]{1,0:T(8,128)(2,1)S(1)}, u32[]{:S(2)}, u32[]{:S(2)}) %collective-permute-start.11) | collective-permute-done | bytes 262176 | tf_op jit(solution)/shard_map/ppermute | solution.py:32
  78.2 2.9 %collective-permute-start.9 = (bf16[256,512]{1,0:T(8,128)(2,1)S(1)}, bf16[256,512]{1,0:T(8,128)(2,1)S(1)}, u32[]{:S(2)}, u32[]{:S(2)}) collective-permute-start(bf16[256,512]{1,0:T(8,128)(2,1)S(1)} %combine.4), channel_id=1, source_target_pairs={{0,2},{1,3},{2,0},{3,1},{4,6},{5,7},{6,4},{7,5},{8,10},{9,11},{10,... | collective-permute-start | bytes 786440 | tf_op jit(solution)/shard_map/ppermute | solution.py:32
  81.9 1.2 %copy-done.4 = bf16[512,2048]{1,0:T(8,128)(2,1)S(1)} copy-done((bf16[512,2048]{1,0:T(8,128)(2,1)S(1)}, bf16[512,2048]{1,0:T(8,128)(2,1)}, u32[]{:S(2)}) %copy-start.4) | copy-done | bytes 2097176
  84.7 1.6 %collective-permute-done.10.x_ref = bf16[256,512]{1,0:T(8,128)(2,1)S(1)} collective-permute-done((bf16[256,512]{1,0:T(8,128)(2,1)S(1)}, bf16[256,512]{1,0:T(8,128)(2,1)S(1)}, u32[]{:S(2)}, u32[]{:S(2)}) %collective-permute-start.10) | collective-permute-done | bytes 262176 | tf_op jit(solution)/shard_map/ppermute | solution.py:32
  87.1 11.0 %collective-permute-done.9.x_ref = bf16[256,512]{1,0:T(8,128)(2,1)S(1)} collective-permute-done((bf16[256,512]{1,0:T(8,128)(2,1)S(1)}, bf16[256,512]{1,0:T(8,128)(2,1)S(1)}, u32[]{:S(2)}, u32[]{:S(2)}) %collective-permute-start.9) | collective-permute-done | bytes 262176 | tf_op jit(solution)/shard_map/ppermute | solution.py:32
  98.1 1.6 %project.5 = bf16[256,2048]{1,0:T(8,128)(2,1)} custom-call(bf16[256,512]{1,0:T(8,128)(2,1)S(1)} %collective-permute-done.9.x_ref, f32[256,2048]{1,0:T(8,128)S(1)} %get-tuple-element.47.base_ref, f32[256,1]{1,0:T(8,128)S(1)} %get-tuple-element.48.squares_ref, bf16[128,2048]{1,0:T(8,128)(2,1)S(1)} %collective-permute-done.12.refs_0_, ...), custom_call_target="tpu_custom_call" | custom-call | tf_op jit(solution)/shard_map/project/pallas_call | solution.py:359
  (68 shorter events, 12.1 us)
Async XLA Ops:
  9.3 9.0 %collective-permute-start = (bf16[2,512,256]{2,1,0:T(8,128)(2,1)S(1)}, bf16[2,512,256]{2,1,0:T(8,128)(2,1)S(1)}, u32[]{:S(2)}, u32[]{:S(2)}) collective-permute-start(bf16[2,512,256]{2,1,0:T(8,128)(2,1)S(1)} %get-tuple-element.29), channel_id=1, source_target_pairs={{0,4},{4,0},{8,12},{12,8},{16,20},{20,16},{24,28},{28,24},{1,5},{5... | collective-permute-start | bytes 1572872 | tf_op jit(solution)/shard_map/ppermute | solution.py:32
  10.4 5.2 %collective-permute-start.5 = (bf16[1,512,256]{2,1,0:T(8,128)(2,1)S(1)}, bf16[1,512,256]{2,1,0:T(8,128)(2,1)S(1)}, u32[]{:S(2)}, u32[]{:S(2)}) collective-permute-start(bf16[1,512,256]{2,1,0:T(8,128)(2,1)S(1)} %contract.5), channel_id=1, source_target_pairs={{0,4},{4,0},{8,12},{12,8},{16,20},{20,16},{24,28},{28,24},{1,5},{5... | collective-permute-start | bytes 786440 | tf_op jit(solution)/shard_map/ppermute | solution.py:32
  11.9 5.7 %copy-start.2 = (bf16[1024,512]{1,0:T(8,128)(2,1)S(1)}, bf16[1024,512]{1,0:T(8,128)(2,1)}, u32[]{:S(2)}) copy-start(bf16[1024,512]{1,0:T(8,128)(2,1)} %k_hbm.3) | copy-start | bytes 3145732
  11.9 15.5 %collective-permute-start.12 = (bf16[128,2048]{1,0:T(8,128)(2,1)S(1)}, bf16[128,2048]{1,0:T(8,128)(2,1)S(1)}, u32[]{:S(2)}, u32[]{:S(2)}) collective-permute-start(bf16[128,2048]{1,0:T(8,128)(2,1)S(1)} %get-tuple-element.43), channel_id=1, source_target_pairs={{0,1},{1,0},{2,3},{3,2},{4,6},{5,7},{6,4},{7,5},{8,9},{9,8},{10,11... | collective-permute-start | bytes 1572872 | tf_op jit(solution)/shard_map/ppermute | solution.py:385
  15.0 23.7 %collective-permute-start.13 = (bf16[128,2048]{1,0:T(8,128)(2,1)S(1)}, bf16[128,2048]{1,0:T(8,128)(2,1)S(1)}, u32[]{:S(2)}, u32[]{:S(2)}) collective-permute-start(bf16[128,2048]{1,0:T(8,128)(2,1)S(1)} %get-tuple-element.44), channel_id=1, source_target_pairs={{0,1},{1,0},{2,3},{3,2},{4,6},{5,7},{6,4},{7,5},{8,9},{9,8},{10,11... | collective-permute-start | bytes 1572872 | tf_op jit(solution)/shard_map/ppermute | solution.py:385
  15.7 6.4 %collective-permute-start.6 = (bf16[1,512,256]{2,1,0:T(8,128)(2,1)S(1)}, bf16[1,512,256]{2,1,0:T(8,128)(2,1)S(1)}, u32[]{:S(2)}, u32[]{:S(2)}) collective-permute-start(bf16[1,512,256]{2,1,0:T(8,128)(2,1)S(1)} %get-tuple-element.38), channel_id=1, source_target_pairs={{0,8},{4,20},{8,0},{12,28},{16,24},{20,4},{24,16},{28,12},{1,9},{5... | collective-permute-start | bytes 786440 | tf_op jit(solution)/shard_map/ppermute | solution.py:419
  18.5 22.7 %collective-permute-start.1 = (bf16[2,512,256]{2,1,0:T(8,128)(2,1)S(1)}, bf16[2,512,256]{2,1,0:T(8,128)(2,1)S(1)}, u32[]{:S(2)}, u32[]{:S(2)}) collective-permute-start(bf16[2,512,256]{2,1,0:T(8,128)(2,1)S(1)} %get-tuple-element.31), channel_id=1, source_target_pairs={{0,8},{4,20},{8,0},{12,28},{16,24},{20,4},{24,16},{28,12},{1,9},{5... | collective-permute-start | bytes 1572872 | tf_op jit(solution)/shard_map/ppermute | solution.py:419
  22.2 18.7 %collective-permute-start.7 = (bf16[1,512,256]{2,1,0:T(8,128)(2,1)S(1)}, bf16[1,512,256]{2,1,0:T(8,128)(2,1)S(1)}, u32[]{:S(2)}, u32[]{:S(2)}) collective-permute-start(bf16[1,512,256]{2,1,0:T(8,128)(2,1)S(1)} %get-tuple-element.40), channel_id=1, source_target_pairs={{0,16},{4,12},{8,24},{12,4},{16,0},{20,28},{24,8},{28,20},{1,17},{... | collective-permute-start | bytes 786440 | tf_op jit(solution)/shard_map/ppermute | solution.py:419
  24.2 18.3 %collective-permute-start.4 = (bf16[512,512]{1,0:T(8,128)(2,1)S(1)}, bf16[512,512]{1,0:T(8,128)(2,1)S(1)}, u32[]{:S(2)}, u32[]{:S(2)}) collective-permute-start(bf16[512,512]{1,0:T(8,128)(2,1)S(1)} %get-tuple-element.34), channel_id=1, source_target_pairs={{0,4},{4,8},{8,12},{12,16},{16,20},{20,24},{24,28},{1,5},{5,9},{9,... | collective-permute-start | bytes 1572872 | tf_op jit(solution)/shard_map/ppermute | solution.py:378
  27.4 16.4 %collective-permute-start.14 = (bf16[128,2048]{1,0:T(8,128)(2,1)S(1)}, bf16[128,2048]{1,0:T(8,128)(2,1)S(1)}, u32[]{:S(2)}, u32[]{:S(2)}) collective-permute-start(bf16[128,2048]{1,0:T(8,128)(2,1)S(1)} %collective-permute-done.12.refs_0_), channel_id=1, source_target_pairs={{0,16},{4,12},{8,24},{12,4},{16,0},{20,28},{24,8},{28,20},{1,17},{... | collective-permute-start | bytes 1572872 | tf_op jit(solution)/shard_map/ppermute | solution.py:387
  38.7 9.9 %collective-permute-start.15 = (bf16[128,2048]{1,0:T(8,128)(2,1)S(1)}, bf16[128,2048]{1,0:T(8,128)(2,1)S(1)}, u32[]{:S(2)}, u32[]{:S(2)}) collective-permute-start(bf16[128,2048]{1,0:T(8,128)(2,1)S(1)} %collective-permute-done.13.refs_1_), channel_id=1, source_target_pairs={{0,16},{4,12},{8,24},{12,4},{16,0},{20,28},{24,8},{28,20},{1,17},{... | collective-permute-start | bytes 1572872 | tf_op jit(solution)/shard_map/ppermute | solution.py:387
  41.2 2.0 %collective-permute-start.8 = (bf16[1,512,256]{2,1,0:T(8,128)(2,1)S(1)}, bf16[1,512,256]{2,1,0:T(8,128)(2,1)S(1)}, u32[]{:S(2)}, u32[]{:S(2)}) collective-permute-start(bf16[1,512,256]{2,1,0:T(8,128)(2,1)S(1)} %renorm.3.down_ref), channel_id=1, source_target_pairs={{0,4},{4,0},{8,12},{12,8},{16,20},{20,16},{24,28},{28,24},{1,5},{5... | collective-permute-start | bytes 786440 | tf_op jit(solution)/shard_map/ppermute | solution.py:32
  41.4 12.3 %collective-permute-start.2 = (bf16[2,512,256]{2,1,0:T(8,128)(2,1)S(1)}, bf16[2,512,256]{2,1,0:T(8,128)(2,1)S(1)}, u32[]{:S(2)}, u32[]{:S(2)}) collective-permute-start(bf16[2,512,256]{2,1,0:T(8,128)(2,1)S(1)} %get-tuple-element.33), channel_id=1, source_target_pairs={{0,16},{4,12},{8,24},{12,4},{16,0},{20,28},{24,8},{28,20},{1,17},{... | collective-permute-start | bytes 1572872 | tf_op jit(solution)/shard_map/ppermute | solution.py:419
  42.4 11.7 %collective-permute-start.20 = (bf16[128,2048]{1,0:T(8,128)(2,1)S(1)}, bf16[128,2048]{1,0:T(8,128)(2,1)S(1)}, u32[]{:S(2)}, u32[]{:S(2)}) collective-permute-start(bf16[128,2048]{1,0:T(8,128)(2,1)S(1)} %collective-permute-done.12.refs_0_), channel_id=1, source_target_pairs={{4,5},{5,4},{6,7},{7,6},{12,13},{13,12},{14,15},{15,14},{20,21},{2... | collective-permute-start | bytes 1572872 | tf_op jit(solution)/shard_map/ppermute | solution.py:386
  43.1 11.9 %collective-permute-start.21 = (bf16[128,2048]{1,0:T(8,128)(2,1)S(1)}, bf16[128,2048]{1,0:T(8,128)(2,1)S(1)}, u32[]{:S(2)}, u32[]{:S(2)}) collective-permute-start(bf16[128,2048]{1,0:T(8,128)(2,1)S(1)} %collective-permute-done.13.refs_1_), channel_id=1, source_target_pairs={{4,5},{5,4},{6,7},{7,6},{12,13},{13,12},{14,15},{15,14},{20,21},{2... | collective-permute-start | bytes 1572872 | tf_op jit(solution)/shard_map/ppermute | solution.py:386
  43.9 12.0 %collective-permute-start.16 = (bf16[128,2048]{1,0:T(8,128)(2,1)S(1)}, bf16[128,2048]{1,0:T(8,128)(2,1)S(1)}, u32[]{:S(2)}, u32[]{:S(2)}) collective-permute-start(bf16[128,2048]{1,0:T(8,128)(2,1)S(1)} %collective-permute-done.12.refs_0_), channel_id=1, source_target_pairs={{0,4},{4,0},{8,12},{12,8},{16,20},{20,16},{24,28},{28,24},{1,5},{5... | collective-permute-start | bytes 1572872 | tf_op jit(solution)/shard_map/ppermute | solution.py:32
  48.6 13.3 %collective-permute-start.17 = (bf16[128,2048]{1,0:T(8,128)(2,1)S(1)}, bf16[128,2048]{1,0:T(8,128)(2,1)S(1)}, u32[]{:S(2)}, u32[]{:S(2)}) collective-permute-start(bf16[128,2048]{1,0:T(8,128)(2,1)S(1)} %collective-permute-done.13.refs_1_), channel_id=1, source_target_pairs={{0,4},{4,0},{8,12},{12,8},{16,20},{20,16},{24,28},{28,24},{1,5},{5... | collective-permute-start | bytes 1572872 | tf_op jit(solution)/shard_map/ppermute | solution.py:32
  53.7 8.2 %collective-permute-start.18 = (bf16[128,2048]{1,0:T(8,128)(2,1)S(1)}, bf16[128,2048]{1,0:T(8,128)(2,1)S(1)}, u32[]{:S(2)}, u32[]{:S(2)}) collective-permute-start(bf16[128,2048]{1,0:T(8,128)(2,1)S(1)} %collective-permute-done.14.refs_2_), channel_id=1, source_target_pairs={{0,4},{4,0},{8,12},{12,8},{16,20},{20,16},{24,28},{28,24},{1,5},{5... | collective-permute-start | bytes 1572872 | tf_op jit(solution)/shard_map/ppermute | solution.py:32
  54.1 14.5 %copy-start = (bf16[1024,512]{1,0:T(8,128)(2,1)S(1)}, bf16[1024,512]{1,0:T(8,128)(2,1)}, u32[]{:S(2)}) copy-start(bf16[1024,512]{1,0:T(8,128)(2,1)} %q_ref.7) | copy-start | bytes 3145732
  54.2 12.6 %collective-permute-start.22 = (bf16[128,2048]{1,0:T(8,128)(2,1)S(1)}, bf16[128,2048]{1,0:T(8,128)(2,1)S(1)}, u32[]{:S(2)}, u32[]{:S(2)}) collective-permute-start(bf16[128,2048]{1,0:T(8,128)(2,1)S(1)} %collective-permute-done.20.refs_0_), channel_id=1, source_target_pairs={{4,12},{12,4},{20,28},{28,20},{5,13},{13,5},{21,29},{29,21},{6,14}... | collective-permute-start | bytes 1572872 | tf_op jit(solution)/shard_map/ppermute | solution.py:388
  55.0 11.9 %collective-permute-start.23 = (bf16[128,2048]{1,0:T(8,128)(2,1)S(1)}, bf16[128,2048]{1,0:T(8,128)(2,1)S(1)}, u32[]{:S(2)}, u32[]{:S(2)}) collective-permute-start(bf16[128,2048]{1,0:T(8,128)(2,1)S(1)} %collective-permute-done.21.refs_1_), channel_id=1, source_target_pairs={{4,20},{12,28},{20,4},{28,12},{5,21},{13,29},{21,5},{29,13},{6,22}... | collective-permute-start | bytes 1572872 | tf_op jit(solution)/shard_map/ppermute | solution.py:388
  55.9 12.7 %collective-permute-start.3 = (bf16[2,512,256]{2,1,0:T(8,128)(2,1)S(1)}, bf16[2,512,256]{2,1,0:T(8,128)(2,1)S(1)}, u32[]{:S(2)}, u32[]{:S(2)}) collective-permute-start(bf16[2,512,256]{2,1,0:T(8,128)(2,1)S(1)} %renorm.2.up_ref), channel_id=1, source_target_pairs={{0,4},{4,0},{8,12},{12,8},{16,20},{20,16},{24,28},{28,24},{1,5},{5... | collective-permute-start | bytes 1572872 | tf_op jit(solution)/shard_map/ppermute | solution.py:32
  61.9 7.6 %collective-permute-start.19 = (bf16[128,2048]{1,0:T(8,128)(2,1)S(1)}, bf16[128,2048]{1,0:T(8,128)(2,1)S(1)}, u32[]{:S(2)}, u32[]{:S(2)}) collective-permute-start(bf16[128,2048]{1,0:T(8,128)(2,1)S(1)} %collective-permute-done.15.refs_3_), channel_id=1, source_target_pairs={{0,4},{4,0},{8,12},{12,8},{16,20},{20,16},{24,28},{28,24},{1,5},{5... | collective-permute-start | bytes 1572872 | tf_op jit(solution)/shard_map/ppermute | solution.py:32
  61.9 9.9 %collective-permute-start.24 = (bf16[128,2048]{1,0:T(8,128)(2,1)S(1)}, bf16[128,2048]{1,0:T(8,128)(2,1)S(1)}, u32[]{:S(2)}, u32[]{:S(2)}) collective-permute-start(bf16[128,2048]{1,0:T(8,128)(2,1)S(1)} %collective-permute-done.20.refs_0_), channel_id=1, source_target_pairs={{0,4},{4,0},{8,12},{12,8},{16,20},{20,16},{24,28},{28,24},{1,5},{5... | collective-permute-start | bytes 1572872 | tf_op jit(solution)/shard_map/ppermute | solution.py:32
  66.8 17.9 %collective-permute-start.25 = (bf16[128,2048]{1,0:T(8,128)(2,1)S(1)}, bf16[128,2048]{1,0:T(8,128)(2,1)S(1)}, u32[]{:S(2)}, u32[]{:S(2)}) collective-permute-start(bf16[128,2048]{1,0:T(8,128)(2,1)S(1)} %collective-permute-done.21.refs_1_), channel_id=1, source_target_pairs={{0,4},{4,0},{8,12},{12,8},{16,20},{20,16},{24,28},{28,24},{1,5},{5... | collective-permute-start | bytes 1572872 | tf_op jit(solution)/shard_map/ppermute | solution.py:32
  66.9 17.8 %collective-permute-start.26 = (bf16[128,2048]{1,0:T(8,128)(2,1)S(1)}, bf16[128,2048]{1,0:T(8,128)(2,1)S(1)}, u32[]{:S(2)}, u32[]{:S(2)}) collective-permute-start(bf16[128,2048]{1,0:T(8,128)(2,1)S(1)} %collective-permute-done.22.refs_2_), channel_id=1, source_target_pairs={{0,4},{4,0},{8,12},{12,8},{16,20},{20,16},{24,28},{28,24},{1,5},{5... | collective-permute-start | bytes 1572872 | tf_op jit(solution)/shard_map/ppermute | solution.py:32
  68.6 16.1 %collective-permute-start.27 = (bf16[128,2048]{1,0:T(8,128)(2,1)S(1)}, bf16[128,2048]{1,0:T(8,128)(2,1)S(1)}, u32[]{:S(2)}, u32[]{:S(2)}) collective-permute-start(bf16[128,2048]{1,0:T(8,128)(2,1)S(1)} %collective-permute-done.23.refs_3_), channel_id=1, source_target_pairs={{0,4},{4,0},{8,12},{12,8},{16,20},{20,16},{24,28},{28,24},{1,5},{5... | collective-permute-start | bytes 1572872 | tf_op jit(solution)/shard_map/ppermute | solution.py:32
  69.4 8.8 %collective-permute-start.11 = (bf16[256,512]{1,0:T(8,128)(2,1)S(1)}, bf16[256,512]{1,0:T(8,128)(2,1)S(1)}, u32[]{:S(2)}, u32[]{:S(2)}) collective-permute-start(bf16[256,512]{1,0:T(8,128)(2,1)S(1)} %combine.6), channel_id=1, source_target_pairs={{0,1},{1,0},{2,3},{3,2},{4,5},{5,4},{6,7},{7,6},{8,9},{9,8},{10,11... | collective-permute-start | bytes 786440 | tf_op jit(solution)/shard_map/ppermute | solution.py:32
  71.8 14.4 %collective-permute-start.10 = (bf16[256,512]{1,0:T(8,128)(2,1)S(1)}, bf16[256,512]{1,0:T(8,128)(2,1)S(1)}, u32[]{:S(2)}, u32[]{:S(2)}) collective-permute-start(bf16[256,512]{1,0:T(8,128)(2,1)S(1)} %combine.5), channel_id=1, source_target_pairs={{0,3},{1,2},{2,1},{3,0},{4,7},{5,6},{6,5},{7,4},{8,11},{9,10},{10,... | collective-permute-start | bytes 786440 | tf_op jit(solution)/shard_map/ppermute | solution.py:32
  78.2 19.9 %collective-permute-start.9 = (bf16[256,512]{1,0:T(8,128)(2,1)S(1)}, bf16[256,512]{1,0:T(8,128)(2,1)S(1)}, u32[]{:S(2)}, u32[]{:S(2)}) collective-permute-start(bf16[256,512]{1,0:T(8,128)(2,1)S(1)} %combine.4), channel_id=1, source_target_pairs={{0,2},{1,3},{2,0},{3,1},{4,6},{5,7},{6,4},{7,5},{8,10},{9,11},{10,... | collective-permute-start | bytes 786440 | tf_op jit(solution)/shard_map/ppermute | solution.py:32
  81.6 1.6 %copy-start.4 = (bf16[512,2048]{1,0:T(8,128)(2,1)S(1)}, bf16[512,2048]{1,0:T(8,128)(2,1)}, u32[]{:S(2)}) copy-start(bf16[512,2048]{1,0:T(8,128)(2,1)} %w_ref.1) | copy-start | bytes 6291460
  81.6 1.6 %copy-start.8 = (bf16[512]{0:T(512)(128)(2,1)S(1)}, bf16[512]{0:T(512)(128)(2,1)}, u32[]{:S(2)}) copy-start(bf16[512]{0:T(512)(128)(2,1)} %gain_ref.1) | copy-start | bytes 3076
  (6 other events, 6.3 us)

commit v7 on v6

--- a/solution.py
+++ b/solution.py
@@ -431,8 +431,8 @@
         combined = combine(k, mixed, seen, weights[0], weights[2])
         blocks[k] = swap(combined, "head", k) if k else combined
     base, squares = own_project(blocks[0], norm_gain, out_weight)
-    for k in (1, 3, 2):
-        scale_by = 1.0 / (heads * width) if k == 2 else None
+    for k in (3, 2, 1):
+        scale_by = 1.0 / (heads * width) if k == 1 else None
         holder, brought = pieces[k]
         result = project(holder, scale_by, blocks[k], base, squares, brought)
         if scale_by is None:
@@ -441,7 +441,7 @@
 
 
 def send_order(heads):
-    return [heads - 1] + list(range(1, heads - 1))
+    return list(range(heads - 1, 0, -1))
 
 
 def solution(mesh):

time: 100 us -> 110 us (1.10)
  waiting for transfers between devices: 35.1 us -> 51 us
  starting transfers between devices: 38 us -> 32.3 us
    ppermute x2, waiting for transfers between devices: 0.01 us -> 15.5 us  [step(): far.append(lax.ppermute(early[j], 'ctx', cross))]
    ppermute x2, waiting for transfers between devices: 10.9 us -> 16 us  [step(): early.append(lax.ppermute(chunk, ('ctx', 'head'), over))]
    ppermute x15, starting transfers between devices: 20.8 us -> 16.4 us  [swap(): lax.ppermute(value, axis, [(i, i ^ mask) for i in range(lax.axis_size(axi...]
    ppermute x15, waiting for transfers between devices: 15.8 us -> 11.7 us  [swap(): lax.ppermute(value, axis, [(i, i ^ mask) for i in range(lax.axis_size(axi...]
    ppermute x2, starting transfers between devices: 4.57 us -> 2.03 us  [step(): far.append(lax.ppermute(early[j], 'ctx', cross))]
    ppermute x4, starting transfers between devices: 5.14 us -> 6.48 us  [step(): got = lax.ppermute(send, 'ctx', pairs)]
  transfers between devices with their start and end apart: 28 -> 28, of which waited for: 7 -> 9; matrix products, arithmetic and copies ran while one was open for 0% -> 0% of each run, Pallas kernels for 14% -> 13%
where the time goes in v7:
time: 110 us
  waiting for transfers between devices  51 us (46%)
  starting transfers between devices  32.3 us (29%)
  Pallas kernels  18.6 us (17%)
  local copies, waits for them, and re-layouts  7.53 us (7%)
    ppermute x15, starting transfers between devices, swap(): lax.ppermute(value, axis, [(i, i ^ mask) for i in range(lax.axis_size(axi...  16.4 us
    ppermute x2, waiting for transfers between devices, step(): early.append(lax.ppermute(chunk, ('ctx', 'head'), over))  16 us
    ppermute x2, waiting for transfers between devices, step(): far.append(lax.ppermute(early[j], 'ctx', cross))  15.5 us
    ppermute x15, waiting for transfers between devices, swap(): lax.ppermute(value, axis, [(i, i ^ mask) for i in range(lax.axis_size(axi...  11.7 us
    ppermute x4, waiting for transfers between devices, step(): got = lax.ppermute(send, 'ctx', pairs)  7.79 us
    unnamed x20, local copies, waits for them, and re-layouts  7.53 us
    ppermute x4, starting transfers between devices, step(): got = lax.ppermute(send, 'ctx', pairs)  6.48 us
    pallas_call x1, Pallas kernels, window(): pl.pallas_call(window_kernel, out_shape=pltpu.VMEM(queries.shape, jnp.flo...  4.36 us
  transfers between devices with their start and end apart: 28, of which 9 were waited for; matrix products, arithmetic and copies ran while one was open for 0% of the time, Pallas kernels for 13%

profile of v7, /device:TPU:0, one launch (start us, length us, event | category | flops | bytes accessed | tf_op | source)
XLA Modules:
  0.0 109.9 jit_solution(16247205431110682121)
XLA Ops:
  0.0 1.2 %copy-done.1 = bf16[1024,512]{1,0:T(8,128)(2,1)S(1)} copy-done((bf16[1024,512]{1,0:T(8,128)(2,1)S(1)}, bf16[1024,512]{1,0:T(8,128)(2,1)}, u32[]{:S(2)}) %copy-start.1) | copy-done | bytes 1048600
  1.2 1.2 %copy-done.3 = bf16[1024,512]{1,0:T(8,128)(2,1)S(1)} copy-done((bf16[1024,512]{1,0:T(8,128)(2,1)S(1)}, bf16[1024,512]{1,0:T(8,128)(2,1)}, u32[]{:S(2)}) %copy-start.3) | copy-done | bytes 1048600
  2.5 1.0 copy-done.5
  3.5 1.0 copy-done.6
  4.5 1.0 copy-done.7
  6.3 3.1 %pushes.1 = (bf16[2,512,256]{2,1,0:T(8,128)(2,1)S(1)}, bf16[1024,512]{1,0:T(8,128)(2,1)S(1)}, bf16[1024,512]{1,0:T(8,128)(2,1)S(1)}, bf16[1024,512]{1,0:T(8,128)(2,1)S(1)}, bf16[1024,512]{1,0:T(8,128)(2,1)S(1)}) custom-call(bf16[1024,512]{1,0:T(8,128)(2,1)S(1)} %copy-done.1, bf16[1024,512]{1,0:T(8,128)(2,1)S(1)} %copy-done.3, f32[1,1024]{1,0:T(1,128)S(1)} %bitcast.1, ...), custom_call_target="tpu_custom_call" | custom-call | tf_op jit(solution)/shard_map/pushes/pallas_call | solution.py:129
  10.5 1.4 %load.1 = (bf16[512,512]{1,0:T(8,128)(2,1)S(1)}, bf16[128,2048]{1,0:T(8,128)(2,1)S(1)}, bf16[128,2048]{1,0:T(8,128)(2,1)S(1)}) custom-call(bf16[1024,512]{1,0:T(8,128)(2,1)} %k_hbm.3, bf16[1024,512]{1,0:T(8,128)(2,1)} %v_hbm.3, bf16[512]{0:T(512)(128)(2,1)} %gain_ref.1, bf16[512,2048]{1,0:T(8,128)(2,1)} %w_ref.1), custom_call_target="tpu_custom_call" | custom-call | tf_op jit(solution)/shard_map/load/pallas_call | solution.py:84
  11.9 3.1 %collective-permute-start.12 = (bf16[128,2048]{1,0:T(8,128)(2,1)S(1)}, bf16[128,2048]{1,0:T(8,128)(2,1)S(1)}, u32[]{:S(2)}, u32[]{:S(2)}) collective-permute-start(bf16[128,2048]{1,0:T(8,128)(2,1)S(1)} %get-tuple-element.43), channel_id=1, source_target_pairs={{0,1},{1,0},{2,3},{3,2},{4,6},{5,7},{6,4},{7,5},{8,9},{9,8},{10,11... | collective-permute-start | bytes 1572872 | tf_op jit(solution)/shard_map/ppermute | solution.py:385
  15.7 1.9 %collective-permute-start.6 = (bf16[1,512,256]{2,1,0:T(8,128)(2,1)S(1)}, bf16[1,512,256]{2,1,0:T(8,128)(2,1)S(1)}, u32[]{:S(2)}, u32[]{:S(2)}) collective-permute-start(bf16[1,512,256]{2,1,0:T(8,128)(2,1)S(1)} %get-tuple-element.38), channel_id=1, source_target_pairs={{0,8},{4,20},{8,0},{12,28},{16,24},{20,4},{24,16},{28,12},{1,9},{5... | collective-permute-start | bytes 786440 | tf_op jit(solution)/shard_map/ppermute | solution.py:419
  17.6 0.7 contract.3.keep_ref
  18.8 3.4 %collective-permute-done.6.got_ref = bf16[1,512,256]{2,1,0:T(8,128)(2,1)S(1)} collective-permute-done((bf16[1,512,256]{2,1,0:T(8,128)(2,1)S(1)}, bf16[1,512,256]{2,1,0:T(8,128)(2,1)S(1)}, u32[]{:S(2)}, u32[]{:S(2)}) %collective-permute-start.6) | collective-permute-done | bytes 262176 | tf_op jit(solution)/shard_map/ppermute | solution.py:419
  22.2 2.0 %collective-permute-start.7 = (bf16[1,512,256]{2,1,0:T(8,128)(2,1)S(1)}, bf16[1,512,256]{2,1,0:T(8,128)(2,1)S(1)}, u32[]{:S(2)}, u32[]{:S(2)}) collective-permute-start(bf16[1,512,256]{2,1,0:T(8,128)(2,1)S(1)} %get-tuple-element.40), channel_id=1, source_target_pairs={{0,16},{4,12},{8,24},{12,4},{16,0},{20,28},{24,8},{28,20},{1,17},{... | collective-permute-start | bytes 786440 | tf_op jit(solution)/shard_map/ppermute | solution.py:419
  24.2 1.3 %collective-permute-start.4 = (bf16[512,512]{1,0:T(8,128)(2,1)S(1)}, bf16[512,512]{1,0:T(8,128)(2,1)S(1)}, u32[]{:S(2)}, u32[]{:S(2)}) collective-permute-start(bf16[512,512]{1,0:T(8,128)(2,1)S(1)} %get-tuple-element.34), channel_id=1, source_target_pairs={{0,4},{4,8},{8,12},{12,16},{16,20},{20,24},{24,28},{1,5},{5,9},{9,... | collective-permute-start | bytes 1572872 | tf_op jit(solution)/shard_map/ppermute | solution.py:378
  25.5 2.0 %collective-permute-done.12.refs_0_ = bf16[128,2048]{1,0:T(8,128)(2,1)S(1)} collective-permute-done((bf16[128,2048]{1,0:T(8,128)(2,1)S(1)}, bf16[128,2048]{1,0:T(8,128)(2,1)S(1)}, u32[]{:S(2)}, u32[]{:S(2)}) %collective-permute-start.12) | collective-permute-done | bytes 524320 | tf_op jit(solution)/shard_map/ppermute | solution.py:385
  28.1 14.0 %collective-permute-done.14.refs_1_ = bf16[128,2048]{1,0:T(8,128)(2,1)S(1)} collective-permute-done((bf16[128,2048]{1,0:T(8,128)(2,1)S(1)}, bf16[128,2048]{1,0:T(8,128)(2,1)S(1)}, u32[]{:S(2)}, u32[]{:S(2)}) %collective-permute-start.14) | collective-permute-done | bytes 524320 | tf_op jit(solution)/shard_map/ppermute | solution.py:385
  43.3 2.4 %collective-permute-start.2 = (bf16[2,512,256]{2,1,0:T(8,128)(2,1)S(1)}, bf16[2,512,256]{2,1,0:T(8,128)(2,1)S(1)}, u32[]{:S(2)}, u32[]{:S(2)}) collective-permute-start(bf16[2,512,256]{2,1,0:T(8,128)(2,1)S(1)} %get-tuple-element.33), channel_id=1, source_target_pairs={{0,16},{4,12},{8,24},{12,4},{16,0},{20,28},{24,8},{28,20},{1,17},{... | collective-permute-start | bytes 1572872 | tf_op jit(solution)/shard_map/ppermute | solution.py:419
  45.8 1.9 %collective-permute-start.23 = (bf16[128,2048]{1,0:T(8,128)(2,1)S(1)}, bf16[128,2048]{1,0:T(8,128)(2,1)S(1)}, u32[]{:S(2)}, u32[]{:S(2)}) collective-permute-start(bf16[128,2048]{1,0:T(8,128)(2,1)S(1)} %collective-permute-done.14.refs_1_), channel_id=1, source_target_pairs={{0,16},{4,12},{8,24},{12,4},{16,0},{20,28},{24,8},{28,20},{1,17},{... | collective-permute-start | bytes 1572872 | tf_op jit(solution)/shard_map/ppermute | solution.py:387
  48.4 4.4 %collective-permute-done.2.got_ref = bf16[2,512,256]{2,1,0:T(8,128)(2,1)S(1)} collective-permute-done((bf16[2,512,256]{2,1,0:T(8,128)(2,1)S(1)}, bf16[2,512,256]{2,1,0:T(8,128)(2,1)S(1)}, u32[]{:S(2)}, u32[]{:S(2)}) %collective-permute-start.2) | collective-permute-done | bytes 524320 | tf_op jit(solution)/shard_map/ppermute | solution.py:419
  52.9 0.9 collective-permute-start.17
  54.2 4.4 %collective-permute-done.22.refs_2_ = bf16[128,2048]{1,0:T(8,128)(2,1)S(1)} collective-permute-done((bf16[128,2048]{1,0:T(8,128)(2,1)S(1)}, bf16[128,2048]{1,0:T(8,128)(2,1)S(1)}, u32[]{:S(2)}, u32[]{:S(2)}) %collective-permute-start.22) | collective-permute-done | bytes 524320 | tf_op jit(solution)/shard_map/ppermute | solution.py:387
  58.6 11.1 %collective-permute-done.23.refs_3_ = bf16[128,2048]{1,0:T(8,128)(2,1)S(1)} collective-permute-done((bf16[128,2048]{1,0:T(8,128)(2,1)S(1)}, bf16[128,2048]{1,0:T(8,128)(2,1)S(1)}, u32[]{:S(2)}, u32[]{:S(2)}) %collective-permute-start.23) | collective-permute-done | bytes 524320 | tf_op jit(solution)/shard_map/ppermute | solution.py:387
  70.7 4.4 %window.1.seen_ref = f32[1024,512]{1,0:T(8,128)S(1)} custom-call(bf16[1024,512]{1,0:T(8,128)(2,1)} %q_ref.7, bf16[1024,512]{1,0:T(8,128)(2,1)} %k_hbm.3, bf16[1024,512]{1,0:T(8,128)(2,1)} %v_hbm.3, bf16[512,512]{1,0:T(8,128)(2,1)S(1)} %collective-permute-done.4.tail_ref), custom_call_target="tpu_custom_call" | custom-call | tf_op jit(solution)/shard_map/window/pallas_call | solution.py:242
  76.6 4.2 %collective-permute-start.11 = (bf16[256,512]{1,0:T(8,128)(2,1)S(1)}, bf16[256,512]{1,0:T(8,128)(2,1)S(1)}, u32[]{:S(2)}, u32[]{:S(2)}) collective-permute-start(bf16[256,512]{1,0:T(8,128)(2,1)S(1)} %combine.6), channel_id=1, source_target_pairs={{0,3},{1,2},{2,1},{3,0},{4,7},{5,6},{6,5},{7,4},{8,11},{9,10},{10,... | collective-permute-start | bytes 786440 | tf_op jit(solution)/shard_map/ppermute | solution.py:32
  82.4 5.6 %collective-permute-done.11.x_ref = bf16[256,512]{1,0:T(8,128)(2,1)S(1)} collective-permute-done((bf16[256,512]{1,0:T(8,128)(2,1)S(1)}, bf16[256,512]{1,0:T(8,128)(2,1)S(1)}, u32[]{:S(2)}, u32[]{:S(2)}) %collective-permute-start.11) | collective-permute-done | bytes 262176 | tf_op jit(solution)/shard_map/ppermute | solution.py:32
  88.0 9.8 %collective-permute-start.9 = (bf16[256,512]{1,0:T(8,128)(2,1)S(1)}, bf16[256,512]{1,0:T(8,128)(2,1)S(1)}, u32[]{:S(2)}, u32[]{:S(2)}) collective-permute-start(bf16[256,512]{1,0:T(8,128)(2,1)S(1)} %combine.4), channel_id=1, source_target_pairs={{0,1},{1,0},{2,3},{3,2},{4,5},{5,4},{6,7},{7,6},{8,9},{9,8},{10,11... | collective-permute-start | bytes 786440 | tf_op jit(solution)/shard_map/ppermute | solution.py:32
  98.6 1.2 %copy-done.4 = bf16[512,2048]{1,0:T(8,128)(2,1)S(1)} copy-done((bf16[512,2048]{1,0:T(8,128)(2,1)S(1)}, bf16[512,2048]{1,0:T(8,128)(2,1)}, u32[]{:S(2)}) %copy-start.4) | copy-done | bytes 2097176
  99.8 0.7 own_project.1
  100.6 0.8 project.3
  101.4 1.3 %collective-permute-done.10.x_ref = bf16[256,512]{1,0:T(8,128)(2,1)S(1)} collective-permute-done((bf16[256,512]{1,0:T(8,128)(2,1)S(1)}, bf16[256,512]{1,0:T(8,128)(2,1)S(1)}, u32[]{:S(2)}, u32[]{:S(2)}) %collective-permute-start.10) | collective-permute-done | bytes 262176 | tf_op jit(solution)/shard_map/ppermute | solution.py:32
  102.7 0.8 project.4
  103.5 4.7 %collective-permute-done.9.x_ref = bf16[256,512]{1,0:T(8,128)(2,1)S(1)} collective-permute-done((bf16[256,512]{1,0:T(8,128)(2,1)S(1)}, bf16[256,512]{1,0:T(8,128)(2,1)S(1)}, u32[]{:S(2)}, u32[]{:S(2)}) %collective-permute-start.9) | collective-permute-done | bytes 262176 | tf_op jit(solution)/shard_map/ppermute | solution.py:32
  108.2 1.6 %project.5 = bf16[256,2048]{1,0:T(8,128)(2,1)} custom-call(bf16[256,512]{1,0:T(8,128)(2,1)S(1)} %collective-permute-done.9.x_ref, f32[256,2048]{1,0:T(8,128)S(1)} %get-tuple-element.47.base_ref, f32[256,1]{1,0:T(8,128)S(1)} %get-tuple-element.48.squares_ref, bf16[128,2048]{1,0:T(8,128)(2,1)S(1)} %collective-permute-done.12.refs_0_, ...), custom_call_target="tpu_custom_call" | custom-call | tf_op jit(solution)/shard_map/project/pallas_call | solution.py:359
  (68 shorter events, 10.8 us)
Async XLA Ops:
  9.3 9.0 %collective-permute-start = (bf16[2,512,256]{2,1,0:T(8,128)(2,1)S(1)}, bf16[2,512,256]{2,1,0:T(8,128)(2,1)S(1)}, u32[]{:S(2)}, u32[]{:S(2)}) collective-permute-start(bf16[2,512,256]{2,1,0:T(8,128)(2,1)S(1)} %get-tuple-element.29), channel_id=1, source_target_pairs={{0,4},{4,0},{8,12},{12,8},{16,20},{20,16},{24,28},{28,24},{1,5},{5... | collective-permute-start | bytes 1572872 | tf_op jit(solution)/shard_map/ppermute | solution.py:32
  10.4 5.2 %collective-permute-start.5 = (bf16[1,512,256]{2,1,0:T(8,128)(2,1)S(1)}, bf16[1,512,256]{2,1,0:T(8,128)(2,1)S(1)}, u32[]{:S(2)}, u32[]{:S(2)}) collective-permute-start(bf16[1,512,256]{2,1,0:T(8,128)(2,1)S(1)} %contract.5), channel_id=1, source_target_pairs={{0,4},{4,0},{8,12},{12,8},{16,20},{20,16},{24,28},{28,24},{1,5},{5... | collective-permute-start | bytes 786440 | tf_op jit(solution)/shard_map/ppermute | solution.py:32
  11.9 5.7 %copy-start.2 = (bf16[1024,512]{1,0:T(8,128)(2,1)S(1)}, bf16[1024,512]{1,0:T(8,128)(2,1)}, u32[]{:S(2)}) copy-start(bf16[1024,512]{1,0:T(8,128)(2,1)} %k_hbm.3) | copy-start | bytes 3145732
  11.9 15.5 %collective-permute-start.12 = (bf16[128,2048]{1,0:T(8,128)(2,1)S(1)}, bf16[128,2048]{1,0:T(8,128)(2,1)S(1)}, u32[]{:S(2)}, u32[]{:S(2)}) collective-permute-start(bf16[128,2048]{1,0:T(8,128)(2,1)S(1)} %get-tuple-element.43), channel_id=1, source_target_pairs={{0,1},{1,0},{2,3},{3,2},{4,6},{5,7},{6,4},{7,5},{8,9},{9,8},{10,11... | collective-permute-start | bytes 1572872 | tf_op jit(solution)/shard_map/ppermute | solution.py:385
  15.0 27.1 %collective-permute-start.14 = (bf16[128,2048]{1,0:T(8,128)(2,1)S(1)}, bf16[128,2048]{1,0:T(8,128)(2,1)S(1)}, u32[]{:S(2)}, u32[]{:S(2)}) collective-permute-start(bf16[128,2048]{1,0:T(8,128)(2,1)S(1)} %get-tuple-element.44), channel_id=1, source_target_pairs={{0,1},{1,0},{2,3},{3,2},{4,6},{5,7},{6,4},{7,5},{8,9},{9,8},{10,11... | collective-permute-start | bytes 1572872 | tf_op jit(solution)/shard_map/ppermute | solution.py:385
  15.7 6.4 %collective-permute-start.6 = (bf16[1,512,256]{2,1,0:T(8,128)(2,1)S(1)}, bf16[1,512,256]{2,1,0:T(8,128)(2,1)S(1)}, u32[]{:S(2)}, u32[]{:S(2)}) collective-permute-start(bf16[1,512,256]{2,1,0:T(8,128)(2,1)S(1)} %get-tuple-element.38), channel_id=1, source_target_pairs={{0,8},{4,20},{8,0},{12,28},{16,24},{20,4},{24,16},{28,12},{1,9},{5... | collective-permute-start | bytes 786440 | tf_op jit(solution)/shard_map/ppermute | solution.py:419
  18.5 24.6 %collective-permute-start.1 = (bf16[2,512,256]{2,1,0:T(8,128)(2,1)S(1)}, bf16[2,512,256]{2,1,0:T(8,128)(2,1)S(1)}, u32[]{:S(2)}, u32[]{:S(2)}) collective-permute-start(bf16[2,512,256]{2,1,0:T(8,128)(2,1)S(1)} %get-tuple-element.31), channel_id=1, source_target_pairs={{0,8},{4,20},{8,0},{12,28},{16,24},{20,4},{24,16},{28,12},{1,9},{5... | collective-permute-start | bytes 1572872 | tf_op jit(solution)/shard_map/ppermute | solution.py:419
  22.2 20.6 %collective-permute-start.7 = (bf16[1,512,256]{2,1,0:T(8,128)(2,1)S(1)}, bf16[1,512,256]{2,1,0:T(8,128)(2,1)S(1)}, u32[]{:S(2)}, u32[]{:S(2)}) collective-permute-start(bf16[1,512,256]{2,1,0:T(8,128)(2,1)S(1)} %get-tuple-element.40), channel_id=1, source_target_pairs={{0,16},{4,12},{8,24},{12,4},{16,0},{20,28},{24,8},{28,20},{1,17},{... | collective-permute-start | bytes 786440 | tf_op jit(solution)/shard_map/ppermute | solution.py:419
  24.2 21.5 %collective-permute-start.4 = (bf16[512,512]{1,0:T(8,128)(2,1)S(1)}, bf16[512,512]{1,0:T(8,128)(2,1)S(1)}, u32[]{:S(2)}, u32[]{:S(2)}) collective-permute-start(bf16[512,512]{1,0:T(8,128)(2,1)S(1)} %get-tuple-element.34), channel_id=1, source_target_pairs={{0,4},{4,8},{8,12},{12,16},{16,20},{20,24},{24,28},{1,5},{5,9},{9,... | collective-permute-start | bytes 1572872 | tf_op jit(solution)/shard_map/ppermute | solution.py:378
  27.4 20.3 %collective-permute-start.13 = (bf16[128,2048]{1,0:T(8,128)(2,1)S(1)}, bf16[128,2048]{1,0:T(8,128)(2,1)S(1)}, u32[]{:S(2)}, u32[]{:S(2)}) collective-permute-start(bf16[128,2048]{1,0:T(8,128)(2,1)S(1)} %collective-permute-done.12.refs_0_), channel_id=1, source_target_pairs={{4,5},{5,4},{6,7},{7,6},{12,13},{13,12},{14,15},{15,14},{20,21},{2... | collective-permute-start | bytes 1572872 | tf_op jit(solution)/shard_map/ppermute | solution.py:386
  42.2 5.6 %collective-permute-start.15 = (bf16[128,2048]{1,0:T(8,128)(2,1)S(1)}, bf16[128,2048]{1,0:T(8,128)(2,1)S(1)}, u32[]{:S(2)}, u32[]{:S(2)}) collective-permute-start(bf16[128,2048]{1,0:T(8,128)(2,1)S(1)} %collective-permute-done.14.refs_1_), channel_id=1, source_target_pairs={{4,5},{5,4},{6,7},{7,6},{12,13},{13,12},{14,15},{15,14},{20,21},{2... | collective-permute-start | bytes 1572872 | tf_op jit(solution)/shard_map/ppermute | solution.py:386
  43.1 2.7 %collective-permute-start.8 = (bf16[1,512,256]{2,1,0:T(8,128)(2,1)S(1)}, bf16[1,512,256]{2,1,0:T(8,128)(2,1)S(1)}, u32[]{:S(2)}, u32[]{:S(2)}) collective-permute-start(bf16[1,512,256]{2,1,0:T(8,128)(2,1)S(1)} %renorm.3.down_ref), channel_id=1, source_target_pairs={{0,4},{4,0},{8,12},{12,8},{16,20},{20,16},{24,28},{28,24},{1,5},{5... | collective-permute-start | bytes 786440 | tf_op jit(solution)/shard_map/ppermute | solution.py:32
  43.3 9.5 %collective-permute-start.2 = (bf16[2,512,256]{2,1,0:T(8,128)(2,1)S(1)}, bf16[2,512,256]{2,1,0:T(8,128)(2,1)S(1)}, u32[]{:S(2)}, u32[]{:S(2)}) collective-permute-start(bf16[2,512,256]{2,1,0:T(8,128)(2,1)S(1)} %get-tuple-element.33), channel_id=1, source_target_pairs={{0,16},{4,12},{8,24},{12,4},{16,0},{20,28},{24,8},{28,20},{1,17},{... | collective-permute-start | bytes 1572872 | tf_op jit(solution)/shard_map/ppermute | solution.py:419
  45.7 12.9 %collective-permute-start.22 = (bf16[128,2048]{1,0:T(8,128)(2,1)S(1)}, bf16[128,2048]{1,0:T(8,128)(2,1)S(1)}, u32[]{:S(2)}, u32[]{:S(2)}) collective-permute-start(bf16[128,2048]{1,0:T(8,128)(2,1)S(1)} %collective-permute-done.12.refs_0_), channel_id=1, source_target_pairs={{0,16},{4,12},{8,24},{12,4},{16,0},{20,28},{24,8},{28,20},{1,17},{... | collective-permute-start | bytes 1572872 | tf_op jit(solution)/shard_map/ppermute | solution.py:387
  45.8 23.9 %collective-permute-start.23 = (bf16[128,2048]{1,0:T(8,128)(2,1)S(1)}, bf16[128,2048]{1,0:T(8,128)(2,1)S(1)}, u32[]{:S(2)}, u32[]{:S(2)}) collective-permute-start(bf16[128,2048]{1,0:T(8,128)(2,1)S(1)} %collective-permute-done.14.refs_1_), channel_id=1, source_target_pairs={{0,16},{4,12},{8,24},{12,4},{16,0},{20,28},{24,8},{28,20},{1,17},{... | collective-permute-start | bytes 1572872 | tf_op jit(solution)/shard_map/ppermute | solution.py:387
  47.7 22.0 %collective-permute-start.24 = (bf16[128,2048]{1,0:T(8,128)(2,1)S(1)}, bf16[128,2048]{1,0:T(8,128)(2,1)S(1)}, u32[]{:S(2)}, u32[]{:S(2)}) collective-permute-start(bf16[128,2048]{1,0:T(8,128)(2,1)S(1)} %collective-permute-done.12.refs_0_), channel_id=1, source_target_pairs={{0,4},{4,0},{8,12},{12,8},{16,20},{20,16},{24,28},{28,24},{1,5},{5... | collective-permute-start | bytes 1572872 | tf_op jit(solution)/shard_map/ppermute | solution.py:32
  47.7 22.5 %collective-permute-start.16 = (bf16[128,2048]{1,0:T(8,128)(2,1)S(1)}, bf16[128,2048]{1,0:T(8,128)(2,1)S(1)}, u32[]{:S(2)}, u32[]{:S(2)}) collective-permute-start(bf16[128,2048]{1,0:T(8,128)(2,1)S(1)} %collective-permute-done.13.refs_0_), channel_id=1, source_target_pairs={{4,12},{12,4},{20,28},{28,20},{5,13},{13,5},{21,29},{29,21},{6,14}... | collective-permute-start | bytes 1572872 | tf_op jit(solution)/shard_map/ppermute | solution.py:388
  52.9 17.4 %collective-permute-start.17 = (bf16[128,2048]{1,0:T(8,128)(2,1)S(1)}, bf16[128,2048]{1,0:T(8,128)(2,1)S(1)}, u32[]{:S(2)}, u32[]{:S(2)}) collective-permute-start(bf16[128,2048]{1,0:T(8,128)(2,1)S(1)} %collective-permute-done.15.refs_1_), channel_id=1, source_target_pairs={{4,20},{12,28},{20,4},{28,12},{5,21},{13,29},{21,5},{29,13},{6,22}... | collective-permute-start | bytes 1572872 | tf_op jit(solution)/shard_map/ppermute | solution.py:388
  54.2 21.6 %copy-start = (bf16[1024,512]{1,0:T(8,128)(2,1)S(1)}, bf16[1024,512]{1,0:T(8,128)(2,1)}, u32[]{:S(2)}) copy-start(bf16[1024,512]{1,0:T(8,128)(2,1)} %q_ref.7) | copy-start | bytes 3145732
  58.6 16.5 %collective-permute-start.18 = (bf16[128,2048]{1,0:T(8,128)(2,1)S(1)}, bf16[128,2048]{1,0:T(8,128)(2,1)S(1)}, u32[]{:S(2)}, u32[]{:S(2)}) collective-permute-start(bf16[128,2048]{1,0:T(8,128)(2,1)S(1)} %collective-permute-done.13.refs_0_), channel_id=1, source_target_pairs={{0,4},{4,0},{8,12},{12,8},{16,20},{20,16},{24,28},{28,24},{1,5},{5... | collective-permute-start | bytes 1572872 | tf_op jit(solution)/shard_map/ppermute | solution.py:32
  69.7 5.6 %collective-permute-start.19 = (bf16[128,2048]{1,0:T(8,128)(2,1)S(1)}, bf16[128,2048]{1,0:T(8,128)(2,1)S(1)}, u32[]{:S(2)}, u32[]{:S(2)}) collective-permute-start(bf16[128,2048]{1,0:T(8,128)(2,1)S(1)} %collective-permute-done.15.refs_1_), channel_id=1, source_target_pairs={{0,4},{4,0},{8,12},{12,8},{16,20},{20,16},{24,28},{28,24},{1,5},{5... | collective-permute-start | bytes 1572872 | tf_op jit(solution)/shard_map/ppermute | solution.py:32
  69.7 6.0 %collective-permute-start.3 = (bf16[2,512,256]{2,1,0:T(8,128)(2,1)S(1)}, bf16[2,512,256]{2,1,0:T(8,128)(2,1)S(1)}, u32[]{:S(2)}, u32[]{:S(2)}) collective-permute-start(bf16[2,512,256]{2,1,0:T(8,128)(2,1)S(1)} %renorm.2.up_ref), channel_id=1, source_target_pairs={{0,4},{4,0},{8,12},{12,8},{16,20},{20,16},{24,28},{28,24},{1,5},{5... | collective-permute-start | bytes 1572872 | tf_op jit(solution)/shard_map/ppermute | solution.py:32
  70.2 6.3 %collective-permute-start.20 = (bf16[128,2048]{1,0:T(8,128)(2,1)S(1)}, bf16[128,2048]{1,0:T(8,128)(2,1)S(1)}, u32[]{:S(2)}, u32[]{:S(2)}) collective-permute-start(bf16[128,2048]{1,0:T(8,128)(2,1)S(1)} %collective-permute-done.16.refs_2_), channel_id=1, source_target_pairs={{0,4},{4,0},{8,12},{12,8},{16,20},{20,16},{24,28},{28,24},{1,5},{5... | collective-permute-start | bytes 1572872 | tf_op jit(solution)/shard_map/ppermute | solution.py:32
  70.3 11.2 %collective-permute-start.21 = (bf16[128,2048]{1,0:T(8,128)(2,1)S(1)}, bf16[128,2048]{1,0:T(8,128)(2,1)S(1)}, u32[]{:S(2)}, u32[]{:S(2)}) collective-permute-start(bf16[128,2048]{1,0:T(8,128)(2,1)S(1)} %collective-permute-done.17.refs_3_), channel_id=1, source_target_pairs={{0,4},{4,0},{8,12},{12,8},{16,20},{20,16},{24,28},{28,24},{1,5},{5... | collective-permute-start | bytes 1572872 | tf_op jit(solution)/shard_map/ppermute | solution.py:32
  75.1 26.2 %collective-permute-start.25 = (bf16[128,2048]{1,0:T(8,128)(2,1)S(1)}, bf16[128,2048]{1,0:T(8,128)(2,1)S(1)}, u32[]{:S(2)}, u32[]{:S(2)}) collective-permute-start(bf16[128,2048]{1,0:T(8,128)(2,1)S(1)} %collective-permute-done.14.refs_1_), channel_id=1, source_target_pairs={{0,4},{4,0},{8,12},{12,8},{16,20},{20,16},{24,28},{28,24},{1,5},{5... | collective-permute-start | bytes 1572872 | tf_op jit(solution)/shard_map/ppermute | solution.py:32
  75.3 26.1 %collective-permute-start.26 = (bf16[128,2048]{1,0:T(8,128)(2,1)S(1)}, bf16[128,2048]{1,0:T(8,128)(2,1)S(1)}, u32[]{:S(2)}, u32[]{:S(2)}) collective-permute-start(bf16[128,2048]{1,0:T(8,128)(2,1)S(1)} %collective-permute-done.22.refs_2_), channel_id=1, source_target_pairs={{0,4},{4,0},{8,12},{12,8},{16,20},{20,16},{24,28},{28,24},{1,5},{5... | collective-permute-start | bytes 1572872 | tf_op jit(solution)/shard_map/ppermute | solution.py:32
  75.7 25.7 %collective-permute-start.27 = (bf16[128,2048]{1,0:T(8,128)(2,1)S(1)}, bf16[128,2048]{1,0:T(8,128)(2,1)S(1)}, u32[]{:S(2)}, u32[]{:S(2)}) collective-permute-start(bf16[128,2048]{1,0:T(8,128)(2,1)S(1)} %collective-permute-done.23.refs_3_), channel_id=1, source_target_pairs={{0,4},{4,0},{8,12},{12,8},{16,20},{20,16},{24,28},{28,24},{1,5},{5... | collective-permute-start | bytes 1572872 | tf_op jit(solution)/shard_map/ppermute | solution.py:32
  76.6 11.4 %collective-permute-start.11 = (bf16[256,512]{1,0:T(8,128)(2,1)S(1)}, bf16[256,512]{1,0:T(8,128)(2,1)S(1)}, u32[]{:S(2)}, u32[]{:S(2)}) collective-permute-start(bf16[256,512]{1,0:T(8,128)(2,1)S(1)} %combine.6), channel_id=1, source_target_pairs={{0,3},{1,2},{2,1},{3,0},{4,7},{5,6},{6,5},{7,4},{8,11},{9,10},{10,... | collective-permute-start | bytes 786440 | tf_op jit(solution)/shard_map/ppermute | solution.py:32
  81.5 21.2 %collective-permute-start.10 = (bf16[256,512]{1,0:T(8,128)(2,1)S(1)}, bf16[256,512]{1,0:T(8,128)(2,1)S(1)}, u32[]{:S(2)}, u32[]{:S(2)}) collective-permute-start(bf16[256,512]{1,0:T(8,128)(2,1)S(1)} %combine.5), channel_id=1, source_target_pairs={{0,2},{1,3},{2,0},{3,1},{4,6},{5,7},{6,4},{7,5},{8,10},{9,11},{10,... | collective-permute-start | bytes 786440 | tf_op jit(solution)/shard_map/ppermute | solution.py:32
  88.0 20.2 %collective-permute-start.9 = (bf16[256,512]{1,0:T(8,128)(2,1)S(1)}, bf16[256,512]{1,0:T(8,128)(2,1)S(1)}, u32[]{:S(2)}, u32[]{:S(2)}) collective-permute-start(bf16[256,512]{1,0:T(8,128)(2,1)S(1)} %combine.4), channel_id=1, source_target_pairs={{0,1},{1,0},{2,3},{3,2},{4,5},{5,4},{6,7},{7,6},{8,9},{9,8},{10,11... | collective-permute-start | bytes 786440 | tf_op jit(solution)/shard_map/ppermute | solution.py:32
  98.2 1.6 %copy-start.4 = (bf16[512,2048]{1,0:T(8,128)(2,1)S(1)}, bf16[512,2048]{1,0:T(8,128)(2,1)}, u32[]{:S(2)}) copy-start(bf16[512,2048]{1,0:T(8,128)(2,1)} %w_ref.1) | copy-start | bytes 6291460
  98.3 1.6 %copy-start.8 = (bf16[512]{0:T(512)(128)(2,1)S(1)}, bf16[512]{0:T(512)(128)(2,1)}, u32[]{:S(2)}) copy-start(bf16[512]{0:T(512)(128)(2,1)} %gain_ref.1) | copy-start | bytes 3076
  (6 other events, 6.3 us)

commit v8 on v6

--- a/solution.py
+++ b/solution.py
@@ -328,9 +328,10 @@
     theirs = pl.ds(pl.multiple_of((1 - half) * rows, rows), rows)
     x = jnp.concatenate([x_ref[:, mine], x_ref[:, theirs]], axis=1)
     scale = lax.rsqrt(squares * scale_by + EPSILON) if scale_by else None
-    block = brought[0].shape[1] // 4
+    parts = 2 if scale_by else 4
+    block = brought[0].shape[1] // parts
     stores = []
-    for j in range(4):
+    for j in range(parts):
         at = slice(j * block, (j + 1) * block)
         w = [jnp.where(core == holder, a[:, at], b[:, at]) for a, b in zip(brought, copied)]
         total = base_ref[:, at] + dot(x, jnp.concatenate(w, axis=0))
@@ -352,7 +353,7 @@
     rows, columns = base.shape
     if scale_by:
         shape = jax.ShapeDtypeStruct((rows, columns), jnp.bfloat16)
-        scratch = [pltpu.VMEM((4, rows, columns // 4), jnp.bfloat16), pltpu.SemaphoreType.DMA((4,))]
+        scratch = [pltpu.VMEM((2, rows, columns // 2), jnp.bfloat16), pltpu.SemaphoreType.DMA((2,))]
     else:
         shape = (pltpu.VMEM((rows, columns), jnp.float32), pltpu.VMEM((rows, 1), jnp.float32))
         scratch = []

time: 100 us -> 100 us (level)
  no operation moved by 1% of the time
where the time goes in v8:
time: 100 us; the launch traced here: 99.9 us
  starting transfers between devices  38 us (38%)
  waiting for transfers between devices  35.1 us (35%)
  Pallas kernels  18.6 us (19%)
  local copies, waits for them, and re-layouts  7.53 us (8%)
    ppermute x15, starting transfers between devices, swap(): lax.ppermute(value, axis, [(i, i ^ mask) for i in range(lax.axis_size(axi...  20.8 us
    ppermute x15, waiting for transfers between devices, swap(): lax.ppermute(value, axis, [(i, i ^ mask) for i in range(lax.axis_size(axi...  15.8 us
    ppermute x2, waiting for transfers between devices, step(): early.append(lax.ppermute(chunk, ('ctx', 'head'), over))  10.9 us
    ppermute x4, waiting for transfers between devices, step(): got = lax.ppermute(send, 'ctx', pairs)  8.45 us
    unnamed x20, local copies, waits for them, and re-layouts  7.53 us
    ppermute x4, starting transfers between devices, step(): got = lax.ppermute(send, 'ctx', pairs)  5.14 us
    ppermute x2, starting transfers between devices, step(): far.append(lax.ppermute(early[j], 'ctx', cross))  4.57 us
    pallas_call x1, Pallas kernels, window(): pl.pallas_call(window_kernel, out_shape=pltpu.VMEM(queries.shape, jnp.flo...  4.37 us
  transfers between devices with their start and end apart: 28, of which 7 were waited for; matrix products, arithmetic and copies ran while one was open for 0% of the time, Pallas kernels for 14%

profile of v8, /device:TPU:0, one launch (start us, length us, event | category | flops | bytes accessed | tf_op | source)
XLA Modules:
  0.0 99.9 jit_solution(9476208775931379179)
XLA Ops:
  0.0 1.2 %copy-done.1 = bf16[1024,512]{1,0:T(8,128)(2,1)S(1)} copy-done((bf16[1024,512]{1,0:T(8,128)(2,1)S(1)}, bf16[1024,512]{1,0:T(8,128)(2,1)}, u32[]{:S(2)}) %copy-start.1) | copy-done | bytes 1048600
  1.2 1.2 %copy-done.3 = bf16[1024,512]{1,0:T(8,128)(2,1)S(1)} copy-done((bf16[1024,512]{1,0:T(8,128)(2,1)S(1)}, bf16[1024,512]{1,0:T(8,128)(2,1)}, u32[]{:S(2)}) %copy-start.3) | copy-done | bytes 1048600
  2.5 1.0 %copy-done.5 = bf16[1,512,512]{2,1,0:T(8,128)(2,1)S(1)} copy-done((bf16[1,512,512]{2,1,0:T(8,128)(2,1)S(1)}, bf16[1,512,512]{2,1,0:T(8,128)(2,1)}, u32[]{:S(2)}) %copy-start.5) | copy-done | bytes 524312
  3.5 1.0 %copy-done.6 = bf16[1,512,512]{2,1,0:T(8,128)(2,1)S(1)} copy-done((bf16[1,512,512]{2,1,0:T(8,128)(2,1)S(1)}, bf16[1,512,512]{2,1,0:T(8,128)(2,1)}, u32[]{:S(2)}) %copy-start.6) | copy-done | bytes 524312
  4.5 1.0 %copy-done.7 = bf16[1,512,512]{2,1,0:T(8,128)(2,1)S(1)} copy-done((bf16[1,512,512]{2,1,0:T(8,128)(2,1)S(1)}, bf16[1,512,512]{2,1,0:T(8,128)(2,1)}, u32[]{:S(2)}) %copy-start.7) | copy-done | bytes 524312
  6.3 3.1 %pushes.1 = (bf16[2,512,256]{2,1,0:T(8,128)(2,1)S(1)}, bf16[1024,512]{1,0:T(8,128)(2,1)S(1)}, bf16[1024,512]{1,0:T(8,128)(2,1)S(1)}, bf16[1024,512]{1,0:T(8,128)(2,1)S(1)}, bf16[1024,512]{1,0:T(8,128)(2,1)S(1)}) custom-call(bf16[1024,512]{1,0:T(8,128)(2,1)S(1)} %copy-done.1, bf16[1024,512]{1,0:T(8,128)(2,1)S(1)} %copy-done.3, f32[1,1024]{1,0:T(1,128)S(1)} %bitcast.1, ...), custom_call_target="tpu_custom_call" | custom-call | tf_op jit(solution)/shard_map/pushes/pallas_call | solution.py:129
  10.5 1.4 %load.1 = (bf16[512,512]{1,0:T(8,128)(2,1)S(1)}, bf16[128,2048]{1,0:T(8,128)(2,1)S(1)}, bf16[128,2048]{1,0:T(8,128)(2,1)S(1)}) custom-call(bf16[1024,512]{1,0:T(8,128)(2,1)} %k_hbm.3, bf16[1024,512]{1,0:T(8,128)(2,1)} %v_hbm.3, bf16[512]{0:T(512)(128)(2,1)} %gain_ref.1, bf16[512,2048]{1,0:T(8,128)(2,1)} %w_ref.1), custom_call_target="tpu_custom_call" | custom-call | tf_op jit(solution)/shard_map/load/pallas_call | solution.py:84
  11.9 3.1 %collective-permute-start.12 = (bf16[128,2048]{1,0:T(8,128)(2,1)S(1)}, bf16[128,2048]{1,0:T(8,128)(2,1)S(1)}, u32[]{:S(2)}, u32[]{:S(2)}) collective-permute-start(bf16[128,2048]{1,0:T(8,128)(2,1)S(1)} %get-tuple-element.43), channel_id=1, source_target_pairs={{0,1},{1,0},{2,3},{3,2},{4,6},{5,7},{6,4},{7,5},{8,9},{9,8},{10,11... | collective-permute-start | bytes 1572872 | tf_op jit(solution)/shard_map/ppermute | solution.py:386
  15.7 1.9 %collective-permute-start.6 = (bf16[1,512,256]{2,1,0:T(8,128)(2,1)S(1)}, bf16[1,512,256]{2,1,0:T(8,128)(2,1)S(1)}, u32[]{:S(2)}, u32[]{:S(2)}) collective-permute-start(bf16[1,512,256]{2,1,0:T(8,128)(2,1)S(1)} %get-tuple-element.38), channel_id=1, source_target_pairs={{0,8},{4,20},{8,0},{12,28},{16,24},{20,4},{24,16},{28,12},{1,9},{5... | collective-permute-start | bytes 786440 | tf_op jit(solution)/shard_map/ppermute | solution.py:420
  18.8 3.4 %collective-permute-done.6.got_ref = bf16[1,512,256]{2,1,0:T(8,128)(2,1)S(1)} collective-permute-done((bf16[1,512,256]{2,1,0:T(8,128)(2,1)S(1)}, bf16[1,512,256]{2,1,0:T(8,128)(2,1)S(1)}, u32[]{:S(2)}, u32[]{:S(2)}) %collective-permute-start.6) | collective-permute-done | bytes 262176 | tf_op jit(solution)/shard_map/ppermute | solution.py:420
  22.2 2.0 %collective-permute-start.7 = (bf16[1,512,256]{2,1,0:T(8,128)(2,1)S(1)}, bf16[1,512,256]{2,1,0:T(8,128)(2,1)S(1)}, u32[]{:S(2)}, u32[]{:S(2)}) collective-permute-start(bf16[1,512,256]{2,1,0:T(8,128)(2,1)S(1)} %get-tuple-element.40), channel_id=1, source_target_pairs={{0,16},{4,12},{8,24},{12,4},{16,0},{20,28},{24,8},{28,20},{1,17},{... | collective-permute-start | bytes 786440 | tf_op jit(solution)/shard_map/ppermute | solution.py:420
  24.2 1.3 %collective-permute-start.4 = (bf16[512,512]{1,0:T(8,128)(2,1)S(1)}, bf16[512,512]{1,0:T(8,128)(2,1)S(1)}, u32[]{:S(2)}, u32[]{:S(2)}) collective-permute-start(bf16[512,512]{1,0:T(8,128)(2,1)S(1)} %get-tuple-element.34), channel_id=1, source_target_pairs={{0,4},{4,8},{8,12},{12,16},{16,20},{20,24},{24,28},{1,5},{5,9},{9,... | collective-permute-start | bytes 1572872 | tf_op jit(solution)/shard_map/ppermute | solution.py:379
  25.5 2.0 %collective-permute-done.12.refs_0_ = bf16[128,2048]{1,0:T(8,128)(2,1)S(1)} collective-permute-done((bf16[128,2048]{1,0:T(8,128)(2,1)S(1)}, bf16[128,2048]{1,0:T(8,128)(2,1)S(1)}, u32[]{:S(2)}, u32[]{:S(2)}) %collective-permute-start.12) | collective-permute-done | bytes 524320 | tf_op jit(solution)/shard_map/ppermute | solution.py:386
  27.4 2.3 %collective-permute-start.14 = (bf16[128,2048]{1,0:T(8,128)(2,1)S(1)}, bf16[128,2048]{1,0:T(8,128)(2,1)S(1)}, u32[]{:S(2)}, u32[]{:S(2)}) collective-permute-start(bf16[128,2048]{1,0:T(8,128)(2,1)S(1)} %collective-permute-done.12.refs_0_), channel_id=1, source_target_pairs={{0,16},{4,12},{8,24},{12,4},{16,0},{20,28},{24,8},{28,20},{1,17},{... | collective-permute-start | bytes 1572872 | tf_op jit(solution)/shard_map/ppermute | solution.py:388
  29.8 8.9 %collective-permute-done.13.refs_1_ = bf16[128,2048]{1,0:T(8,128)(2,1)S(1)} collective-permute-done((bf16[128,2048]{1,0:T(8,128)(2,1)S(1)}, bf16[128,2048]{1,0:T(8,128)(2,1)S(1)}, u32[]{:S(2)}, u32[]{:S(2)}) %collective-permute-start.13) | collective-permute-done | bytes 524320 | tf_op jit(solution)/shard_map/ppermute | solution.py:386
  38.7 2.3 %collective-permute-start.15 = (bf16[128,2048]{1,0:T(8,128)(2,1)S(1)}, bf16[128,2048]{1,0:T(8,128)(2,1)S(1)}, u32[]{:S(2)}, u32[]{:S(2)}) collective-permute-start(bf16[128,2048]{1,0:T(8,128)(2,1)S(1)} %collective-permute-done.13.refs_1_), channel_id=1, source_target_pairs={{0,16},{4,12},{8,24},{12,4},{16,0},{20,28},{24,8},{28,20},{1,17},{... | collective-permute-start | bytes 1572872 | tf_op jit(solution)/shard_map/ppermute | solution.py:388
  41.4 1.0 %collective-permute-start.2 = (bf16[2,512,256]{2,1,0:T(8,128)(2,1)S(1)}, bf16[2,512,256]{2,1,0:T(8,128)(2,1)S(1)}, u32[]{:S(2)}, u32[]{:S(2)}) collective-permute-start(bf16[2,512,256]{2,1,0:T(8,128)(2,1)S(1)} %get-tuple-element.33), channel_id=1, source_target_pairs={{0,16},{4,12},{8,24},{12,4},{16,0},{20,28},{24,8},{28,20},{1,17},{... | collective-permute-start | bytes 1572872 | tf_op jit(solution)/shard_map/ppermute | solution.py:420
  43.9 4.7 %collective-permute-start.16 = (bf16[128,2048]{1,0:T(8,128)(2,1)S(1)}, bf16[128,2048]{1,0:T(8,128)(2,1)S(1)}, u32[]{:S(2)}, u32[]{:S(2)}) collective-permute-start(bf16[128,2048]{1,0:T(8,128)(2,1)S(1)} %collective-permute-done.12.refs_0_), channel_id=1, source_target_pairs={{0,4},{4,0},{8,12},{12,8},{16,20},{20,16},{24,28},{28,24},{1,5},{5... | collective-permute-start | bytes 1572872 | tf_op jit(solution)/shard_map/ppermute | solution.py:32
  48.6 5.1 %collective-permute-done.2.got_ref = bf16[2,512,256]{2,1,0:T(8,128)(2,1)S(1)} collective-permute-done((bf16[2,512,256]{2,1,0:T(8,128)(2,1)S(1)}, bf16[2,512,256]{2,1,0:T(8,128)(2,1)S(1)}, u32[]{:S(2)}, u32[]{:S(2)}) %collective-permute-start.2) | collective-permute-done | bytes 524320 | tf_op jit(solution)/shard_map/ppermute | solution.py:420
  54.2 0.8 collective-permute-start.22
  55.0 0.9 collective-permute-start.23
  55.9 6.0 %collective-permute-start.3 = (bf16[2,512,256]{2,1,0:T(8,128)(2,1)S(1)}, bf16[2,512,256]{2,1,0:T(8,128)(2,1)S(1)}, u32[]{:S(2)}, u32[]{:S(2)}) collective-permute-start(bf16[2,512,256]{2,1,0:T(8,128)(2,1)S(1)} %renorm.2.up_ref), channel_id=1, source_target_pairs={{0,4},{4,0},{8,12},{12,8},{16,20},{20,16},{24,28},{28,24},{1,5},{5... | collective-permute-start | bytes 1572872 | tf_op jit(solution)/shard_map/ppermute | solution.py:32
  62.4 4.4 %window.1.seen_ref = f32[1024,512]{1,0:T(8,128)S(1)} custom-call(bf16[1024,512]{1,0:T(8,128)(2,1)} %q_ref.7, bf16[1024,512]{1,0:T(8,128)(2,1)} %k_hbm.3, bf16[1024,512]{1,0:T(8,128)(2,1)} %v_hbm.3, bf16[512,512]{1,0:T(8,128)(2,1)S(1)} %collective-permute-done.4.tail_ref), custom_call_target="tpu_custom_call" | custom-call | tf_op jit(solution)/shard_map/window/pallas_call | solution.py:242
  66.9 1.7 %collective-permute-start.26 = (bf16[128,2048]{1,0:T(8,128)(2,1)S(1)}, bf16[128,2048]{1,0:T(8,128)(2,1)S(1)}, u32[]{:S(2)}, u32[]{:S(2)}) collective-permute-start(bf16[128,2048]{1,0:T(8,128)(2,1)S(1)} %collective-permute-done.22.refs_2_), channel_id=1, source_target_pairs={{0,4},{4,0},{8,12},{12,8},{16,20},{20,16},{24,28},{28,24},{1,5},{5... | collective-permute-start | bytes 1572872 | tf_op jit(solution)/shard_map/ppermute | solution.py:32
  69.4 1.6 %collective-permute-start.11 = (bf16[256,512]{1,0:T(8,128)(2,1)S(1)}, bf16[256,512]{1,0:T(8,128)(2,1)S(1)}, u32[]{:S(2)}, u32[]{:S(2)}) collective-permute-start(bf16[256,512]{1,0:T(8,128)(2,1)S(1)} %combine.6), channel_id=1, source_target_pairs={{0,1},{1,0},{2,3},{3,2},{4,5},{5,4},{6,7},{7,6},{8,9},{9,8},{10,11... | collective-permute-start | bytes 786440 | tf_op jit(solution)/shard_map/ppermute | solution.py:32
  71.8 2.4 %collective-permute-start.10 = (bf16[256,512]{1,0:T(8,128)(2,1)S(1)}, bf16[256,512]{1,0:T(8,128)(2,1)S(1)}, u32[]{:S(2)}, u32[]{:S(2)}) collective-permute-start(bf16[256,512]{1,0:T(8,128)(2,1)S(1)} %combine.5), channel_id=1, source_target_pairs={{0,3},{1,2},{2,1},{3,0},{4,7},{5,6},{6,5},{7,4},{8,11},{9,10},{10,... | collective-permute-start | bytes 786440 | tf_op jit(solution)/shard_map/ppermute | solution.py:32
  75.0 3.2 %collective-permute-done.11.x_ref = bf16[256,512]{1,0:T(8,128)(2,1)S(1)} collective-permute-done((bf16[256,512]{1,0:T(8,128)(2,1)S(1)}, bf16[256,512]{1,0:T(8,128)(2,1)S(1)}, u32[]{:S(2)}, u32[]{:S(2)}) %collective-permute-start.11) | collective-permute-done | bytes 262176 | tf_op jit(solution)/shard_map/ppermute | solution.py:32
  78.2 2.9 %collective-permute-start.9 = (bf16[256,512]{1,0:T(8,128)(2,1)S(1)}, bf16[256,512]{1,0:T(8,128)(2,1)S(1)}, u32[]{:S(2)}, u32[]{:S(2)}) collective-permute-start(bf16[256,512]{1,0:T(8,128)(2,1)S(1)} %combine.4), channel_id=1, source_target_pairs={{0,2},{1,3},{2,0},{3,1},{4,6},{5,7},{6,4},{7,5},{8,10},{9,11},{10,... | collective-permute-start | bytes 786440 | tf_op jit(solution)/shard_map/ppermute | solution.py:32
  81.9 1.2 %copy-done.4 = bf16[512,2048]{1,0:T(8,128)(2,1)S(1)} copy-done((bf16[512,2048]{1,0:T(8,128)(2,1)S(1)}, bf16[512,2048]{1,0:T(8,128)(2,1)}, u32[]{:S(2)}) %copy-start.4) | copy-done | bytes 2097176
  84.7 1.6 %collective-permute-done.10.x_ref = bf16[256,512]{1,0:T(8,128)(2,1)S(1)} collective-permute-done((bf16[256,512]{1,0:T(8,128)(2,1)S(1)}, bf16[256,512]{1,0:T(8,128)(2,1)S(1)}, u32[]{:S(2)}, u32[]{:S(2)}) %collective-permute-start.10) | collective-permute-done | bytes 262176 | tf_op jit(solution)/shard_map/ppermute | solution.py:32
  87.1 11.0 %collective-permute-done.9.x_ref = bf16[256,512]{1,0:T(8,128)(2,1)S(1)} collective-permute-done((bf16[256,512]{1,0:T(8,128)(2,1)S(1)}, bf16[256,512]{1,0:T(8,128)(2,1)S(1)}, u32[]{:S(2)}, u32[]{:S(2)}) %collective-permute-start.9) | collective-permute-done | bytes 262176 | tf_op jit(solution)/shard_map/ppermute | solution.py:32
  98.1 1.6 %project.5 = bf16[256,2048]{1,0:T(8,128)(2,1)} custom-call(bf16[256,512]{1,0:T(8,128)(2,1)S(1)} %collective-permute-done.9.x_ref, f32[256,2048]{1,0:T(8,128)S(1)} %get-tuple-element.47.base_ref, f32[256,1]{1,0:T(8,128)S(1)} %get-tuple-element.48.squares_ref, bf16[128,2048]{1,0:T(8,128)(2,1)S(1)} %collective-permute-done.12.refs_0_, ...), custom_call_target="tpu_custom_call" | custom-call | tf_op jit(solution)/shard_map/project/pallas_call | solution.py:360
  (68 shorter events, 12.1 us)
Async XLA Ops:
  9.3 9.0 %collective-permute-start = (bf16[2,512,256]{2,1,0:T(8,128)(2,1)S(1)}, bf16[2,512,256]{2,1,0:T(8,128)(2,1)S(1)}, u32[]{:S(2)}, u32[]{:S(2)}) collective-permute-start(bf16[2,512,256]{2,1,0:T(8,128)(2,1)S(1)} %get-tuple-element.29), channel_id=1, source_target_pairs={{0,4},{4,0},{8,12},{12,8},{16,20},{20,16},{24,28},{28,24},{1,5},{5... | collective-permute-start | bytes 1572872 | tf_op jit(solution)/shard_map/ppermute | solution.py:32
  10.4 5.2 %collective-permute-start.5 = (bf16[1,512,256]{2,1,0:T(8,128)(2,1)S(1)}, bf16[1,512,256]{2,1,0:T(8,128)(2,1)S(1)}, u32[]{:S(2)}, u32[]{:S(2)}) collective-permute-start(bf16[1,512,256]{2,1,0:T(8,128)(2,1)S(1)} %contract.5), channel_id=1, source_target_pairs={{0,4},{4,0},{8,12},{12,8},{16,20},{20,16},{24,28},{28,24},{1,5},{5... | collective-permute-start | bytes 786440 | tf_op jit(solution)/shard_map/ppermute | solution.py:32
  11.9 5.7 %copy-start.2 = (bf16[1024,512]{1,0:T(8,128)(2,1)S(1)}, bf16[1024,512]{1,0:T(8,128)(2,1)}, u32[]{:S(2)}) copy-start(bf16[1024,512]{1,0:T(8,128)(2,1)} %k_hbm.3) | copy-start | bytes 3145732
  11.9 15.5 %collective-permute-start.12 = (bf16[128,2048]{1,0:T(8,128)(2,1)S(1)}, bf16[128,2048]{1,0:T(8,128)(2,1)S(1)}, u32[]{:S(2)}, u32[]{:S(2)}) collective-permute-start(bf16[128,2048]{1,0:T(8,128)(2,1)S(1)} %get-tuple-element.43), channel_id=1, source_target_pairs={{0,1},{1,0},{2,3},{3,2},{4,6},{5,7},{6,4},{7,5},{8,9},{9,8},{10,11... | collective-permute-start | bytes 1572872 | tf_op jit(solution)/shard_map/ppermute | solution.py:386
  15.0 23.7 %collective-permute-start.13 = (bf16[128,2048]{1,0:T(8,128)(2,1)S(1)}, bf16[128,2048]{1,0:T(8,128)(2,1)S(1)}, u32[]{:S(2)}, u32[]{:S(2)}) collective-permute-start(bf16[128,2048]{1,0:T(8,128)(2,1)S(1)} %get-tuple-element.44), channel_id=1, source_target_pairs={{0,1},{1,0},{2,3},{3,2},{4,6},{5,7},{6,4},{7,5},{8,9},{9,8},{10,11... | collective-permute-start | bytes 1572872 | tf_op jit(solution)/shard_map/ppermute | solution.py:386
  15.7 6.4 %collective-permute-start.6 = (bf16[1,512,256]{2,1,0:T(8,128)(2,1)S(1)}, bf16[1,512,256]{2,1,0:T(8,128)(2,1)S(1)}, u32[]{:S(2)}, u32[]{:S(2)}) collective-permute-start(bf16[1,512,256]{2,1,0:T(8,128)(2,1)S(1)} %get-tuple-element.38), channel_id=1, source_target_pairs={{0,8},{4,20},{8,0},{12,28},{16,24},{20,4},{24,16},{28,12},{1,9},{5... | collective-permute-start | bytes 786440 | tf_op jit(solution)/shard_map/ppermute | solution.py:420
  18.5 22.7 %collective-permute-start.1 = (bf16[2,512,256]{2,1,0:T(8,128)(2,1)S(1)}, bf16[2,512,256]{2,1,0:T(8,128)(2,1)S(1)}, u32[]{:S(2)}, u32[]{:S(2)}) collective-permute-start(bf16[2,512,256]{2,1,0:T(8,128)(2,1)S(1)} %get-tuple-element.31), channel_id=1, source_target_pairs={{0,8},{4,20},{8,0},{12,28},{16,24},{20,4},{24,16},{28,12},{1,9},{5... | collective-permute-start | bytes 1572872 | tf_op jit(solution)/shard_map/ppermute | solution.py:420
  22.2 18.7 %collective-permute-start.7 = (bf16[1,512,256]{2,1,0:T(8,128)(2,1)S(1)}, bf16[1,512,256]{2,1,0:T(8,128)(2,1)S(1)}, u32[]{:S(2)}, u32[]{:S(2)}) collective-permute-start(bf16[1,512,256]{2,1,0:T(8,128)(2,1)S(1)} %get-tuple-element.40), channel_id=1, source_target_pairs={{0,16},{4,12},{8,24},{12,4},{16,0},{20,28},{24,8},{28,20},{1,17},{... | collective-permute-start | bytes 786440 | tf_op jit(solution)/shard_map/ppermute | solution.py:420
  24.2 18.3 %collective-permute-start.4 = (bf16[512,512]{1,0:T(8,128)(2,1)S(1)}, bf16[512,512]{1,0:T(8,128)(2,1)S(1)}, u32[]{:S(2)}, u32[]{:S(2)}) collective-permute-start(bf16[512,512]{1,0:T(8,128)(2,1)S(1)} %get-tuple-element.34), channel_id=1, source_target_pairs={{0,4},{4,8},{8,12},{12,16},{16,20},{20,24},{24,28},{1,5},{5,9},{9,... | collective-permute-start | bytes 1572872 | tf_op jit(solution)/shard_map/ppermute | solution.py:379
  27.4 16.4 %collective-permute-start.14 = (bf16[128,2048]{1,0:T(8,128)(2,1)S(1)}, bf16[128,2048]{1,0:T(8,128)(2,1)S(1)}, u32[]{:S(2)}, u32[]{:S(2)}) collective-permute-start(bf16[128,2048]{1,0:T(8,128)(2,1)S(1)} %collective-permute-done.12.refs_0_), channel_id=1, source_target_pairs={{0,16},{4,12},{8,24},{12,4},{16,0},{20,28},{24,8},{28,20},{1,17},{... | collective-permute-start | bytes 1572872 | tf_op jit(solution)/shard_map/ppermute | solution.py:388
  38.7 9.9 %collective-permute-start.15 = (bf16[128,2048]{1,0:T(8,128)(2,1)S(1)}, bf16[128,2048]{1,0:T(8,128)(2,1)S(1)}, u32[]{:S(2)}, u32[]{:S(2)}) collective-permute-start(bf16[128,2048]{1,0:T(8,128)(2,1)S(1)} %collective-permute-done.13.refs_1_), channel_id=1, source_target_pairs={{0,16},{4,12},{8,24},{12,4},{16,0},{20,28},{24,8},{28,20},{1,17},{... | collective-permute-start | bytes 1572872 | tf_op jit(solution)/shard_map/ppermute | solution.py:388
  41.2 2.0 %collective-permute-start.8 = (bf16[1,512,256]{2,1,0:T(8,128)(2,1)S(1)}, bf16[1,512,256]{2,1,0:T(8,128)(2,1)S(1)}, u32[]{:S(2)}, u32[]{:S(2)}) collective-permute-start(bf16[1,512,256]{2,1,0:T(8,128)(2,1)S(1)} %renorm.3.down_ref), channel_id=1, source_target_pairs={{0,4},{4,0},{8,12},{12,8},{16,20},{20,16},{24,28},{28,24},{1,5},{5... | collective-permute-start | bytes 786440 | tf_op jit(solution)/shard_map/ppermute | solution.py:32
  41.4 12.3 %collective-permute-start.2 = (bf16[2,512,256]{2,1,0:T(8,128)(2,1)S(1)}, bf16[2,512,256]{2,1,0:T(8,128)(2,1)S(1)}, u32[]{:S(2)}, u32[]{:S(2)}) collective-permute-start(bf16[2,512,256]{2,1,0:T(8,128)(2,1)S(1)} %get-tuple-element.33), channel_id=1, source_target_pairs={{0,16},{4,12},{8,24},{12,4},{16,0},{20,28},{24,8},{28,20},{1,17},{... | collective-permute-start | bytes 1572872 | tf_op jit(solution)/shard_map/ppermute | solution.py:420
  42.4 11.7 %collective-permute-start.20 = (bf16[128,2048]{1,0:T(8,128)(2,1)S(1)}, bf16[128,2048]{1,0:T(8,128)(2,1)S(1)}, u32[]{:S(2)}, u32[]{:S(2)}) collective-permute-start(bf16[128,2048]{1,0:T(8,128)(2,1)S(1)} %collective-permute-done.12.refs_0_), channel_id=1, source_target_pairs={{4,5},{5,4},{6,7},{7,6},{12,13},{13,12},{14,15},{15,14},{20,21},{2... | collective-permute-start | bytes 1572872 | tf_op jit(solution)/shard_map/ppermute | solution.py:387
  43.1 11.9 %collective-permute-start.21 = (bf16[128,2048]{1,0:T(8,128)(2,1)S(1)}, bf16[128,2048]{1,0:T(8,128)(2,1)S(1)}, u32[]{:S(2)}, u32[]{:S(2)}) collective-permute-start(bf16[128,2048]{1,0:T(8,128)(2,1)S(1)} %collective-permute-done.13.refs_1_), channel_id=1, source_target_pairs={{4,5},{5,4},{6,7},{7,6},{12,13},{13,12},{14,15},{15,14},{20,21},{2... | collective-permute-start | bytes 1572872 | tf_op jit(solution)/shard_map/ppermute | solution.py:387
  43.9 12.0 %collective-permute-start.16 = (bf16[128,2048]{1,0:T(8,128)(2,1)S(1)}, bf16[128,2048]{1,0:T(8,128)(2,1)S(1)}, u32[]{:S(2)}, u32[]{:S(2)}) collective-permute-start(bf16[128,2048]{1,0:T(8,128)(2,1)S(1)} %collective-permute-done.12.refs_0_), channel_id=1, source_target_pairs={{0,4},{4,0},{8,12},{12,8},{16,20},{20,16},{24,28},{28,24},{1,5},{5... | collective-permute-start | bytes 1572872 | tf_op jit(solution)/shard_map/ppermute | solution.py:32
  48.6 13.3 %collective-permute-start.17 = (bf16[128,2048]{1,0:T(8,128)(2,1)S(1)}, bf16[128,2048]{1,0:T(8,128)(2,1)S(1)}, u32[]{:S(2)}, u32[]{:S(2)}) collective-permute-start(bf16[128,2048]{1,0:T(8,128)(2,1)S(1)} %collective-permute-done.13.refs_1_), channel_id=1, source_target_pairs={{0,4},{4,0},{8,12},{12,8},{16,20},{20,16},{24,28},{28,24},{1,5},{5... | collective-permute-start | bytes 1572872 | tf_op jit(solution)/shard_map/ppermute | solution.py:32
  53.7 8.2 %collective-permute-start.18 = (bf16[128,2048]{1,0:T(8,128)(2,1)S(1)}, bf16[128,2048]{1,0:T(8,128)(2,1)S(1)}, u32[]{:S(2)}, u32[]{:S(2)}) collective-permute-start(bf16[128,2048]{1,0:T(8,128)(2,1)S(1)} %collective-permute-done.14.refs_2_), channel_id=1, source_target_pairs={{0,4},{4,0},{8,12},{12,8},{16,20},{20,16},{24,28},{28,24},{1,5},{5... | collective-permute-start | bytes 1572872 | tf_op jit(solution)/shard_map/ppermute | solution.py:32
  54.1 14.5 %copy-start = (bf16[1024,512]{1,0:T(8,128)(2,1)S(1)}, bf16[1024,512]{1,0:T(8,128)(2,1)}, u32[]{:S(2)}) copy-start(bf16[1024,512]{1,0:T(8,128)(2,1)} %q_ref.7) | copy-start | bytes 3145732
  54.2 12.6 %collective-permute-start.22 = (bf16[128,2048]{1,0:T(8,128)(2,1)S(1)}, bf16[128,2048]{1,0:T(8,128)(2,1)S(1)}, u32[]{:S(2)}, u32[]{:S(2)}) collective-permute-start(bf16[128,2048]{1,0:T(8,128)(2,1)S(1)} %collective-permute-done.20.refs_0_), channel_id=1, source_target_pairs={{4,12},{12,4},{20,28},{28,20},{5,13},{13,5},{21,29},{29,21},{6,14}... | collective-permute-start | bytes 1572872 | tf_op jit(solution)/shard_map/ppermute | solution.py:389
  55.0 11.9 %collective-permute-start.23 = (bf16[128,2048]{1,0:T(8,128)(2,1)S(1)}, bf16[128,2048]{1,0:T(8,128)(2,1)S(1)}, u32[]{:S(2)}, u32[]{:S(2)}) collective-permute-start(bf16[128,2048]{1,0:T(8,128)(2,1)S(1)} %collective-permute-done.21.refs_1_), channel_id=1, source_target_pairs={{4,20},{12,28},{20,4},{28,12},{5,21},{13,29},{21,5},{29,13},{6,22}... | collective-permute-start | bytes 1572872 | tf_op jit(solution)/shard_map/ppermute | solution.py:389
  55.9 12.7 %collective-permute-start.3 = (bf16[2,512,256]{2,1,0:T(8,128)(2,1)S(1)}, bf16[2,512,256]{2,1,0:T(8,128)(2,1)S(1)}, u32[]{:S(2)}, u32[]{:S(2)}) collective-permute-start(bf16[2,512,256]{2,1,0:T(8,128)(2,1)S(1)} %renorm.2.up_ref), channel_id=1, source_target_pairs={{0,4},{4,0},{8,12},{12,8},{16,20},{20,16},{24,28},{28,24},{1,5},{5... | collective-permute-start | bytes 1572872 | tf_op jit(solution)/shard_map/ppermute | solution.py:32
  61.9 7.6 %collective-permute-start.19 = (bf16[128,2048]{1,0:T(8,128)(2,1)S(1)}, bf16[128,2048]{1,0:T(8,128)(2,1)S(1)}, u32[]{:S(2)}, u32[]{:S(2)}) collective-permute-start(bf16[128,2048]{1,0:T(8,128)(2,1)S(1)} %collective-permute-done.15.refs_3_), channel_id=1, source_target_pairs={{0,4},{4,0},{8,12},{12,8},{16,20},{20,16},{24,28},{28,24},{1,5},{5... | collective-permute-start | bytes 1572872 | tf_op jit(solution)/shard_map/ppermute | solution.py:32
  61.9 9.9 %collective-permute-start.24 = (bf16[128,2048]{1,0:T(8,128)(2,1)S(1)}, bf16[128,2048]{1,0:T(8,128)(2,1)S(1)}, u32[]{:S(2)}, u32[]{:S(2)}) collective-permute-start(bf16[128,2048]{1,0:T(8,128)(2,1)S(1)} %collective-permute-done.20.refs_0_), channel_id=1, source_target_pairs={{0,4},{4,0},{8,12},{12,8},{16,20},{20,16},{24,28},{28,24},{1,5},{5... | collective-permute-start | bytes 1572872 | tf_op jit(solution)/shard_map/ppermute | solution.py:32
  66.8 17.9 %collective-permute-start.25 = (bf16[128,2048]{1,0:T(8,128)(2,1)S(1)}, bf16[128,2048]{1,0:T(8,128)(2,1)S(1)}, u32[]{:S(2)}, u32[]{:S(2)}) collective-permute-start(bf16[128,2048]{1,0:T(8,128)(2,1)S(1)} %collective-permute-done.21.refs_1_), channel_id=1, source_target_pairs={{0,4},{4,0},{8,12},{12,8},{16,20},{20,16},{24,28},{28,24},{1,5},{5... | collective-permute-start | bytes 1572872 | tf_op jit(solution)/shard_map/ppermute | solution.py:32
  66.9 17.8 %collective-permute-start.26 = (bf16[128,2048]{1,0:T(8,128)(2,1)S(1)}, bf16[128,2048]{1,0:T(8,128)(2,1)S(1)}, u32[]{:S(2)}, u32[]{:S(2)}) collective-permute-start(bf16[128,2048]{1,0:T(8,128)(2,1)S(1)} %collective-permute-done.22.refs_2_), channel_id=1, source_target_pairs={{0,4},{4,0},{8,12},{12,8},{16,20},{20,16},{24,28},{28,24},{1,5},{5... | collective-permute-start | bytes 1572872 | tf_op jit(solution)/shard_map/ppermute | solution.py:32
  68.6 16.1 %collective-permute-start.27 = (bf16[128,2048]{1,0:T(8,128)(2,1)S(1)}, bf16[128,2048]{1,0:T(8,128)(2,1)S(1)}, u32[]{:S(2)}, u32[]{:S(2)}) collective-permute-start(bf16[128,2048]{1,0:T(8,128)(2,1)S(1)} %collective-permute-done.23.refs_3_), channel_id=1, source_target_pairs={{0,4},{4,0},{8,12},{12,8},{16,20},{20,16},{24,28},{28,24},{1,5},{5... | collective-permute-start | bytes 1572872 | tf_op jit(solution)/shard_map/ppermute | solution.py:32
  69.4 8.8 %collective-permute-start.11 = (bf16[256,512]{1,0:T(8,128)(2,1)S(1)}, bf16[256,512]{1,0:T(8,128)(2,1)S(1)}, u32[]{:S(2)}, u32[]{:S(2)}) collective-permute-start(bf16[256,512]{1,0:T(8,128)(2,1)S(1)} %combine.6), channel_id=1, source_target_pairs={{0,1},{1,0},{2,3},{3,2},{4,5},{5,4},{6,7},{7,6},{8,9},{9,8},{10,11... | collective-permute-start | bytes 786440 | tf_op jit(solution)/shard_map/ppermute | solution.py:32
  71.8 14.4 %collective-permute-start.10 = (bf16[256,512]{1,0:T(8,128)(2,1)S(1)}, bf16[256,512]{1,0:T(8,128)(2,1)S(1)}, u32[]{:S(2)}, u32[]{:S(2)}) collective-permute-start(bf16[256,512]{1,0:T(8,128)(2,1)S(1)} %combine.5), channel_id=1, source_target_pairs={{0,3},{1,2},{2,1},{3,0},{4,7},{5,6},{6,5},{7,4},{8,11},{9,10},{10,... | collective-permute-start | bytes 786440 | tf_op jit(solution)/shard_map/ppermute | solution.py:32
  78.2 19.9 %collective-permute-start.9 = (bf16[256,512]{1,0:T(8,128)(2,1)S(1)}, bf16[256,512]{1,0:T(8,128)(2,1)S(1)}, u32[]{:S(2)}, u32[]{:S(2)}) collective-permute-start(bf16[256,512]{1,0:T(8,128)(2,1)S(1)} %combine.4), channel_id=1, source_target_pairs={{0,2},{1,3},{2,0},{3,1},{4,6},{5,7},{6,4},{7,5},{8,10},{9,11},{10,... | collective-permute-start | bytes 786440 | tf_op jit(solution)/shard_map/ppermute | solution.py:32
  81.6 1.6 %copy-start.4 = (bf16[512,2048]{1,0:T(8,128)(2,1)S(1)}, bf16[512,2048]{1,0:T(8,128)(2,1)}, u32[]{:S(2)}) copy-start(bf16[512,2048]{1,0:T(8,128)(2,1)} %w_ref.1) | copy-start | bytes 6291460
  81.6 1.6 %copy-start.8 = (bf16[512]{0:T(512)(128)(2,1)S(1)}, bf16[512]{0:T(512)(128)(2,1)}, u32[]{:S(2)}) copy-start(bf16[512]{0:T(512)(128)(2,1)} %gain_ref.1) | copy-start | bytes 3076
  (6 other events, 6.3 us)
